TPU v7x, 32 devices: a whole 2x2x4 slice. The times are simulated.
32 devices in a mesh: dp: 2 (over x), ctx: 4 (over y, core), tp: 4 (over z).
Axes of the slice: x: 2, y: 2, z: 4, core: 2. Of those that a mesh axis runs over, the one named last changes fastest.
Arguments:
- tokens: bfloat16 [12, 1024, 768], P('dp', 'ctx'), may hold values from -6 to 6
- segments: int32 [12, 1024], P('dp', 'ctx'), may hold values from 0 to 15, never falling along the last dimension, each value on 1 to 512 neighbouring positions
- w_qkv: bfloat16 [768, 3, 768], P(('dp', 'ctx'), None, 'tp'), may hold values from -0.21875 to 0.21875
- q_bias: float32 [768], P('tp'), may hold values from -3 to 3
- v_bias: float32 [768], P('tp'), may hold values from -3 to 3
- w_out: bfloat16 [768, 768], P(('dp', 'ctx'), 'tp'), may hold values from -0.875 to 0.875
- out_bias: float32 [768], replicated, may hold values from -3 to 3
- gain_one: float32 [768], replicated, may hold values from 0.25 to 1.75
- shift_one: float32 [768], replicated, may hold values from -2 to 2
- w_in: bfloat16 [768, 3072], P(('dp', 'ctx'), 'tp'), may hold values from -0.21875 to 0.21875
- in_bias: float32 [3072], P('tp'), may hold values from -3 to 3
- w_back: bfloat16 [768, 3072], P(('dp', 'ctx'), 'tp'), may hold values from -0.15625 to 0.15625
- back_bias: float32 [768], replicated, may hold values from -3 to 3
- gain_two: float32 [768], replicated, may hold values from 0.25 to 1.75
- shift_two: float32 [768], replicated, may hold values from -2 to 2
- cotangent: bfloat16 [12, 1024, 768], P('dp', 'ctx'), may hold values from -6 to 6
Outputs:
- output: bfloat16 [12, 1024, 768], P('dp', 'ctx')
- d_tokens: float32 [12, 1024, 768], P('dp', 'ctx')
- d_w_qkv: float32 [768, 3, 768], P(('dp', 'ctx'), None, 'tp')
- d_q_bias: float32 [768], P('tp')
- d_v_bias: float32 [768], P('tp')
- d_w_out: float32 [768, 768], P(('dp', 'ctx'), 'tp')
- d_out_bias: float32 [768], replicated
- d_gain_one: float32 [768], replicated
- d_shift_one: float32 [768], replicated
- d_w_in: float32 [768, 3072], P(('dp', 'ctx'), 'tp')
- d_in_bias: float32 [3072], P('tp')
- d_w_back: float32 [768, 3072], P(('dp', 'ctx'), 'tp')
- d_back_bias: float32 [768], replicated
- d_gain_two: float32 [768], replicated
- d_shift_two: float32 [768], replicated
Inputs may be any that keep to these rules, and one draw needn't show every extreme that they name: `segments`: within one sequence segment numbers never fall; each of the 16 numbers covers 1 to 512 consecutive positions, one exactly 512.
All inputs are finite; a program needn't handle non-finite values.
Results may differ from a plain program's by a relative error of at most 0.013.
The roundings to bfloat16 on the way count: a program that leaves them out, or rounds other values in their place, can miss the bound.
Values may be sent and summed in bfloat16 or wider, within the bound.
A program may use at most 128 MiB of HBM per device.

v0:
```python
import math

import jax
import jax.numpy as jnp
from jax import lax
from jax.sharding import PartitionSpec as P

HEAD = 64


def norm_parts(value):
    mean = jnp.mean(value, -1, keepdims=True)
    centered = value - mean
    rstd = lax.rsqrt(jnp.mean(centered * centered, -1, keepdims=True) + 1e-12)
    return (centered * rstd, rstd)


def norm_back(grad, normal, rstd, gain):
    d_gain = jnp.sum(grad * normal, 0)
    d_shift = jnp.sum(grad, 0)
    scaled = grad * gain
    d_value = rstd * (
        scaled
        - jnp.mean(scaled, -1, keepdims=True)
        - normal * jnp.mean(scaled * normal, -1, keepdims=True)
    )
    return (d_value, d_gain, d_shift)


def gelu_slope(inner):
    return 0.5 * (1.0 + lax.erf(inner / math.sqrt(2.0))) + inner * jnp.exp(
        -0.5 * inner * inner
    ) / math.sqrt(2.0 * math.pi)


def masked_scores(q_heads, k_heads, seg_query, seg_key):
    raw = jnp.einsum("qhe,khe->hqk", q_heads, k_heads, preferred_element_type=jnp.float32)
    same = seg_query[:, None] == seg_key[None, :]
    return jnp.where(same[None], raw * (1.0 / math.sqrt(HEAD)), -1e30)


def per_device(
    tokens,
    segments,
    w_qkv,
    q_bias,
    v_bias,
    w_out,
    out_bias,
    gain_one,
    shift_one,
    w_in,
    in_bias,
    w_back,
    back_bias,
    gain_two,
    shift_two,
    cotangent,
):
    seqs, local_len, width = tokens.shape
    rows = seqs * local_len
    gathered = (
        lax.all_gather(w_qkv, ("dp", "ctx"), axis=0, tiled=True),
        lax.all_gather(w_out, ("dp", "ctx"), axis=0, tiled=True),
        lax.all_gather(w_in, ("dp", "ctx"), axis=0, tiled=True),
        lax.all_gather(w_back, ("dp", "ctx"), axis=0, tiled=True),
    )
    full_qkv, full_out, full_in, full_back = gathered
    col_width = full_out.shape[1]
    heads_here = col_width // HEAD
    x_rows = tokens.reshape(rows, width)
    grad_rows = cotangent.reshape(rows, width)
    projected = jnp.einsum("td,dcf->tcf", x_rows, full_qkv, preferred_element_type=jnp.float32)
    query = (projected[:, 0] + q_bias).astype(jnp.bfloat16).reshape(seqs, local_len, col_width)
    key = projected[:, 1].astype(jnp.bfloat16).reshape(seqs, local_len, col_width)
    value = (projected[:, 2] + v_bias).astype(jnp.bfloat16).reshape(seqs, local_len, col_width)
    key_full, value_full, seg_full = (
        lax.all_gather(key, "ctx", axis=1, tiled=True),
        lax.all_gather(value, "ctx", axis=1, tiled=True),
        lax.all_gather(segments, "ctx", axis=1, tiled=True),
    )
    full_len = key_full.shape[1]

    def attend(item):
        q_one, k_one, v_one, s_query, s_key = item
        q_heads = q_one.reshape(local_len, heads_here, HEAD)
        k_heads = k_one.reshape(full_len, heads_here, HEAD)
        v_heads = v_one.reshape(full_len, heads_here, HEAD)
        scores = masked_scores(q_heads, k_heads, s_query, s_key)
        peak = jnp.max(scores, -1, keepdims=True)
        expo = jnp.exp(scores - peak)
        total = jnp.sum(expo, -1, keepdims=True)
        probs_low = (expo / total).astype(jnp.bfloat16)
        context = jnp.einsum("hqk,khe->qhe", probs_low, v_heads, preferred_element_type=jnp.float32)
        lse = (peak + jnp.log(total))[..., 0]
        return (context.astype(jnp.bfloat16).reshape(local_len, col_width), lse)

    context, lse_kept = lax.map(attend, (query, key_full, value_full, segments, seg_full))
    context_rows = context.reshape(rows, col_width)
    attn_part = jnp.einsum("tf,df->td", context_rows, full_out, preferred_element_type=jnp.float32)
    attended = lax.psum(attn_part, "tp") + out_bias
    normal_one, rstd_one = norm_parts(x_rows.astype(jnp.float32) + attended)
    normed = normal_one * gain_one + shift_one
    normed_low = normed.astype(jnp.bfloat16)
    inner = jnp.dot(normed_low, full_in, preferred_element_type=jnp.float32) + in_bias
    active = jax.nn.gelu(inner, approximate=False).astype(jnp.bfloat16)
    ffn_part = jnp.einsum("tf,df->td", active, full_back, preferred_element_type=jnp.float32)
    second = normed + lax.psum(ffn_part, "tp") + back_bias
    normal_two, rstd_two = norm_parts(second)
    output = (normal_two * gain_two + shift_two).astype(jnp.bfloat16)
    d_second, d_gain_two, d_shift_two = norm_back(
        grad_rows.astype(jnp.float32), normal_two, rstd_two, gain_two
    )
    d_second_low = d_second.astype(jnp.bfloat16)
    d_back_bias = jnp.sum(d_second, 0)
    back_set = (
        lax.all_gather(w_qkv, ("dp", "ctx"), axis=0, tiled=True),
        lax.all_gather(w_out, ("dp", "ctx"), axis=0, tiled=True),
        lax.all_gather(w_in, ("dp", "ctx"), axis=0, tiled=True),
        lax.all_gather(w_back, ("dp", "ctx"), axis=0, tiled=True),
    )
    back_qkv, back_out, back_in, back_ffn = back_set
    d_w_back = jnp.einsum("td,tf->df", d_second_low, active, preferred_element_type=jnp.float32)
    d_active = jnp.dot(d_second_low, back_ffn, preferred_element_type=jnp.float32)
    d_inner = d_active * gelu_slope(inner)
    d_in_bias = jnp.sum(d_inner, 0)
    d_inner_low = d_inner.astype(jnp.bfloat16)
    d_w_in = jnp.einsum("td,tf->df", normed_low, d_inner_low, preferred_element_type=jnp.float32)
    hidden_part = jnp.einsum("tf,df->td", d_inner_low, back_in, preferred_element_type=jnp.float32)
    d_normed = lax.psum(hidden_part, "tp") + d_second
    d_first, d_gain_one, d_shift_one = norm_back(d_normed, normal_one, rstd_one, gain_one)
    d_first_low = d_first.astype(jnp.bfloat16)
    d_out_bias = jnp.sum(d_first, 0)
    d_w_out = jnp.einsum("td,tf->df", d_first_low, context_rows, preferred_element_type=jnp.float32)
    d_context = jnp.dot(d_first_low, back_out, preferred_element_type=jnp.float32).astype(
        jnp.bfloat16
    )
    d_context = d_context.reshape(seqs, local_len, col_width)

    def attend_back(item):
        q_one, k_one, v_one, s_query, s_key, lse, d_ctx = item
        q_heads = q_one.reshape(local_len, heads_here, HEAD)
        k_heads = k_one.reshape(full_len, heads_here, HEAD)
        v_heads = v_one.reshape(full_len, heads_here, HEAD)
        d_heads = d_ctx.reshape(local_len, heads_here, HEAD)
        scores = masked_scores(q_heads, k_heads, s_query, s_key)
        probs = jnp.exp(scores - lse[..., None])
        probs_low = probs.astype(jnp.bfloat16)
        d_probs = jnp.einsum("qhe,khe->hqk", d_heads, v_heads, preferred_element_type=jnp.float32)
        delta = jnp.sum(probs * d_probs, -1, keepdims=True)
        d_raw = (probs * (d_probs - delta) * (1.0 / math.sqrt(HEAD))).astype(jnp.bfloat16)
        d_query = jnp.einsum("hqk,khe->qhe", d_raw, k_heads, preferred_element_type=jnp.float32)
        d_key = jnp.einsum("hqk,qhe->khe", d_raw, q_heads, preferred_element_type=jnp.float32)
        d_value = jnp.einsum("hqk,qhe->khe", probs_low, d_heads, preferred_element_type=jnp.float32)
        return (
            d_query.reshape(local_len, col_width),
            d_key.reshape(full_len, col_width),
            d_value.reshape(full_len, col_width),
        )

    d_query, key_part, value_part = lax.map(
        attend_back, (query, key_full, value_full, segments, seg_full, lse_kept, d_context)
    )
    d_key, d_value = (
        lax.psum_scatter(key_part, "ctx", scatter_dimension=1, tiled=True),
        lax.psum_scatter(value_part, "ctx", scatter_dimension=1, tiled=True),
    )
    d_query = d_query.reshape(rows, col_width)
    d_value = d_value.reshape(rows, col_width)
    d_q_bias = jnp.sum(d_query, 0)
    d_v_bias = jnp.sum(d_value, 0)
    d_proj = jnp.stack([d_query, d_key.reshape(rows, col_width), d_value], 1).astype(jnp.bfloat16)
    d_w_qkv = jnp.einsum("td,tcf->dcf", x_rows, d_proj, preferred_element_type=jnp.float32)
    input_part = jnp.einsum("tcf,dcf->td", d_proj, back_qkv, preferred_element_type=jnp.float32)
    w_grads = (
        lax.psum_scatter(d_w_qkv, ("dp", "ctx"), scatter_dimension=0, tiled=True),
        lax.psum_scatter(d_w_out, ("dp", "ctx"), scatter_dimension=0, tiled=True),
        lax.psum_scatter(d_w_in, ("dp", "ctx"), scatter_dimension=0, tiled=True),
        lax.psum_scatter(d_w_back, ("dp", "ctx"), scatter_dimension=0, tiled=True),
    )
    d_tokens = lax.psum(input_part, "tp") + d_first
    small = lax.psum(
        (
            d_q_bias,
            d_v_bias,
            d_out_bias,
            d_gain_one,
            d_shift_one,
            d_in_bias,
            d_back_bias,
            d_gain_two,
            d_shift_two,
        ),
        ("dp", "ctx"),
    )
    return (
        output.reshape(seqs, local_len, width),
        d_tokens.reshape(seqs, local_len, width),
        w_grads[0],
        small[0],
        small[1],
        w_grads[1],
        small[2],
        small[3],
        small[4],
        w_grads[2],
        small[5],
        w_grads[3],
        small[6],
        small[7],
        small[8],
    )


def solution(mesh):
    return jax.shard_map(
        per_device,
        mesh=mesh,
        in_specs=(
            P("dp", "ctx", None),
            P("dp", "ctx"),
            P(("dp", "ctx"), None, "tp"),
            P("tp"),
            P("tp"),
            P(("dp", "ctx"), "tp"),
            P(),
            P(),
            P(),
            P(("dp", "ctx"), "tp"),
            P("tp"),
            P(("dp", "ctx"), "tp"),
            P(),
            P(),
            P(),
            P("dp", "ctx", None),
        ),
        out_specs=(
            P("dp", "ctx", None),
            P("dp", "ctx", None),
            P(("dp", "ctx"), None, "tp"),
            P("tp"),
            P("tp"),
            P(("dp", "ctx"), "tp"),
            P(),
            P(),
            P(),
            P(("dp", "ctx"), "tp"),
            P("tp"),
            P(("dp", "ctx"), "tp"),
            P(),
            P(),
            P(),
        ),
        check_vma=False,
    )
```

profile of v0, /device:TPU:0, one launch (start us, length us, event | category | flops | bytes accessed | tf_op | source)
XLA Modules:
  0.0 1147.5 jit_solution(3269655352616793134)
XLA Ops:
  9.1 14.6 %all_gather.25 = bf16[768,3,192]{2,1,0:T(4,128)(2,1)S(1)} all-gather(bf16[96,3,192]{2,1,0:T(4,128)(2,1)S(1)} %copy.55), channel_id=1, replica_groups=mesh['dp'=2,'ctx'=4,'tp'=4] {'dp','ctx'}, dimensions={0}, use_global_device_ids=true | all-gather | bytes 995328 | tf_op jit(solution)/shard_map/all_gather | solution.py:63
  24.6 3.6 fusion.69
  31.6 2.8 fusion.62
  38.0 5.8 all_gather.27
  43.9 11.3 all_gather.29
  55.1 7.5 all-gather.7.cloned.1.call-done
  62.7 3.2 copy.59
  65.8 28.0 %all-gather.5.cloned.1.call-done = bf16[6,1024,192]{1,0,2:T(8,128)(2,1)} async-done(((bf16[6,256,192]{1,0,2:T(8,128)(2,1)}), bf16[6,1024,192]{1,0,2:T(8,128)(2,1)}) %all-gather.5.cloned.1.call-update) | async-done | bytes 2359312 | tf_op jit(solution)/shard_map/all_gather | solution.py:79
  93.8 4.6 copy.57
  98.4 40.9 %while.26 = (s32[]{:T(128)}, bf16[6,256,192]{1,2,0:T(8,128)(2,1)}, f32[6,3,256]{2,1,0:T(4,128)}, bf16[6,1024,192]{1,2,0:T(8,128)(2,1)}, s32[6,256]{1,0:T(8,128)}...) while((s32[]{:T(128)}, bf16[6,256,192]{1,2,0:T(8,128)(2,1)}, ...), condition=%wide.region_3.4_spmd, body=%wide.region_0.3_spmd.sunk | while | flops 211074304 | bytes 13475965 | solution.py:98
  141.7 3.0 fusion.70
  146.2 170.6 %all-reduce.6.cloned.1.call-done = f32[1536,768]{1,0:T(8,128)} async-done(((f32[1536,768]{1,0:T(8,128)}), f32[1536,768]{1,0:T(8,128)}) %all-reduce.6.cloned.1.call-update) | async-done | bytes 4718608 | tf_op jit(solution)/shard_map/psum | solution.py:101
  316.8 3.8 fusion.61
  323.6 14.6 %fusion.26 = (bf16[1536,768]{1,0:T(8,128)(2,1)S(1)}, f32[1536,768]{1,0:T(8,128)}) fusion(f32[768]{0:T(1024)S(1)} %copy-done.37, bf16[768,768]{1,0:T(8,128)(2,1)} %all-gather.9.cloned.1.call-done, f32[1536,768]{1,0:T(8,128)} %copy-done, f32[768]{0:T(1024)S(1)} %copy-done.31, f32[768]{0:T(1024)S(1)} %copy-done.19, f32[1536]{0:T(1024)S(1)} %add_rsqrt_fusion.1, ...), kind=kOutput, calls=%fused_computation.47 | convolution fusion | flops 1895694336 | bytes 12997632 | tf_op jit(solution)/shard_map/dot_general | solution.py:105
  339.6 5.5 fusion.71
  348.4 167.8 %all-reduce.8.cloned.1.call-done = f32[1536,768]{1,0:T(8,128)} async-done(((f32[1536,768]{1,0:T(8,128)}), f32[1536,768]{1,0:T(8,128)}) %all-reduce.8.cloned.1.call-update) | async-done | bytes 4718608 | tf_op jit(solution)/shard_map/psum | solution.py:108
  516.2 4.7 fusion.60
  521.6 2.7 fusion.38
  524.3 3.7 fusion.57
  528.1 4.0 fusion.65
  533.6 4.1 fusion.52
  538.0 170.9 %all-reduce.10.cloned.1.call-done = f32[1536,768]{1,0:T(8,128)} async-done(((f32[1536,768]{1,0:T(8,128)}), f32[1536,768]{1,0:T(8,128)}) %all-reduce.10.cloned.1.call-update) | async-done | bytes 4718608 | tf_op jit(solution)/shard_map/psum | solution.py:130
  708.9 7.1 multiply_reduce_fusion.1
  716.0 4.5 fusion.59
  723.7 123.8 %while.27 = (s32[]{:T(128)}, f32[6,256,192]{1,2,0:T(8,128)}, f32[6,1024,192]{1,2,0:T(8,128)}, f32[6,1024,192]{1,2,0:T(8,128)}, bf16[6,1024,192]{1,2,0:T(8,128)(2...) while((s32[]{:T(128)}, f32[6,256,192]{1,2,0:T(8,128)}, ...), condition=%wide.region_17.18_spmd, body=%wide.region_15.17_spmd.sunk | while | flops 514592256 | bytes 45572424 | solution.py:161
  731.6 3.8 fusion.138
  735.5 4.5 fusion.140
  752.3 3.8 fusion.138
  756.1 4.5 fusion.140
  772.9 3.8 fusion.138
  776.8 4.5 fusion.140
  793.5 3.8 fusion.138
  797.4 4.5 fusion.140
  811.6 2.6 subtract_exponential_fusion.3
  814.2 3.8 fusion.138
  818.0 4.5 fusion.140
  834.7 3.8 fusion.138
  838.6 4.5 fusion.140
  850.8 43.7 %reduce-scatter.9.cloned.1.call-done = f32[6,256,192]{1,2,0:T(8,128)} async-done(((f32[6,1024,192]{1,2,0:T(8,128)}), f32[6,256,192]{1,2,0:T(8,128)}) %reduce-scatter.9.cloned.1.call-update) | async-done | bytes 1179664 | tf_op jit(solution)/shard_map/reduce_scatter | solution.py:165
  896.9 48.2 %reduce-scatter.11.cloned.1.call-done = f32[6,256,192]{1,2,0:T(8,128)} async-done(((f32[6,1024,192]{1,2,0:T(8,128)}), f32[6,256,192]{1,2,0:T(8,128)}) %reduce-scatter.11.cloned.1.call-update) | async-done | bytes 1179664 | tf_op jit(solution)/shard_map/reduce_scatter | solution.py:166
  949.6 3.7 fusion.72
  955.4 5.7 convolution_bitcast_fusion
  961.2 6.9 fusion.54
  968.2 7.0 fusion.50
  975.4 4.3 fusion.47
  979.9 25.9 %all-reduce = (f32[192]{0:T(256)}, f32[192]{0:T(256)}, f32[768]{0:T(1024)}, f32[768]{0:T(1024)}, f32[768]{0:T(1024)}, /*index=5*/f32[768]{0:T(1024)}, f32[768]{0:T(1024)}, f32[768]{0:T(1024)}, f32[768]{0:T(1024)}) all-reduce(f32[192]{0:T(256)S(1)} %get-tuple-element.291, ...), channel_id=1, replica_groups=mesh['dp'=2,'ctx'=4,'tp'=4] {'dp','ctx'}, use_global_device_ids=true, to_apply=%region_23.24 | all-reduce | flops 5760 | bytes 46080 | tf_op jit(solution)/shard_map/psum | solution.py:182
  1007.8 125.5 %all-reduce.12.cloned.1.call-done = f32[1536,768]{1,0:T(8,128)} async-done(((f32[1536,768]{1,0:T(8,128)}), f32[1536,768]{1,0:T(8,128)}) %all-reduce.12.cloned.1.call-update) | async-done | bytes 4718608 | tf_op jit(solution)/shard_map/psum | solution.py:181
  1133.2 6.6 add.172
  (359 shorter events, 151.6 us)
Async XLA Ops:
  8.0 54.6 %all-gather.7.cloned.1.call-start = ((), (), s32[]{:S(2)}) async-start(), calls=%async_computation.7 | async-start | bytes 3932160 | tf_op jit(solution)/shard_map/all_gather | solution.py:78
  24.6 5.4 copy-start.15
  30.1 6.0 copy-start.33
  31.6 62.2 %all-gather.5.cloned.1.call-start = ((), (), s32[]{:S(2)}) async-start(), calls=%async_computation.6 | async-start | bytes 3932160 | tf_op jit(solution)/shard_map/all_gather | solution.py:79
  36.0 7.8 copy-start.17
  37.2 279.6 %all-reduce.6.cloned.1.call-start = ((), (), s32[]{:S(2)}) async-start(), calls=%async_computation.8 | async-start | bytes 9437184 | tf_op jit(solution)/shard_map/psum | solution.py:101
  139.3 5.4 copy-start.5
  141.7 175.2 %copy-start.27 = (f32[768]{0:T(1024)S(1)}, f32[768]{0:T(1024)}, u32[]{:S(2)}) copy-start(f32[768]{0:T(1024)} %param.26) | copy-start | bytes 9220
  144.7 178.8 %all-gather.9.cloned.1.call-start = ((), (), s32[]{:S(2)}) async-start(), calls=%async_computation.9 | async-start | bytes 1327104 | tf_op jit(solution)/shard_map/all_gather | solution.py:65
  145.3 192.9 %all-gather.11.cloned.1.call-start = ((), (), s32[]{:S(2)}) async-start(), calls=%async_computation.10 | async-start | bytes 1327104 | tf_op jit(solution)/shard_map/all_gather | solution.py:66
  145.9 370.3 %all-reduce.8.cloned.1.call-start = ((), (), s32[]{:S(2)}) async-start(), calls=%async_computation.11 | async-start | bytes 9437184 | tf_op jit(solution)/shard_map/psum | solution.py:108
  345.1 171.1 %copy-start.30 = (f32[768]{0:T(1024)S(1)}, f32[768]{0:T(1024)}, u32[]{:S(2)}) copy-start(f32[768]{0:T(1024)} %param.32) | copy-start | bytes 9220
  345.1 363.8 %all-reduce.10.cloned.1.call-start = ((), (), s32[]{:S(2)}) async-start(), calls=%async_computation.12 | async-start | bytes 9437184 | tf_op jit(solution)/shard_map/psum | solution.py:130
  521.6 6.5 slice-start
  528.1 5.5 copy-start.35
  537.8 356.7 %reduce-scatter.9.cloned.1.call-start = ((), (), s32[]{:S(2)}) async-start(), calls=%async_computation.13 | async-start | bytes 5898240 | tf_op jit(solution)/shard_map/reduce_scatter | solution.py:165
  723.7 4.5 copy-start.9
  723.7 4.5 copy-start.12
  740.0 4.4 copy-start.10
  740.0 4.4 copy-start.13
  744.4 4.5 copy-start.9
  744.4 4.5 copy-start.12
  765.1 4.5 copy-start.9
  765.1 4.5 copy-start.12
  781.3 4.4 copy-start.10
  781.3 4.4 copy-start.13
  785.7 4.5 copy-start.9
  785.7 4.5 copy-start.12
  806.3 4.5 copy-start.9
  806.3 4.5 copy-start.12
  826.9 4.5 copy-start.9
  826.9 4.5 copy-start.12
  847.5 97.6 %reduce-scatter.11.cloned.1.call-start = ((), (), s32[]{:S(2)}) async-start(), calls=%async_computation.14 | async-start | bytes 5898240 | tf_op jit(solution)/shard_map/reduce_scatter | solution.py:166
  848.3 157.5 %reduce-scatter.19.cloned.1.call-start = ((), (), s32[]{:S(2)}) async-start(), calls=%async_computation.19 | async-start | bytes 2211840
  955.2 178.1 %all-reduce.12.cloned.1.call-start = ((), (), s32[]{:S(2)}) async-start(), calls=%async_computation.15 | async-start | bytes 9437184 | tf_op jit(solution)/shard_map/psum | solution.py:181
  961.1 7.1 copy-start.20
  961.1 7.1 copy-start.32
  961.2 178.6 %reduce-scatter.17.cloned.1.call-start = ((), (), s32[]{:S(2)}) async-start(), calls=%async_computation.18 | async-start | bytes 2654208 | tf_op jit(solution)/shard_map/reduce_scatter | solution.py:179
  968.2 7.3 copy-start.8
  968.2 171.6 %reduce-scatter.15.cloned.1.call-start = ((), (), s32[]{:S(2)}) async-start(), calls=%async_computation.17 | async-start | bytes 2654208 | tf_op jit(solution)/shard_map/reduce_scatter | solution.py:178
  975.3 4.5 copy-start.21
  975.3 4.5 copy-start.22
  975.3 4.5 copy-start.23
  975.3 4.5 copy-start.24
  975.3 4.5 copy-start.25
  975.3 4.5 copy-start.26
  975.3 4.5 copy-start.29
  975.4 164.4 %reduce-scatter.13.cloned.1.call-start = ((), (), s32[]{:S(2)}) async-start(), calls=%async_computation.16 | async-start | bytes 884736 | tf_op jit(solution)/shard_map/reduce_scatter | solution.py:177
  (38 other events, 101.3 us)
Sparse Core Ops, SparseCore 0:
  31.7 30.8 all-gather.6
  64.8 28.9 all-gather.4
  144.8 171.9 all-reduce.5
  345.2 170.9 all-reduce.7
  537.9 170.9 all-reduce.9
  847.7 46.8 reduce-scatter.8
  897.2 47.8 reduce-scatter.10
  961.3 171.9 all-reduce.11
Sparse Core Ops, SparseCore 1:
  147.1 23.9 all-gather.8
  172.8 23.9 all-gather.10
  955.2 40.2 reduce-scatter.18
  999.8 42.4 reduce-scatter.16
  1046.2 42.3 reduce-scatter.14
  1092.6 34.9 reduce-scatter.12
where the time goes:
time: 1150 us
  waiting for transfers between devices  764 us (66%)
  matrix products  159 us (14%)
  local copies, waits for them, and re-layouts  95.9 us (8%)
  blocking collectives  57.6 us (5%)
  other arithmetic  52.4 us (5%)
  between operations  16.5 us (1%)
    psum x1, waiting for transfers between devices, per_device(): d_normed = lax.psum(hidden_part, 'tp') + d_second  171 us
    psum x1, waiting for transfers between devices, per_device(): attended = lax.psum(attn_part, 'tp') + out_bias  171 us
    psum x1, waiting for transfers between devices, per_device(): second = normed + lax.psum(ffn_part, 'tp') + back_bias  168 us
    psum x1, waiting for transfers between devices, per_device(): d_tokens = lax.psum(input_part, 'tp') + d_first  125 us
    reduce_scatter x1, waiting for transfers between devices, per_device(): lax.psum_scatter(value_part, 'ctx', scatter_dimension=1, tiled=True)  48.2 us
    reduce_scatter x1, waiting for transfers between devices, per_device(): lax.psum_scatter(key_part, 'ctx', scatter_dimension=1, tiled=True)  43.7 us
    dynamic_slice x60, local copies, waits for them, and re-layouts, per_device(): lax.map(attend, (query, key_full, value_full, segments, seg_full))  36.6 us
    all_gather x1, waiting for transfers between devices, per_device(): lax.all_gather(value, 'ctx', axis=1, tiled=True)  28 us
  transfers between devices with their start and end apart: 14, of which 8 were waited for; matrix products, arithmetic and copies ran while one was open for 6% of the time, Pallas kernels for 0%

commit v1 on v0

v1 whole, which is shorter than its diff:
```python
import functools
import math

import jax
import jax.numpy as jnp
from jax import lax
from jax.experimental import pallas as pl
from jax.experimental.pallas import tpu as pltpu
from jax.sharding import PartitionSpec as P

HEAD = 64
NEG = -1e30
BF = jnp.bfloat16
F32 = jnp.float32
ALL = ("dp", "ctx", "tp")


def norm_parts(value):
    mean = jnp.mean(value, -1, keepdims=True)
    centered = value - mean
    rstd = lax.rsqrt(jnp.mean(centered * centered, -1, keepdims=True) + 1e-12)
    return (centered * rstd, rstd)


def norm_back(grad, normal, rstd, gain):
    d_gain = jnp.sum(grad * normal, 0)
    d_shift = jnp.sum(grad, 0)
    scaled = grad * gain
    d_value = rstd * (
        scaled
        - jnp.mean(scaled, -1, keepdims=True)
        - normal * jnp.mean(scaled * normal, -1, keepdims=True)
    )
    return (d_value, d_gain, d_shift)


def gelu_slope(inner):
    return 0.5 * (1.0 + lax.erf(inner / math.sqrt(2.0))) + inner * jnp.exp(
        -0.5 * inner * inner
    ) / math.sqrt(2.0 * math.pi)


def swap_with(value, axis, size, mask):
    return lax.ppermute(value, axis, [(i, i ^ mask) for i in range(size)])


def in_order(parts, me, axis=0):
    shape = list(parts[0].shape)
    shape.insert(axis, len(parts))
    out = jnp.zeros(tuple(shape), parts[0].dtype)
    for k, part in enumerate(parts):
        out = lax.dynamic_update_index_in_dim(out, part, me ^ k, axis)
    return out


def gather_axis(value, axis, size, me):
    parts = [value] + [swap_with(value, axis, size, k) for k in range(1, size)]
    return in_order(parts, me)


def exchange_axis(blocks, axis, size, me):
    parts = [lax.dynamic_index_in_dim(blocks, me, 0, keepdims=False)]
    for k in range(1, size):
        parts.append(
            swap_with(lax.dynamic_index_in_dim(blocks, me ^ k, 0, keepdims=False), axis, size, k)
        )
    return parts


def gather_weight(shard, sizes, me):
    nd, nc, nt = sizes
    d, c, z = me
    zset = gather_axis(shard, "tp", nt, z)
    if nd != 2:
        full = lax.all_gather(zset, ("dp", "ctx"), axis=1, tiled=False)
        return full
    half = nt // 2
    px = swap_with(zset, "dp", nd, 1)
    py = swap_with(zset, "ctx", nc, 2)
    pd = jnp.concatenate(
        [swap_with(px[:half], "ctx", nc, 2), swap_with(py[half:], "dp", nd, 1)], 0
    )
    own = [zset, px, py, pd]
    other = [swap_with(v, "ctx", nc, 1) for v in own]
    row = d * nc + c
    out = jnp.zeros((nt, nd * nc) + shard.shape, shard.dtype)
    for core, group in ((0, own), (1, other)):
        for k, part in enumerate(group):
            at = row ^ (core + (nc if k in (1, 3) else 0) + (2 if k in (2, 3) else 0))
            out = lax.dynamic_update_index_in_dim(out, part, at, 1)
    return out


def add_low(a, b):
    return (a.astype(F32) + b.astype(F32)).astype(BF)


def scatter_weight(grad, sizes, me):
    nd, nc, nt = sizes
    d, c, z = me
    if nd != 2:
        part = lax.psum_scatter(
            grad.astype(F32), ("dp", "ctx"), scatter_dimension=1, tiled=False
        ).astype(BF)
    else:
        rows, cols = grad.shape[2:]
        view = grad.reshape(nt, nd, nc // 2, 2, rows, cols)
        core = c % 2
        y = c // 2
        keep = lax.dynamic_index_in_dim(view, core, 3, keepdims=False)
        send = lax.dynamic_index_in_dim(view, 1 - core, 3, keepdims=False)
        a = add_low(keep, swap_with(send, "ctx", nc, 1))
        half = nt // 2
        one, two = a[:half], a[half:]
        r1 = swap_with(lax.dynamic_index_in_dim(one, 1 - d, 1, keepdims=False), "dp", nd, 1)
        r2 = swap_with(lax.dynamic_index_in_dim(two, 1 - y, 2, keepdims=False), "ctx", nc, 2)
        one = add_low(lax.dynamic_index_in_dim(one, d, 1, keepdims=False), r1)
        two = add_low(lax.dynamic_index_in_dim(two, y, 2, keepdims=False), r2)
        r1 = swap_with(lax.dynamic_index_in_dim(one, 1 - y, 1, keepdims=False), "ctx", nc, 2)
        r2 = swap_with(lax.dynamic_index_in_dim(two, 1 - d, 1, keepdims=False), "dp", nd, 1)
        one = add_low(lax.dynamic_index_in_dim(one, y, 1, keepdims=False), r1)
        two = add_low(lax.dynamic_index_in_dim(two, d, 1, keepdims=False), r2)
        part = jnp.concatenate([one, two], 0)
    parts = exchange_axis(part, "tp", nt, z)
    return sum(p.astype(F32) for p in parts)


def transpose_ctx_tp(value, n):
    pairs = [(a * n + b, b * n + a) for a in range(n) for b in range(n)]
    return lax.ppermute(value, ("ctx", "tp"), pairs)


def pair_perm(value, sizes, kd, kt):
    nd, _, nt = sizes
    pairs = [
        (a * nt + b, (a ^ kd) * nt + (b ^ kt)) for a in range(nd) for b in range(nt)
    ]
    return lax.ppermute(value, ("dp", "tp"), pairs)


def gather_heads(shard, sizes, me):
    nd, nc, nt = sizes
    d, c, z = me
    mine = transpose_ctx_tp(shard, nc)
    if nd != 2:
        return lax.all_gather(mine, ("dp", "tp"), axis=0, tiled=True)
    out = jnp.zeros((nd * nt,) + shard.shape, shard.dtype)
    for kd in range(nd):
        for kt in range(nt):
            part = pair_perm(mine, sizes, kd, kt) if kd or kt else mine
            out = lax.dynamic_update_index_in_dim(out, part, (d ^ kd) * nt + (z ^ kt), 0)
    return out.reshape((nd * nt * shard.shape[0],) + shard.shape[1:])


def scatter_heads(grad, sizes, me):
    nd, nc, nt = sizes
    d, c, z = me
    blocks = grad.reshape((nd * nt, grad.shape[0] // (nd * nt)) + grad.shape[1:])
    if nd != 2:
        total = lax.psum_scatter(
            blocks.astype(F32), ("dp", "tp"), scatter_dimension=0, tiled=False
        )
    else:
        total = 0.0
        for kd in range(nd):
            for kt in range(nt):
                block = lax.dynamic_index_in_dim(
                    blocks, (d ^ kd) * nt + (z ^ kt), 0, keepdims=False
                )
                if kd or kt:
                    block = pair_perm(block, sizes, kd, kt)
                total = total + block.astype(F32)
    return transpose_ctx_tp(total, nc)


def sum_all(value, sizes):
    nd, nc, nt = sizes
    if nd != 2:
        return lax.psum(value, ALL)
    for axis, size, mask in (
        ("ctx", nc, 1),
        ("ctx", nc, 2),
        ("dp", nd, 1),
        ("tp", nt, 1),
        ("tp", nt, 2),
    ):
        value = value + swap_with(value, axis, size, mask)
    return value


def block_rows(qb, half, ln):
    hl = ln // 2
    whole = qb < 4
    b = jnp.where(whole, qb, qb - 4)
    r0 = jnp.where(whole, 2 * ln * b, (4 * b + 1) * ln + hl * half)
    r1 = jnp.where(whole, r0 + hl, r0 + 2 * ln)
    o0 = jnp.where(whole, 3 * hl * b, 6 * hl * b + ln)
    o1 = jnp.where(whole, o0 + hl, o0 + 3 * hl)
    seq = jnp.where(whole, 0, 1)
    m = lambda v: pl.multiple_of(v, 128)
    return m(r0), m(r1), m(o0), m(o1), seq


def two(ref, r0, r1, hl, cols):
    return jnp.concatenate([ref[pl.ds(r0, hl), cols], ref[pl.ds(r1, hl), cols]], 0)


def two_lanes(ref, rows, r0, r1, hl):
    return jnp.concatenate([ref[rows, pl.ds(r0, hl)], ref[rows, pl.ds(r1, hl)]], 1)


def dot_nt(a, b):
    return lax.dot_general(a, b, (((1,), (1,)), ((), ())), preferred_element_type=F32)


def dot_nn(a, b):
    return lax.dot_general(a, b, (((1,), (0,)), ((), ())), preferred_element_type=F32)


def fill_transposed(kv, kvt, ln, nc, heads):
    @pl.loop(0, nc)
    def _(j):
        for seq in range(2):
            rows = pl.ds(pl.multiple_of((2 * j + seq) * ln, ln), ln)
            for h in range(heads):
                kvt[seq * heads + h, :, pl.ds(pl.multiple_of(j * ln, ln), ln)] = kv[
                    rows, 128 * h : 128 * h + 128
                ].T


def attend_kernel(heads, ln, nc, info, q_ref, kv, seg_col, seg_row, out, lse, ctx_t, s_scr, kvt, acc):
    half = info[12]
    hl = ln // 2
    fill_transposed(kv, kvt, ln, nc, heads)

    @pl.loop(0, 6)
    def _(qb):
        r0, r1, o0, o1, seq = block_rows(qb, half, ln)
        lo, hi = info[qb], info[6 + qb]
        sq = two_lanes(seg_row, slice(0, 1), r0, r1, hl)
        q = [two(q_ref, r0, r1, hl, slice(128 * h, 128 * h + 128)) for h in range(heads)]

        def score(j, peaks):
            rows = pl.ds(pl.multiple_of((2 * j + seq) * ln, ln), ln)
            same = seg_col[rows, :] == sq
            new = []
            for h in range(heads):
                s = dot_nt(kv[rows, 128 * h : 128 * h + 128], q[h])
                s = jnp.where(same, s, NEG)
                s_scr[h, pl.ds(pl.multiple_of(j * ln, ln), ln), :] = s
                new.append(jnp.maximum(peaks[h], jnp.max(s, 0, keepdims=True)))
            return tuple(new)

        peaks = lax.fori_loop(
            lo, hi, score, tuple(jnp.full((1, ln), NEG, F32) for _ in range(heads))
        )
        acc[...] = jnp.zeros_like(acc)

        def collect(j, sums):
            keys = pl.ds(pl.multiple_of(j * ln, ln), ln)
            new = []
            for h in range(heads):
                p = jnp.exp(s_scr[h, keys, :] - peaks[h])
                new.append(sums[h] + jnp.sum(p, 0, keepdims=True))
                acc[h] += dot_nn(kvt[seq * heads + h, :, keys], p.astype(BF))
            return tuple(new)

        sums = lax.fori_loop(
            lo, hi, collect, tuple(jnp.zeros((1, ln), F32) for _ in range(heads))
        )
        whole = []
        for h in range(heads):
            one = acc[h, HEAD:, :] / sums[h]
            whole.append(one)
            line = peaks[h] + jnp.log(sums[h])
            for part, at in ((0, o0), (hl, o1)):
                ctx_t[HEAD * h : HEAD * h + HEAD, pl.ds(at, hl)] = one[:, part : part + hl]
                lse[h : h + 1, pl.ds(at, hl)] = line[:, part : part + hl]
        turned = jnp.concatenate(whole, 0).T.astype(BF)
        out[pl.ds(o0, hl), :] = turned[:hl]
        out[pl.ds(o1, hl), :] = turned[hl:]


def attend(info, q_ref, kv, seg_col, seg_row, heads, ln, nc):
    rows = 3 * ln // 2 * nc
    vm = pl.BlockSpec(memory_space=pltpu.VMEM)
    return pl.pallas_call(
        functools.partial(attend_kernel, heads, ln, nc),
        out_shape=(
            jax.ShapeDtypeStruct((rows, heads * HEAD), BF),
            jax.ShapeDtypeStruct((8, rows), F32),
            jax.ShapeDtypeStruct((heads * HEAD, rows), F32),
        ),
        in_specs=[pl.BlockSpec(memory_space=pltpu.SMEM), vm, vm, vm, vm],
        out_specs=(vm, vm, vm),
        scratch_shapes=[
            pltpu.VMEM((heads, nc * ln, ln), F32),
            pltpu.VMEM((2 * heads, 128, nc * ln), BF),
            pltpu.VMEM((heads, 128, ln), F32),
        ],
        compiler_params=pltpu.CompilerParams(vmem_limit_bytes=32 << 20),
        cost_estimate=pl.CostEstimate(
            flops=8 * heads * rows * nc * ln * 128,
            bytes_accessed=8 << 20,
            transcendentals=heads * rows * nc * ln,
        ),
        name="attend",
    )(info, q_ref, kv, seg_col, seg_row)


def attend_back_kernel(
    heads, ln, nc, info, q_ref, kv, d_out, seg_col, seg_row, lse, ctx_t, d_q, d_kv, d_bias, dkv, kvt, dqt
):
    half = info[12]
    hl = ln // 2
    fill_transposed(kv, kvt, ln, nc, heads)
    dkv[...] = jnp.zeros_like(dkv)
    d_bias[...] = jnp.zeros_like(d_bias)

    @pl.loop(0, nc)
    def _(c):
        rows = pl.ds(pl.multiple_of((2 * c + 1) * ln, ln), ln)
        d_q[rows, :] = jnp.zeros((ln, heads * HEAD), BF)

    @pl.loop(0, 6)
    def _(qb):
        r0, r1, o0, o1, seq = block_rows(qb, half, ln)
        lo, hi = info[qb], info[6 + qb]
        sq = two_lanes(seg_row, slice(0, 1), r0, r1, hl)
        q, do, line, delta = [], [], [], []
        for h in range(heads):
            q.append(two(q_ref, r0, r1, hl, slice(128 * h, 128 * h + 128)))
            do.append(two(d_out, o0, o1, hl, slice(128 * h, 128 * h + 128)))
            line.append(two_lanes(lse, slice(h, h + 1), o0, o1, hl))
            turned = do[h].astype(F32).T[HEAD:, :]
            kept = two_lanes(ctx_t, slice(HEAD * h, HEAD * h + HEAD), o0, o1, hl)
            delta.append(jnp.sum(turned * kept, 0, keepdims=True))
        dqt[...] = jnp.zeros_like(dqt)

        @pl.loop(lo, hi)
        def _(j):
            rows = pl.ds(pl.multiple_of((2 * j + seq) * ln, ln), ln)
            keys = pl.ds(pl.multiple_of(j * ln, ln), ln)
            same = seg_col[rows, :] == sq
            for h in range(heads):
                kvh = kv[rows, 128 * h : 128 * h + 128]
                p = jnp.where(same, jnp.exp(dot_nt(kvh, q[h]) - line[h]), 0.0)
                ds = (p * (dot_nt(kvh, do[h]) - delta[h])).astype(BF)
                dkv[rows, 128 * h : 128 * h + 128] += dot_nn(ds, q[h]) + dot_nn(
                    p.astype(BF), do[h]
                )
                dqt[h] += dot_nn(kvt[seq * heads + h, :, keys], ds)

        turned = jnp.concatenate([dqt[h, :HEAD, :] for h in range(heads)], 0).T * 0.125
        d_bias[0:1, heads * 128 :] += jnp.sum(turned, 0, keepdims=True)
        low = turned.astype(BF)
        d_q[pl.ds(r0, hl), :] = low[:hl]
        d_q[pl.ds(r1, hl), :] = low[hl:]

    @pl.loop(0, 2 * nc)
    def _(c):
        rows = pl.ds(pl.multiple_of(c * ln, ln), ln)
        for h in range(heads):
            got = dkv[rows, 128 * h : 128 * h + 128]
            d_bias[0:1, 128 * h : 128 * h + 128] += jnp.sum(got, 0, keepdims=True)
            d_kv[rows, 128 * h : 128 * h + 128] = got.astype(BF)


def attend_back(info, q_ref, kv, d_out, seg_col, seg_row, lse, ctx_t, heads, ln, nc):
    rows = 3 * ln // 2 * nc
    vm = pl.BlockSpec(memory_space=pltpu.VMEM)
    return pl.pallas_call(
        functools.partial(attend_back_kernel, heads, ln, nc),
        out_shape=(
            jax.ShapeDtypeStruct((2 * nc * ln, heads * HEAD), BF),
            jax.ShapeDtypeStruct((2 * nc * ln, heads * 128), BF),
            jax.ShapeDtypeStruct((8, heads * (HEAD + 128)), F32),
        ),
        in_specs=[pl.BlockSpec(memory_space=pltpu.SMEM)] + [vm] * 7,
        out_specs=(vm, vm, vm),
        scratch_shapes=[
            pltpu.VMEM((2 * nc * ln, heads * 128), F32),
            pltpu.VMEM((2 * heads, 128, nc * ln), BF),
            pltpu.VMEM((heads, 128, ln), F32),
        ],
        compiler_params=pltpu.CompilerParams(vmem_limit_bytes=40 << 20),
        cost_estimate=pl.CostEstimate(
            flops=20 * heads * rows * nc * ln * 128,
            bytes_accessed=14 << 20,
            transcendentals=heads * rows * nc * ln,
        ),
        name="attend_back",
    )(info, q_ref, kv, d_out, seg_col, seg_row, lse, ctx_t)


MESH = pl.DeviceIdType.MESH


class Copies:
    def __init__(self, send, recv):
        self.send, self.recv, self.open = send, recv, []

    def make(self, i, src, dst, device):
        return pltpu.make_async_remote_copy(
            src_ref=src,
            dst_ref=dst,
            send_sem=self.send.at[i],
            recv_sem=self.recv.at[i],
            device_id=device,
            device_id_type=MESH,
        )

    def start(self, i, src, dst, device):
        copy = self.make(i, src, dst, device)
        copy.start()
        self.open.append(copy)

    def arrived(self, i, dst, device):
        self.make(i, dst, dst, device).wait_recv()

    def sent(self):
        for copy in self.open:
            copy.wait_send()
        self.open = []


def forward_kernel(
    heads,
    ln,
    tok2,
    seg2,
    w_head,
    b_head,
    b_unit,
    w_o,
    w_i,
    w_b,
    ctx_all,
    x_out,
    q_out,
    kv_out,
    wh_out,
    o_full,
    i_full,
    b_full,
    bu_full,
    lse,
    ctx_t,
    seg,
    x2,
    wh,
    bh,
    q_scr,
    kv,
    s_scr,
    kvt,
    acc,
    segc,
    segr,
    context,
    send,
    recv,
    local,
):
    d, c, z = (lax.axis_index(n) for n in ALL)
    nc = 4
    hl = ln // 2
    own = ln + hl
    half = z % 2
    wr = w_i.shape[0]
    units = w_i.shape[1]
    row = d * nc + c
    rc = Copies(send, recv)
    at_c = lambda k: (d, c ^ k, z)
    at_x = (1 - d, c, z)
    at_xz = lambda kd, kt: (d ^ kd, c, z ^ kt)
    across = (d, z, c)
    pairs = [(kd, kt) for kd in range(2) for kt in range(4) if kd or kt]

    barrier = pltpu.get_barrier_semaphore()
    everyone = [at_c(k) for k in (1, 2, 3)] + [at_xz(*p) for p in pairs]
    for device in everyone:
        pl.semaphore_signal(barrier, inc=1, device_id=device, device_id_type=MESH)

    @pl.when(c != z)
    def _():
        pl.semaphore_signal(barrier, inc=1, device_id=across, device_id_type=MESH)

    pl.semaphore_wait(barrier, len(everyone) + jnp.where(c != z, 1, 0))

    number = iter(range(100))
    locals_ = []

    def copy_here(src, dst):
        copy = pltpu.make_async_copy(src, dst, local.at[len(locals_)])
        copy.start()
        locals_.append(copy)
        return copy

    n_ty, n_tc, n_tf = next(number), next(number), next(number)
    tok_at = lambda i: x2.at[pl.ds(2 * i, 2)]
    rc.start(n_ty, tok2, tok_at(c), at_c(2))
    n_wa, n_ba = next(number), next(number)
    wh_at = lambda r: wh.at[pl.ds(pl.multiple_of(r * wr, wr), wr)]

    def across_copies():
        return (
            rc.make(n_wa, w_head, wh_at(row), across),
            rc.make(n_ba, b_head, bh, across),
        )

    @pl.when(c != z)
    def _():
        for copy in across_copies():
            copy.start()

    mine = copy_here(tok2, tok_at(c))
    here = [
        pltpu.make_async_copy(w_head, wh_at(row), local.at[30]),
        pltpu.make_async_copy(b_head, bh, local.at[31]),
    ]

    @pl.when(c == z)
    def _():
        for copy in here:
            copy.start()

    rc.start(n_tc, tok2, tok_at(c), at_c(1))
    n_seg = [next(number) for _ in range(3)]
    for k in (1, 2, 3):
        rc.start(n_seg[k - 1], seg2, seg.at[c], at_c(k))
    seg_here = copy_here(seg2, seg.at[c])
    bu_here = copy_here(b_unit, bu_full.at[z])
    i_at = lambda r, t: i_full.at[r, :, pl.ds(pl.multiple_of(t * units, 128), units)]
    b_at = lambda r, t: b_full.at[r, :, pl.ds(pl.multiple_of(t * units, 128), units)]
    o_at = lambda r, t: o_full.at[t, r]
    w_here = [
        copy_here(w_o, o_at(row, z)),
        copy_here(w_i, i_at(row, z)),
        copy_here(w_b, b_at(row, z)),
    ]

    row_w = d * nc + z

    @pl.when(c != z)
    def _():
        for copy in across_copies():
            copy.wait_recv()

    @pl.when(c == z)
    def _():
        for copy in here:
            copy.wait()

    n_wx = [next(number) for _ in pairs]
    for i, p in zip(n_wx, pairs):
        rc.start(i, wh_at(row_w), wh_at(row_w), at_xz(*p))

    n_bu = [next(number) for _ in range(3)]
    n_z = [[next(number) for _ in range(3)] for _ in range(3)]
    full_at = (o_at, i_at, b_at)
    for k in (1, 2, 3):
        rc.start(n_bu[k - 1], b_unit, bu_full.at[z], at_xz(0, k))
    for w, src in enumerate((w_o, w_i, w_b)):
        for k in (1, 2, 3):
            rc.start(n_z[w][k - 1], src, full_at[w](row, z), at_xz(0, k))

    rc.arrived(n_ty, tok_at(c ^ 2), at_c(2))
    rc.start(n_tf, tok_at(c ^ 2), tok_at(c ^ 2), at_c(1))
    for k in (1, 2, 3):
        rc.arrived(n_seg[k - 1], seg.at[c ^ k], at_c(k))
    seg_here.wait()
    q_scr[...] = jnp.zeros_like(q_scr)
    for i in range(nc):
        for s in range(2):
            line = seg[i, s : s + 1, :].astype(F32)
            segr[2 * i + s, 0:1, :] = line
            segc[2 * i + s] = jnp.broadcast_to(line, (128, ln)).T
    for i, (kd, kt) in zip(n_wx, pairs):
        rc.arrived(i, wh_at((d ^ kd) * nc + (z ^ kt)), at_xz(kd, kt))
    mine.wait()
    rc.arrived(n_tc, tok_at(c ^ 1), at_c(1))
    rc.arrived(n_tf, tok_at(c ^ 3), at_c(1))
    x_here = copy_here(x2, x_out)
    wh_here = copy_here(wh, wh_out)
    wide = heads * 128

    @pl.loop(0, 2 * nc)
    def _(i):
        x = x2[i]
        rows = pl.ds(pl.multiple_of(i * ln, ln), ln)
        got = (dot_nn(x, wh[:, :wide]) + bh[0:1, :wide]).astype(BF)
        kv[rows, :] = got
        qp = ((dot_nn(x, wh[:, wide:]) + bh[0:1, wide:]).astype(BF).astype(F32) * 0.125).astype(BF)
        for h in range(heads):
            q_scr[rows, 128 * h : 128 * h + HEAD] = qp[:, HEAD * h : HEAD * h + HEAD]

    q_here = copy_here(q_scr, q_out)
    kv_here = copy_here(kv, kv_out)

    @pl.loop(0, nc)
    def _(j):
        for s in range(2):
            rows = pl.ds(pl.multiple_of((2 * j + s) * ln, ln), ln)
            for h in range(heads):
                kvt[s * heads + h, :, pl.ds(pl.multiple_of(j * ln, ln), ln)] = kv[
                    rows, 128 * h : 128 * h + 128
                ].T

    groups = ((0, 1), (2,))
    row_at = (lambda r: o_full.at[:, r], lambda r: i_full.at[r], lambda r: b_full.at[r])
    hw = wr // 2
    low_at = (
        lambda r: o_full.at[:, r, pl.ds(0, hw)],
        lambda r: i_full.at[r, pl.ds(0, hw)],
        lambda r: b_full.at[r, pl.ds(0, hw)],
    )
    high_at = (
        lambda r: o_full.at[:, r, pl.ds(hw, hw)],
        lambda r: i_full.at[r, pl.ds(hw, hw)],
        lambda r: b_full.at[r, pl.ds(hw, hw)],
    )
    n_x, n_y, n_d1, n_d2 = ([next(number) for _ in range(3)] for _ in range(4))
    n_c = [[next(number) for _ in range(4)] for _ in range(3)]

    def stage_plane(w):
        w_here[w].wait()
        for k in (1, 2, 3):
            rc.arrived(n_z[w][k - 1], full_at[w](row, z ^ k), at_xz(0, k))
        rc.start(n_x[w], row_at[w](row), row_at[w](row), at_x)
        rc.start(n_y[w], row_at[w](row), row_at[w](row), at_c(2))
        rc.start(n_c[w][0], row_at[w](row), row_at[w](row), at_c(1))

    row_x, row_y, row_d = row ^ 4, row ^ 2, row ^ 6

    def stage_corner(w):
        rc.arrived(n_x[w], row_at[w](row_x), at_x)
        rc.start(n_d1[w], low_at[w](row_x), low_at[w](row_x), at_c(2))
        rc.start(n_c[w][1], row_at[w](row_x), row_at[w](row_x), at_c(1))
        rc.arrived(n_y[w], row_at[w](row_y), at_c(2))
        rc.start(n_d2[w], high_at[w](row_y), high_at[w](row_y), at_x)
        rc.start(n_c[w][2], row_at[w](row_y), row_at[w](row_y), at_c(1))

    def stage_core(w):
        rc.arrived(n_d1[w], low_at[w](row_d), at_c(2))
        rc.arrived(n_d2[w], high_at[w](row_d), at_x)
        rc.start(n_c[w][3], row_at[w](row_d), row_at[w](row_d), at_c(1))

    def stage_end(w):
        for i, r in zip(n_c[w], (row, row_x, row_y, row_d)):
            rc.arrived(i, row_at[w](r ^ 1), at_c(1))

    def block(qb):
        r0, r1, o0, o1, seq = block_rows(qb, half, ln)
        b0 = jnp.where(qb < 4, qb, 2 * (qb - 4))
        b1 = jnp.where(qb < 4, qb, 2 * (qb - 4) + 1)
        s0 = pl.multiple_of(jnp.where(qb < 4, 0, hl * half), 128)
        s1 = pl.multiple_of(jnp.where(qb < 4, hl, hl * half), 128)
        sq = jnp.concatenate(
            [
                segr[2 * b0 + seq, 0:1, pl.ds(s0, hl)],
                segr[2 * b1 + seq, 0:1, pl.ds(s1, hl)],
            ],
            1,
        )
        q = [two(q_scr, r0, r1, hl, slice(128 * h, 128 * h + 128)) for h in range(heads)]

        def score(j, peaks):
            rows = pl.ds(pl.multiple_of((2 * j + seq) * ln, ln), ln)
            key_seg = segc[2 * j + seq]
            same = jnp.concatenate([key_seg, key_seg], 1) == sq
            new = []
            for h in range(heads):
                s = dot_nt(kv[rows, 128 * h : 128 * h + 128], q[h])
                s = jnp.where(same, s, NEG)
                s_scr[h, pl.ds(pl.multiple_of(j * ln, ln), ln), :] = s
                new.append(jnp.maximum(peaks[h], jnp.max(s, 0, keepdims=True)))
            return tuple(new)

        peaks = lax.fori_loop(
            0, nc, score, tuple(jnp.full((1, ln), NEG, F32) for _ in range(heads))
        )
        acc[...] = jnp.zeros_like(acc)

        def collect(j, sums):
            keys = pl.ds(pl.multiple_of(j * ln, ln), ln)
            new = []
            for h in range(heads):
                p = jnp.exp(s_scr[h, keys, :] - peaks[h])
                new.append(sums[h] + jnp.sum(p, 0, keepdims=True))
                acc[h] += dot_nn(kvt[seq * heads + h, :, keys], p.astype(BF))
            return tuple(new)

        sums = lax.fori_loop(
            0, nc, collect, tuple(jnp.zeros((1, ln), F32) for _ in range(heads))
        )
        whole = []
        for h in range(heads):
            one = acc[h, HEAD:, :] / sums[h]
            whole.append(one)
            line = peaks[h] + jnp.log(sums[h])
            for part, at in ((0, o0), (hl, o1)):
                ctx_t[HEAD * h : HEAD * h + HEAD, pl.ds(at, hl)] = one[:, part : part + hl]
                lse[h : h + 1, pl.ds(at, hl)] = line[:, part : part + hl]
        turned = jnp.concatenate(whole, 0).T.astype(BF)
        context[pl.ds(o0, hl), :] = turned[:hl]
        context[pl.ds(o1, hl), :] = turned[hl:]

    stage_plane(0)
    stage_plane(1)
    pl.loop(0, 2)(block)
    stage_plane(2)
    pl.loop(2, 4)(block)
    stage_corner(0)
    stage_corner(1)
    pl.loop(4, 6)(block)

    n_ctx = [next(number) for _ in range(3)]
    ctx_at = lambda i: context.at[pl.ds(pl.multiple_of(i * own, 128), own)]
    for k in (1, 2, 3):
        rc.start(n_ctx[k - 1], ctx_at(c ^ k), ctx_all.at[c], at_c(k))
    ctx_here = copy_here(ctx_at(c), ctx_all.at[c])
    stage_corner(2)
    stage_core(0)
    stage_core(1)
    for k in (1, 2, 3):
        rc.arrived(n_ctx[k - 1], ctx_all.at[c ^ k], at_c(k))
        rc.arrived(n_bu[k - 1], bu_full.at[z ^ k], at_xz(0, k))
    stage_core(2)
    for w in range(3):
        stage_end(w)
    for copy in (bu_here, x_here, wh_here, q_here, kv_here, ctx_here):
        copy.wait()
    rc.sent()

    @pl.when(c != z)
    def _():
        for copy in across_copies():
            copy.wait_send()


def forward(tok2, seg2, w_head, b_head, b_unit, w_o, w_i, w_b, heads):
    ln, width = tok2.shape[1:]
    wr, units = w_i.shape
    group = w_o.shape[1]
    nc, nt, nr = 4, 4, 8
    rows = 3 * ln // 2 * nc
    hb = pl.BlockSpec(memory_space=pl.ANY)
    vm = pl.BlockSpec(memory_space=pltpu.VMEM)
    sds = jax.ShapeDtypeStruct
    return pl.pallas_call(
        functools.partial(forward_kernel, heads, ln),
        out_shape=(
            sds((nc, 3 * ln // 2, group), BF),
            sds((2 * nc, ln, width), BF),
            sds((2 * nc * ln, heads * 128), BF),
            sds((2 * nc * ln, heads * 128), BF),
            sds((nr * wr, 3 * group), BF),
            sds((nt, nr, wr, group), BF),
            sds((nr, wr, nt * units), BF),
            sds((nr, wr, nt * units), BF),
            sds((nt, 8, units), F32),
            sds((8, rows), F32),
            sds((group, rows), F32),
            sds((nc, 8, ln), jnp.int32),
        ),
        in_specs=[hb] * 8,
        out_specs=(hb,) * 9 + (vm,) * 3,
        scratch_shapes=[
            pltpu.VMEM((2 * nc, ln, width), BF),
            pltpu.VMEM((nr * wr, 3 * group), BF),
            pltpu.VMEM((8, 3 * group), F32),
            pltpu.VMEM((2 * nc * ln, heads * 128), BF),
            pltpu.VMEM((2 * nc * ln, heads * 128), BF),
            pltpu.VMEM((heads, nc * ln, ln), F32),
            pltpu.VMEM((2 * heads, 128, nc * ln), BF),
            pltpu.VMEM((heads, 128, ln), F32),
            pltpu.VMEM((2 * nc, ln, 128), F32),
            pltpu.VMEM((2 * nc, 8, ln), F32),
            pltpu.VMEM((rows, group), BF),
            pltpu.SemaphoreType.DMA((80,)),
            pltpu.SemaphoreType.DMA((80,)),
            pltpu.SemaphoreType.DMA((32,)),
        ],
        compiler_params=pltpu.CompilerParams(
            vmem_limit_bytes=40 << 20, collective_id=0, has_side_effects=True
        ),
        name="forward",
    )(tok2, seg2, w_head, b_head, b_unit, w_o, w_i, w_b)


def head_order(kinds, heads):
    lead = kinds[0].shape[:-1]
    q, k, v = (a.reshape(lead + (heads, HEAD)) for a in kinds)
    kv = jnp.concatenate([k, v], -1).reshape(lead + (heads * 2 * HEAD,))
    return jnp.concatenate([kv, q.reshape(lead + (heads * HEAD,))], -1)


def head_kinds(value, heads):
    lead = value.shape[:-1]
    kv = value[..., : heads * 2 * HEAD].reshape(lead + (heads, 2, HEAD))
    flat = lambda a: a.reshape(lead + (heads * HEAD,))
    return value[..., heads * 2 * HEAD :], flat(kv[..., 0, :]), flat(kv[..., 1, :])


def forward_plain(sizes, me, tok2, seg2, w_head, b_head, b_unit, w_o, w_i, w_b, heads):
    nd, nc, nt = sizes
    d, c, z = me
    ln, width = tok2.shape[1:]
    hl = ln // 2
    half = z % 2
    group = w_o.shape[1]
    seg_all = gather_axis(seg2, "ctx", nc, c)
    x2 = gather_axis(tok2, "ctx", nc, c).reshape(2 * nc, ln, width)
    wh = gather_heads(w_head, sizes, me)
    bh = transpose_ctx_tp(b_head, nc)[0]
    b_all = gather_axis(b_unit, "tp", nt, z)
    gather = lambda w: lax.all_gather(
        lax.all_gather(w, "tp", axis=1, tiled=True), ("dp", "ctx"), axis=0, tiled=True
    )
    o_full = jnp.transpose(gather(w_o).reshape(width, nt, group), (1, 0, 2))
    proj = (jnp.dot(x2.reshape(-1, width), wh, preferred_element_type=F32) + bh).astype(BF)
    kv = proj[:, : 2 * group]
    q = (proj[:, 2 * group :].astype(F32) * 0.125).astype(BF).reshape(-1, heads, HEAD)
    q = jnp.concatenate([q, jnp.zeros_like(q)], -1).reshape(-1, heads * 128)
    info, seg_col, seg_row = key_blocks(seg_all, half, ln, nc)
    context, lse, ctx_t = attend(info, q, kv, seg_col, seg_row, heads, ln, nc)
    ctx_all = in_order(exchange_axis(context.reshape(nc, ln + hl, group), "ctx", nc, c), c)
    return (
        ctx_all,
        x2,
        q,
        kv,
        wh,
        o_full,
        gather(w_i),
        gather(w_b),
        b_all,
        lse,
        ctx_t,
        seg_all,
    )


def key_blocks(seg_all, half, ln, nc):
    hl = ln // 2
    seg2 = seg_all[:, :2]
    flat = jnp.transpose(seg2, (1, 0, 2)).reshape(2, nc * ln)
    first = jnp.concatenate([seg2[:, 0, 0], jnp.take(seg2[0::2, 1], half * hl, axis=1)])
    last = jnp.concatenate([seg2[:, 0, -1], jnp.take(seg2[1::2, 1], half * hl + hl - 1, axis=1)])
    of = jnp.concatenate(
        [
            jnp.broadcast_to(flat[:1], (nc, nc * ln)),
            jnp.broadcast_to(flat[1:], (nc // 2, nc * ln)),
        ],
        0,
    )
    lo = jnp.sum(of < first[:, None], 1) // ln
    hi = (jnp.sum(of <= last[:, None], 1) + ln - 1) // ln
    info = jnp.concatenate([lo, hi, half[None]]).astype(jnp.int32)
    seg_flat = seg2.reshape(2 * nc * ln)
    return info, seg_flat[:, None], seg_flat[None, :]


def per_device(
    sizes,
    tokens,
    segments,
    w_qkv,
    q_bias,
    v_bias,
    w_out,
    out_bias,
    gain_one,
    shift_one,
    w_in,
    in_bias,
    w_back,
    back_bias,
    gain_two,
    shift_two,
    cotangent,
):
    nd, nc, nt = sizes
    seqs, ln, width = tokens.shape
    hl = ln // 2
    group = w_out.shape[1]
    heads = group // HEAD
    units = w_in.shape[1]
    wr = w_in.shape[0]
    d, c, z = (lax.axis_index(n) for n in ALL)
    me = (d, c, z)
    whole_of = lambda t: (3 * t + 1) // 2
    shared_of = lambda t: 1 + 3 * (t // 2)
    half_of = lambda t: t % 2
    sf, sh, half = whole_of(z), shared_of(z), half_of(z)

    def own_rows(a):
        one = lax.dynamic_index_in_dim(a, sf, 0, keepdims=False)
        two_ = lax.dynamic_index_in_dim(a, sh, 0, keepdims=False)
        return jnp.concatenate([one, lax.dynamic_slice_in_dim(two_, half * hl, hl, 0)], 0)

    def own_pair(a):
        return jnp.stack(
            [
                lax.dynamic_index_in_dim(a, sf, 0, keepdims=False),
                lax.dynamic_index_in_dim(a, sh, 0, keepdims=False),
            ],
            0,
        )

    tok2 = own_pair(tokens)
    seg2 = jnp.concatenate([own_pair(segments), jnp.zeros((6, ln), jnp.int32)], 0)
    w_head = head_order([w_qkv[:, i] for i in range(3)], heads)
    b_head = head_order([q_bias, jnp.zeros_like(q_bias), v_bias], heads)
    b_head = jnp.broadcast_to(b_head[None], (8, 3 * group))
    b_unit = jnp.broadcast_to(in_bias[None], (8, units))
    args = (tok2, seg2, w_head, b_head, b_unit, w_out, w_in, w_back, heads)
    got = forward(*args) if sizes == (2, 4, 4) else forward_plain(sizes, me, *args)
    ctx_all, x2, q, kv, wh, w_o, w_i, w_b, b_in, lse, ctx_t, seg_all = got
    x2 = x2.reshape(2 * nc * ln, width)
    w_o = w_o.reshape(nt, width, group)
    w_i = w_i.reshape(width, nt * units)
    w_b = w_b.reshape(width, nt * units)
    b_in = b_in[:, 0].reshape(nt * units)
    info, seg_col, seg_row = key_blocks(seg_all, half, ln, nc)
    own = ln + hl

    x_own = own_rows(tokens).astype(F32)
    attended = jnp.einsum("gtf,gdf->td", ctx_all, w_o, preferred_element_type=F32) + out_bias
    normal_one, rstd_one = norm_parts(x_own + attended)
    normed = normal_one * gain_one + shift_one
    normed_low = normed.astype(BF)
    inner = jnp.dot(normed_low, w_i, preferred_element_type=F32) + b_in
    active = jax.nn.gelu(inner, approximate=False).astype(BF)
    branch = jnp.einsum("tf,df->td", active, w_b, preferred_element_type=F32)
    second = normed + branch + back_bias
    normal_two, rstd_two = norm_parts(second)
    out_low = (normal_two * gain_two + shift_two).astype(BF)

    def spread_rows(rows_low, dtype):
        out = jnp.zeros((seqs, ln, width), dtype)
        parts = [rows_low] + [swap_with(rows_low, "tp", nt, k) for k in range(1, nt)]
        for k, part in enumerate(parts):
            t = z ^ k
            part = part.astype(dtype)
            out = lax.dynamic_update_slice(out, part[None, :ln], (whole_of(t), 0, 0))
            out = lax.dynamic_update_slice(
                out, part[None, ln:], (shared_of(t), half_of(t) * hl, 0)
            )
        return out

    d_second, d_gain_two, d_shift_two = norm_back(
        own_rows(cotangent).astype(F32), normal_two, rstd_two, gain_two
    )
    d_second_low = d_second.astype(BF)
    d_back_bias = jnp.sum(d_second, 0)
    d_w_back = jnp.einsum("td,tf->df", d_second_low, active, preferred_element_type=F32)
    d_active = jnp.dot(d_second_low, w_b, preferred_element_type=F32)
    d_inner = d_active * gelu_slope(inner)
    d_in_bias = jnp.sum(d_inner, 0)
    d_inner_low = d_inner.astype(BF)
    d_w_in = jnp.einsum("td,tf->df", normed_low, d_inner_low, preferred_element_type=F32)
    d_normed = jnp.einsum("tf,df->td", d_inner_low, w_i, preferred_element_type=F32) + d_second
    d_first, d_gain_one, d_shift_one = norm_back(d_normed, normal_one, rstd_one, gain_one)
    d_first_low = d_first.astype(BF)
    d_out_bias = jnp.sum(d_first, 0)
    d_w_out = jnp.einsum("td,gtf->gdf", d_first_low, ctx_all, preferred_element_type=F32)
    d_ctx = jnp.einsum("td,gdf->gtf", d_first_low, w_o, preferred_element_type=F32).astype(BF)
    d_ctx = in_order(exchange_axis(d_ctx, "ctx", nc, c), c).reshape(nc * own, heads, HEAD)
    d_ctx = jnp.concatenate([jnp.zeros_like(d_ctx), d_ctx], -1).reshape(nc * own, heads * 128)

    nr = nd * nc
    by_unit = lambda g: jnp.transpose(g.astype(BF).reshape(nr, wr, nt, units), (2, 0, 1, 3))
    g_back = scatter_weight(by_unit(d_w_back), sizes, me)
    g_in = scatter_weight(by_unit(d_w_in), sizes, me)
    g_out = scatter_weight(d_w_out.astype(BF).reshape(nt, nr, wr, group), sizes, me)
    output = spread_rows(out_low, BF)
    small = sum_all(
        jnp.concatenate(
            [
                jnp.stack(
                    [d_out_bias, d_gain_one, d_shift_one, d_back_bias, d_gain_two, d_shift_two]
                ).reshape(-1),
                d_in_bias.reshape(-1),
            ]
        ),
        sizes,
    )

    d_q, d_kv, d_bias = attend_back(
        info, q, kv, d_ctx, seg_col, seg_row, lse, ctx_t, heads, ln, nc
    )
    d_proj = jnp.concatenate([d_kv, d_q], -1)
    part = jnp.einsum("tf,df->td", d_proj, wh, preferred_element_type=F32).astype(BF)
    part = part.reshape(nc // 2, 2, 2, ln, width)
    core, y = c % 2, c // 2
    part = add_low(
        lax.dynamic_index_in_dim(part, core, 1, keepdims=False),
        swap_with(lax.dynamic_index_in_dim(part, 1 - core, 1, keepdims=False), "ctx", nc, 1),
    )
    part = add_low(
        lax.dynamic_index_in_dim(part, y, 0, keepdims=False),
        swap_with(lax.dynamic_index_in_dim(part, 1 - y, 0, keepdims=False), "ctx", nc, 2),
    )
    shared = part[1].reshape(2, hl, width)
    shared = lax.dynamic_index_in_dim(shared, half, 0, keepdims=False).astype(F32) + swap_with(
        lax.dynamic_index_in_dim(shared, 1 - half, 0, keepdims=False), "tp", nt, 1
    ).astype(F32)
    d_own = (jnp.concatenate([part[0].astype(F32), shared], 0) + d_first).astype(BF)
    d_tokens = spread_rows(d_own, F32)

    d_wh = jnp.einsum("td,tf->df", x2, d_proj, preferred_element_type=F32).astype(BF)
    g_qkv = jnp.stack(head_kinds(scatter_heads(d_wh, sizes, me), heads), 1)
    d_qb, _, d_vb = head_kinds(d_bias[0], heads)
    qv = jnp.concatenate([d_qb, d_vb])
    slots = lax.dynamic_update_index_in_dim(jnp.zeros((nc, 2 * group), F32), qv, c, 0)
    slots = sum_all(slots, sizes)
    qv = lax.dynamic_index_in_dim(slots, z, 0, keepdims=False)
    wide = small[: 6 * width].reshape(6, width)
    g_in_bias = lax.dynamic_index_in_dim(
        small[6 * width :].reshape(nt, units), z, 0, keepdims=False
    )
    return (
        output,
        d_tokens,
        g_qkv,
        qv[:group],
        qv[group:],
        g_out,
        wide[0],
        wide[1],
        wide[2],
        g_in,
        g_in_bias,
        g_back,
        wide[3],
        wide[4],
        wide[5],
    )


def solution(mesh):
    sizes = tuple(mesh.shape[n] for n in ALL)
    rows = P(("dp", "ctx"), "tp")
    return jax.shard_map(
        functools.partial(per_device, sizes),
        mesh=mesh,
        in_specs=(
            P("dp", "ctx", None),
            P("dp", "ctx"),
            P(("dp", "ctx"), None, "tp"),
            P("tp"),
            P("tp"),
            rows,
            P(),
            P(),
            P(),
            rows,
            P("tp"),
            rows,
            P(),
            P(),
            P(),
            P("dp", "ctx", None),
        ),
        out_specs=(
            P("dp", "ctx", None),
            P("dp", "ctx", None),
            P(("dp", "ctx"), None, "tp"),
            P("tp"),
            P("tp"),
            rows,
            P(),
            P(),
            P(),
            rows,
            P("tp"),
            rows,
            P(),
            P(),
            P(),
        ),
        check_vma=False,
    )
```

time: 1150 us -> 534 us (0.46)
  waiting for transfers between devices: 764 us -> 77.1 us
  starting transfers between devices: 1.69 us -> 142 us
  Pallas kernels: 0 us -> 128 us
  matrix products: 159 us -> 45.6 us
  blocking collectives: 57.6 us -> 0 us
  other arithmetic: 52.4 us -> 16.5 us
  local copies, waits for them, and re-layouts: 95.9 us -> 117 us
  between operations: 16.5 us -> 2.99 us
    psum x4 -> x0, waiting for transfers between devices: 635 us -> none  [the longest x1 171 us: per_device(): d_normed = lax.psum(hidden_part, 'tp') + d_second]
    ppermute x0 -> x54, starting transfers between devices: none -> 142 us  [the longest x46 130 us: swap_with(): return lax.ppermute(value, axis, [(i, i ^ mask) for i in range(size)])]
    pallas_call x0 -> x2, Pallas kernels: none -> 128 us  [the longest x1 106 us: forward(): pl.pallas_call(functools.partial(forward_kernel, heads, ln), out_shape=(s...]
    dot_general x53 -> x11, matrix products: 155 us -> 45.6 us  [the longest x1 12.2 us: per_device(): inner = jnp.dot(normed_low, w_i, preferred_element_type=F32) + b_in]
    reduce_scatter x5 -> x0, waiting for transfers between devices: 92 us -> none  [the longest x1 48.2 us: per_device(): lax.psum_scatter(value_part, 'ctx', scatter_dimension=1, tiled=True)]
    ppermute x0 -> x54, waiting for transfers between devices: none -> 77.1 us  [the longest x46 74.2 us: swap_with(): return lax.ppermute(value, axis, [(i, i ^ mask) for i in range(size)])]
    all_gather x4 -> x0, waiting for transfers between devices: 35.5 us -> none  [the longest x1 28 us: per_device(): lax.all_gather(value, 'ctx', axis=1, tiled=True)]
    all_gather x3 -> x0, blocking collectives: 31.7 us -> none  [the longest x1 14.6 us: per_device(): lax.all_gather(w_qkv, ('dp', 'ctx'), axis=0, tiled=True)]
  transfers between devices with their start and end apart: 14 -> 54, of which waited for: 8 -> 20; matrix products, arithmetic and copies ran while one was open for 6% -> 25% of each run, Pallas kernels for 0% -> 4%
where the time goes in v1:
time: 534 us; the launch traced here: 529 us
  starting transfers between devices  142 us (27%)
  Pallas kernels  128 us (24%)
  local copies, waits for them, and re-layouts  117 us (22%)
  waiting for transfers between devices  77.1 us (14%)
  matrix products  45.6 us (9%)
  other arithmetic  16.5 us (3%)
    ppermute x46, starting transfers between devices, swap_with(): return lax.ppermute(value, axis, [(i, i ^ mask) for i in range(size)])  130 us
    pallas_call x1, Pallas kernels, forward(): pl.pallas_call(functools.partial(forward_kernel, heads, ln), out_shape=(s...  106 us
    ppermute x46, waiting for transfers between devices, swap_with(): return lax.ppermute(value, axis, [(i, i ^ mask) for i in range(size)])  74.2 us
    reshape x4, local copies, waits for them, and re-layouts, per_device(): g.astype(BF).reshape(nr, wr, nt, units)  26 us
    pallas_call x1, Pallas kernels, attend_back(): pl.pallas_call(functools.partial(attend_back_kernel, heads, ln, nc), out_...  21.4 us
    unnamed x114, local copies, waits for them, and re-layouts  20.7 us
    dynamic_update_slice x4, local copies, waits for them, and re-layouts, in_order(): out = lax.dynamic_update_index_in_dim(out, part, me ^ k, axis)  15.5 us
    dot_general x1, matrix products, per_device(): inner = jnp.dot(normed_low, w_i, preferred_element_type=F32) + b_in  12.2 us
  transfers between devices with their start and end apart: 54, of which 20 were waited for; matrix products, arithmetic and copies ran while one was open for 25% of the time, Pallas kernels for 4%

profile of v1, /device:TPU:0, one launch (start us, length us, event | category | flops | bytes accessed | tf_op | source)
XLA Modules:
  0.0 528.8 jit_solution(15762974757513626519)
XLA Ops:
  6.6 106.5 %forward.1 = (bf16[4,384,192]{2,1,0:T(8,128)(2,1)S(1)}, bf16[8,256,768]{2,1,0:T(8,128)(2,1)S(1)}, bf16[2048,384]{1,0:T(8,128)(2,1)S(1)}, bf16[2048,384]{1,0:T(8,...) custom-call(bf16[2,256,768]{2,1,0:T(8,128)(2,1)S(1)} %pad_maximum_fu, ...), custom_call_target="tpu_custom_call" | custom-call | tf_op jit(solution)/shard_map/forward/pallas_call | solution.py:751
  120.9 12.2 %fusion.2 = (bf16[384,3072]{1,0:T(8,128)(2,1)S(1)}, f32[384,3072]{1,0:T(8,128)S(1)}) fusion(f32[3072]{0:T(1024)S(1)} %bitcast.343, bf16[768,3072]{1,0:T(8,128)(2,1)S(1)} %bitcast.350, f32[384,768]{1,0:T(8,128)S(1)} %get-tuple-element.134, f32[768]{0:T(1024)S(1)} %copy-done.44, f32[768]{0:T(1024)S(1)} %copy-done.34, f32[384]{0:T(512)S(1)} %add_rsqrt_fusion.1, ...), kind=kOutput, calls=%fused_computation.6 | convolution fusion | flops 1891270656 | bytes 12997632 | tf_op jit(solution)/shard_map/dot_general | solution.py:934
  133.2 2.2 fusion.135
  137.7 3.8 fusion.136
  141.6 2.4 multiply_reduce_fusion
  146.2 2.5 collective-permute-start.33
  148.7 2.3 convolution_convert_fusion.5
  151.8 4.6 collective-permute-start.4
  156.4 6.9 %convolution_convert_fusion = bf16[768,3072]{1,0:T(8,128)(2,1)} fusion(bf16[384,3072]{1,0:T(8,128)(2,1)} %copy-done.45, f32[384,768]{1,0:T(8,128)} %copy-done.28), kind=kOutput, calls=%fused_computation.2 | convolution fusion | flops 1814593536 | bytes 8257536 | tf_op jit(solution)/shard_map/td,tf->df/dot_general | solution.py:958
  163.3 6.4 %convolution_convert_fusion.1 = bf16[768,3072]{1,0:T(8,128)(2,1)} fusion(bf16[384,3072]{1,0:T(8,128)(2,1)} %copy-done.46, f32[384,768]{1,0:T(8,128)S(1)} %copy-done.22, f32[768]{0:T(1024)S(1)} %copy-done.44, f32[768]{0:T(1024)S(1)} %copy-done.34, f32[384]{0:T(512)S(1)} %add_rsqrt_fusion.1, f32[384]{0:T(512)S(1)} %broadcast_multiply_fusion.5), kind=kOutput, calls=%fused_computation.3 | convolution fusion | flops 1815773184 | bytes 8266752 | tf_op jit(solution)/shard_map/td,tf->df/dot_general | solution.py:963
  171.9 5.5 %reshape_reshape.3 = bf16[4,2,2,2,96,192]{4,3,2,1,5,0:T(2,128)(2,1)S(1)} reshape(bf16[4,768,192]{1,2,0:T(8,128)(2,1)} %fusion.23) | data formatting | bytes 2359296 | tf_op jit(solution)/shard_map/reshape;reshape | solution.py:107
  182.9 4.4 constant_dynamic-slice_fusion.9
  188.1 9.8 %reshape.233 = bf16[8,96,4,768]{3,2,1,0:T(4,128)(2,1)} reshape(bf16[768,3072]{1,0:T(8,128)(2,1)} %convolution_convert_fusion) | data formatting | bytes 9437184 | tf_op jit(solution)/shard_map/reshape | solution.py:974
  197.8 3.2 copy.95
  204.8 9.9 %reshape.231 = bf16[8,96,4,768]{3,2,1,0:T(4,128)(2,1)} reshape(bf16[768,3072]{1,0:T(8,128)(2,1)} %convolution_convert_fusion.1) | data formatting | bytes 9437184 | tf_op jit(solution)/shard_map/reshape | solution.py:974
  214.7 3.2 copy.93
  221.9 3.4 collective-permute-start.36
  227.6 3.9 copy.92
  231.5 3.8 copy.107
  235.7 3.9 dynamic_update_slice.75
  244.3 3.9 dynamic_update_slice.76
  248.2 3.9 dynamic_update_slice.77
  252.1 3.9 dynamic_update_slice.78
  262.4 21.4 %attend_back.1 = (bf16[2048,192]{1,0:T(8,128)(2,1)S(1)}, bf16[2048,384]{1,0:T(8,128)(2,1)S(1)}, f32[8,576]{1,0:T(8,128)S(1)}) custom-call(s32[13]{0:T(128)S(1)} %pad_add_fusion.3.info, bf16[2048,384]{1,0:T(8,128)(2,1)S(1)} %copy-done.9, bf16[2048,384]{1,0:T(8,128)(2,1)S(1)} %copy-done.11, bf16[1536,384]{1,0:T(8,128)(2,1)S(1)} %copy.83.d_out, ...), custom_call_target="tpu_custom_call" | custom-call | flops 12079595520 | bytes 14680064 | tf_op jit(solution)/shard_map/attend_back/pallas_call | solution.py:372
  287.6 2.2 convolution_convert_fusion.4
  297.8 4.4 convolution_convert_fusion.2
  311.9 2.5 collective-permute-start.17
  314.4 2.2 collective-permute-start.18
  316.7 3.0 collective-permute-start.1
  321.0 2.8 collective-permute-done.17
  325.4 34.1 %collective-permute-start.46 = (bf16[4,2,2,96,768]{4,3,2,1,0:T(8,128)(2,1)}, bf16[4,2,2,96,768]{4,3,2,1,0:T(8,128)(2,1)S(1)}, u32[]{:S(2)}, u32[]{:S(2)}) collective-permute-start(bf16[4,2,2,96,768]{4,3,2,1,0:T(8,128)(2,1)} %dynamic-slice_bitcast_fusion), channel_id=1, source_target_pairs={{0,4},{4,0},{8,12},{12,8},{1,5},{5,1},{9,13},{13,9},{2,6},{6,2},{1... | collective-permute-start | bytes 7077896 | tf_op jit(solution)/shard_map/ppermute | solution.py:44
  369.0 27.7 %collective-permute-start.28 = (bf16[2,2,96,192]{3,2,0,1:T(8,128)(2,1)S(1)}, bf16[2,2,96,192]{3,2,0,1:T(8,128)(2,1)S(1)}, u32[]{:S(2)}, u32[]{:S(2)}) collective-permute-start(bf16[2,2,96,192]{3,2,0,1:T(8,128)(2,1)S(1)} %dynamic-slice_bitcast_fusion.11), channel_id=1, source_target_pairs={{0,8},{4,12},{8,0},{12,4},{1,9},{5,13},{9,1},{13,5},{2,10},{6,14},... | collective-permute-start | bytes 442376 | tf_op jit(solution)/shard_map/ppermute | solution.py:44
  403.0 4.7 collective-permute-done.26
  409.1 3.2 collective-permute-done.29
  413.8 3.2 collective-permute-done.27
  419.0 2.1 collective-permute-start.31
  421.2 2.5 collective-permute-start.32
  434.3 14.6 %collective-permute-done.7 = bf16[2,256,768]{2,1,0:T(8,128)(2,1)S(1)} collective-permute-done((bf16[2,256,768]{2,1,0:T(8,128)(2,1)S(1)}, bf16[2,256,768]{2,1,0:T(8,128)(2,1)S(1)}, u32[]{:S(2)}, u32[]{:S(2)}) %collective-permute-start.7) | collective-permute-done | bytes 786464 | tf_op jit(solution)/shard_map/ppermute | solution.py:44
  452.3 3.8 collective-permute-done.8
  457.0 4.5 collective-permute-done.49
  462.2 2.0 collective-permute-start.11
  464.3 2.0 collective-permute-start.50
  466.5 4.9 collective-permute-done.41
  474.8 5.8 %collective-permute-done.48 = bf16[2,96,768]{2,1,0:T(8,128)(2,1)S(1)} collective-permute-done((bf16[2,96,768]{2,1,0:T(8,128)(2,1)S(1)}, bf16[2,96,768]{2,1,0:T(8,128)(2,1)S(1)}, u32[]{:S(2)}, u32[]{:S(2)}) %collective-permute-start.48) | collective-permute-done | bytes 294944 | tf_op jit(solution)/shard_map/ppermute | solution.py:44
  482.1 5.3 collective-permute-done.40
  489.7 12.0 %collective-permute-done.10 = bf16[384,768]{1,0:T(8,128)(2,1)S(1)} collective-permute-done((bf16[384,768]{1,0:T(8,128)(2,1)S(1)}, bf16[384,768]{1,0:T(8,128)(2,1)S(1)}, u32[]{:S(2)}, u32[]{:S(2)}) %collective-permute-start.10) | collective-permute-done | bytes 589856 | tf_op jit(solution)/shard_map/ppermute | solution.py:44
  502.0 16.9 %collective-permute-start.44 = (bf16[96,768]{1,0:T(8,128)(2,1)S(1)}, bf16[96,768]{1,0:T(8,128)(2,1)S(1)}, u32[]{:S(2)}, u32[]{:S(2)}) collective-permute-start(bf16[96,768]{1,0:T(8,128)(2,1)S(1)} %get-tuple-element.103), channel_id=1, source_target_pairs={{0,2},{1,3},{2,0},{3,1},{4,6},{5,7},{6,4},{7,5},{8,10},{9,11},{10,... | collective-permute-start | bytes 442376 | tf_op jit(solution)/shard_map/ppermute | solution.py:44
  521.6 6.0 %collective-permute-done.44 = bf16[96,768]{1,0:T(8,128)(2,1)S(1)} collective-permute-done((bf16[96,768]{1,0:T(8,128)(2,1)S(1)}, bf16[96,768]{1,0:T(8,128)(2,1)S(1)}, u32[]{:S(2)}, u32[]{:S(2)}) %collective-permute-start.44) | collective-permute-done | bytes 147488 | tf_op jit(solution)/shard_map/ppermute | solution.py:44
  (368 shorter events, 119.8 us)
Async XLA Ops:
  146.2 54.9 %collective-permute-start.33 = (f32[7680]{0:T(1024)}, f32[7680]{0:T(1024)}, u32[]{:S(2)}, u32[]{:S(2)}) collective-permute-start(f32[7680]{0:T(1024)} %pad_maximum_fusion.5), channel_id=1, source_target_pairs={{0,4},{4,0},{8,12},{12,8},{1,5},{5,1},{9,13},{13,9},{2,6},{6,2},{1... | collective-permute-start | bytes 92168 | tf_op jit(solution)/shard_map/ppermute | solution.py:44
  151.8 89.1 %collective-permute-start.3 = (bf16[384,192]{0,1:T(8,128)(2,1)}, bf16[384,192]{0,1:T(8,128)(2,1)}, u32[]{:S(2)}, u32[]{:S(2)}) collective-permute-start(bf16[384,192]{0,1:T(8,128)(2,1)} %get-tuple-element.107), channel_id=1, source_target_pairs={{0,4},{4,0},{8,12},{12,8},{1,5},{5,1},{9,13},{13,9},{2,6},{6,2},{1... | collective-permute-start | bytes 442376 | tf_op jit(solution)/shard_map/ppermute | solution.py:44
  151.8 90.2 %collective-permute-start.4 = (bf16[384,192]{0,1:T(8,128)(2,1)}, bf16[384,192]{0,1:T(8,128)(2,1)}, u32[]{:S(2)}, u32[]{:S(2)}) collective-permute-start(bf16[384,192]{0,1:T(8,128)(2,1)} %get-tuple-element.106), channel_id=1, source_target_pairs={{0,8},{4,12},{8,0},{12,4},{1,9},{5,13},{9,1},{13,5},{2,10},{6,14},... | collective-permute-start | bytes 442376 | tf_op jit(solution)/shard_map/ppermute | solution.py:44
  156.4 86.8 %collective-permute-start.5 = (bf16[384,192]{0,1:T(8,128)(2,1)S(1)}, bf16[384,192]{0,1:T(8,128)(2,1)}, u32[]{:S(2)}, u32[]{:S(2)}) collective-permute-start(bf16[384,192]{0,1:T(8,128)(2,1)S(1)} %get-tuple-element.105), channel_id=1, source_target_pairs={{0,12},{4,8},{8,4},{12,0},{1,13},{5,9},{9,5},{13,1},{2,14},{6,10},... | collective-permute-start | bytes 442376 | tf_op jit(solution)/shard_map/ppermute | solution.py:44
  201.9 16.1 %collective-permute-start.34 = (f32[7680]{0:T(1024)S(1)}, f32[7680]{0:T(1024)S(1)}, u32[]{:S(2)}, u32[]{:S(2)}) collective-permute-start(f32[7680]{0:T(1024)S(1)} %fusion.115), channel_id=1, source_target_pairs={{0,8},{4,12},{8,0},{12,4},{1,9},{5,13},{9,1},{13,5},{2,10},{6,14},... | collective-permute-start | bytes 92168 | tf_op jit(solution)/shard_map/ppermute | solution.py:44
  221.9 17.8 %collective-permute-start.36 = (f32[7680]{0:T(1024)S(1)}, f32[7680]{0:T(1024)}, u32[]{:S(2)}, u32[]{:S(2)}) collective-permute-start(f32[7680]{0:T(1024)S(1)} %add.630), channel_id=1, source_target_pairs={{0,1},{1,0},{2,3},{3,2},{4,5},{5,4},{6,7},{7,6},{8,9},{9,8},{10,11... | collective-permute-start | bytes 92168 | tf_op jit(solution)/shard_map/ppermute | solution.py:44
  240.5 64.7 %collective-permute-start.37 = (f32[7680]{0:T(1024)S(1)}, f32[7680]{0:T(1024)S(1)}, u32[]{:S(2)}, u32[]{:S(2)}) collective-permute-start(f32[7680]{0:T(1024)S(1)} %add.631), channel_id=1, source_target_pairs={{0,2},{1,3},{2,0},{3,1},{4,6},{5,7},{6,4},{7,5},{8,10},{9,11},{10,... | collective-permute-start | bytes 92168 | tf_op jit(solution)/shard_map/ppermute | solution.py:44
  285.1 5.3 collective-permute-start.20
  290.7 5.7 %collective-permute-start.21 = (f32[4,384]{1,0:T(4,128)S(1)}, f32[4,384]{1,0:T(4,128)S(1)}, u32[]{:S(2)}, u32[]{:S(2)}) collective-permute-start(f32[4,384]{1,0:T(4,128)S(1)} %add.609), channel_id=1, source_target_pairs={{0,8},{4,12},{8,0},{12,4},{1,9},{5,13},{9,1},{13,5},{2,10},{6,14},... | collective-permute-start | bytes 18440 | tf_op jit(solution)/shard_map/ppermute | solution.py:44
  292.0 19.9 %collective-permute-start.12 = (bf16[96,576]{1,0:T(8,128)(2,1)S(1)}, bf16[96,576]{1,0:T(8,128)(2,1)S(1)}, u32[]{:S(2)}, u32[]{:S(2)}) collective-permute-start(bf16[96,576]{1,0:T(8,128)(2,1)S(1)} %get-tuple-element.88), channel_id=1, source_target_pairs={{0,1},{1,0},{2,3},{3,2},{16,17},{17,16},{18,19},{19,18},{4,5},{5,4... | collective-permute-start | bytes 331784 | tf_op jit(solution)/shard_map/ppermute | solution.py:138
  293.6 20.7 %collective-permute-start.13 = (bf16[96,576]{1,0:T(8,128)(2,1)S(1)}, bf16[96,576]{1,0:T(8,128)(2,1)S(1)}, u32[]{:S(2)}, u32[]{:S(2)}) collective-permute-start(bf16[96,576]{1,0:T(8,128)(2,1)S(1)} %get-tuple-element.94), channel_id=1, source_target_pairs={{0,2},{1,3},{2,0},{3,1},{16,18},{17,19},{18,16},{19,17},{4,6},{5,7... | collective-permute-start | bytes 331784 | tf_op jit(solution)/shard_map/ppermute | solution.py:138
  295.0 21.6 %collective-permute-start.14 = (bf16[96,576]{1,0:T(8,128)(2,1)S(1)}, bf16[96,576]{1,0:T(8,128)(2,1)S(1)}, u32[]{:S(2)}, u32[]{:S(2)}) collective-permute-start(bf16[96,576]{1,0:T(8,128)(2,1)S(1)} %get-tuple-element.93), channel_id=1, source_target_pairs={{0,3},{1,2},{2,1},{3,0},{16,19},{17,18},{18,17},{19,16},{4,7},{5,6... | collective-permute-start | bytes 331784 | tf_op jit(solution)/shard_map/ppermute | solution.py:138
  296.5 5.8 %collective-permute-start.22 = (f32[4,384]{1,0:T(4,128)S(1)}, f32[4,384]{1,0:T(4,128)S(1)}, u32[]{:S(2)}, u32[]{:S(2)}) collective-permute-start(f32[4,384]{1,0:T(4,128)S(1)} %add.610), channel_id=1, source_target_pairs={{0,16},{16,0},{1,17},{17,1},{2,18},{18,2},{3,19},{19,3},{4,20},{20... | collective-permute-start | bytes 18440 | tf_op jit(solution)/shard_map/ppermute | solution.py:44
  305.2 11.5 %collective-permute-start.15 = (bf16[96,576]{1,0:T(8,128)(2,1)S(1)}, bf16[96,576]{1,0:T(8,128)(2,1)S(1)}, u32[]{:S(2)}, u32[]{:S(2)}) collective-permute-start(bf16[96,576]{1,0:T(8,128)(2,1)S(1)} %get-tuple-element.92), channel_id=1, source_target_pairs={{0,16},{1,17},{2,18},{3,19},{16,0},{17,1},{18,2},{19,3},{4,20},{5,... | collective-permute-start | bytes 331784 | tf_op jit(solution)/shard_map/ppermute | solution.py:138
  310.5 9.1 %collective-permute-start.16 = (bf16[96,576]{1,0:T(8,128)(2,1)S(1)}, bf16[96,576]{1,0:T(8,128)(2,1)S(1)}, u32[]{:S(2)}, u32[]{:S(2)}) collective-permute-start(bf16[96,576]{1,0:T(8,128)(2,1)S(1)} %get-tuple-element.91), channel_id=1, source_target_pairs={{0,17},{1,16},{2,19},{3,18},{16,1},{17,0},{18,3},{19,2},{4,21},{5,... | collective-permute-start | bytes 331784 | tf_op jit(solution)/shard_map/ppermute | solution.py:138
  311.9 11.9 %collective-permute-start.17 = (bf16[96,576]{1,0:T(8,128)(2,1)S(1)}, bf16[96,576]{1,0:T(8,128)(2,1)S(1)}, u32[]{:S(2)}, u32[]{:S(2)}) collective-permute-start(bf16[96,576]{1,0:T(8,128)(2,1)S(1)} %get-tuple-element.90), channel_id=1, source_target_pairs={{0,18},{1,19},{2,16},{3,17},{16,2},{17,3},{18,0},{19,1},{4,22},{5,... | collective-permute-start | bytes 331784 | tf_op jit(solution)/shard_map/ppermute | solution.py:138
  314.4 9.6 %collective-permute-start.18 = (bf16[96,576]{1,0:T(8,128)(2,1)S(1)}, bf16[96,576]{1,0:T(8,128)(2,1)S(1)}, u32[]{:S(2)}, u32[]{:S(2)}) collective-permute-start(bf16[96,576]{1,0:T(8,128)(2,1)S(1)} %get-tuple-element.89), channel_id=1, source_target_pairs={{0,19},{1,18},{2,17},{3,16},{16,3},{17,2},{18,1},{19,0},{4,23},{5,... | collective-permute-start | bytes 331784 | tf_op jit(solution)/shard_map/ppermute | solution.py:138
  316.6 48.7 %collective-permute-start = (bf16[384,768]{1,0:T(8,128)(2,1)}, bf16[384,768]{1,0:T(8,128)(2,1)}, u32[]{:S(2)}, u32[]{:S(2)}) collective-permute-start(bf16[384,768]{1,0:T(8,128)(2,1)} %get-tuple-element.83), channel_id=1, source_target_pairs={{0,1},{1,0},{2,3},{3,2},{4,5},{5,4},{6,7},{7,6},{8,9},{9,8},{10,11... | collective-permute-start | bytes 1769480 | tf_op jit(solution)/shard_map/ppermute | solution.py:44
  316.7 52.4 %collective-permute-start.1 = (bf16[384,768]{1,0:T(8,128)(2,1)}, bf16[384,768]{1,0:T(8,128)(2,1)}, u32[]{:S(2)}, u32[]{:S(2)}) collective-permute-start(bf16[384,768]{1,0:T(8,128)(2,1)} %get-tuple-element.83), channel_id=1, source_target_pairs={{0,2},{1,3},{2,0},{3,1},{4,6},{5,7},{6,4},{7,5},{8,10},{9,11},{10,... | collective-permute-start | bytes 1769480 | tf_op jit(solution)/shard_map/ppermute | solution.py:44
  319.6 97.5 %collective-permute-start.2 = (bf16[384,768]{1,0:T(8,128)(2,1)}, bf16[384,768]{1,0:T(8,128)(2,1)}, u32[]{:S(2)}, u32[]{:S(2)}) collective-permute-start(bf16[384,768]{1,0:T(8,128)(2,1)} %get-tuple-element.83), channel_id=1, source_target_pairs={{0,3},{1,2},{2,1},{3,0},{4,7},{5,6},{6,5},{7,4},{8,11},{9,10},{10,... | collective-permute-start | bytes 1769480 | tf_op jit(solution)/shard_map/ppermute | solution.py:44
  323.8 39.3 %collective-permute-start.25 = (bf16[4,2,2,96,192]{4,3,0,1,2:T(8,128)(2,1)}, bf16[4,2,2,96,192]{4,3,0,1,2:T(8,128)(2,1)}, u32[]{:S(2)}, u32[]{:S(2)}) collective-permute-start(bf16[4,2,2,96,192]{4,3,0,1,2:T(8,128)(2,1)} %bitcast.74), channel_id=1, source_target_pairs={{0,4},{4,0},{8,12},{12,8},{1,5},{5,1},{9,13},{13,9},{2,6},{6,2},{1... | collective-permute-start | bytes 1769480 | tf_op jit(solution)/shard_map/ppermute | solution.py:44
  325.4 104.4 %collective-permute-start.46 = (bf16[4,2,2,96,768]{4,3,2,1,0:T(8,128)(2,1)}, bf16[4,2,2,96,768]{4,3,2,1,0:T(8,128)(2,1)S(1)}, u32[]{:S(2)}, u32[]{:S(2)}) collective-permute-start(bf16[4,2,2,96,768]{4,3,2,1,0:T(8,128)(2,1)} %dynamic-slice_bitcast_fusion), channel_id=1, source_target_pairs={{0,4},{4,0},{8,12},{12,8},{1,5},{5,1},{9,13},{13,9},{2,6},{6,2},{1... | collective-permute-start | bytes 7077896 | tf_op jit(solution)/shard_map/ppermute | solution.py:44
  363.1 70.3 %collective-permute-start.38 = (bf16[4,2,2,96,768]{4,3,2,1,0:T(8,128)(2,1)}, bf16[4,2,2,96,768]{4,3,2,1,0:T(8,128)(2,1)S(1)}, u32[]{:S(2)}, u32[]{:S(2)}) collective-permute-start(bf16[4,2,2,96,768]{4,3,2,1,0:T(8,128)(2,1)} %dynamic-slice_bitcast_fusion.1), channel_id=1, source_target_pairs={{0,4},{4,0},{8,12},{12,8},{1,5},{5,1},{9,13},{13,9},{2,6},{6,2},{1... | collective-permute-start | bytes 7077896 | tf_op jit(solution)/shard_map/ppermute | solution.py:44
  365.3 62.5 %collective-permute-start.6 = (bf16[2,2,256,768]{3,2,1,0:T(8,128)(2,1)S(1)}, bf16[2,2,256,768]{3,2,1,0:T(8,128)(2,1)S(1)}, u32[]{:S(2)}, u32[]{:S(2)}) collective-permute-start(bf16[2,2,256,768]{3,2,1,0:T(8,128)(2,1)S(1)} %copy-done.27), channel_id=1, source_target_pairs={{0,4},{4,0},{8,12},{12,8},{1,5},{5,1},{9,13},{13,9},{2,6},{6,2},{1... | collective-permute-start | bytes 4718600 | tf_op jit(solution)/shard_map/ppermute | solution.py:44
  369.0 32.6 %collective-permute-start.28 = (bf16[2,2,96,192]{3,2,0,1:T(8,128)(2,1)S(1)}, bf16[2,2,96,192]{3,2,0,1:T(8,128)(2,1)S(1)}, u32[]{:S(2)}, u32[]{:S(2)}) collective-permute-start(bf16[2,2,96,192]{3,2,0,1:T(8,128)(2,1)S(1)} %dynamic-slice_bitcast_fusion.11), channel_id=1, source_target_pairs={{0,8},{4,12},{8,0},{12,4},{1,9},{5,13},{9,1},{13,5},{2,10},{6,14},... | collective-permute-start | bytes 442376 | tf_op jit(solution)/shard_map/ppermute | solution.py:44
  401.6 6.1 %collective-permute-start.26 = (bf16[2,2,96,192]{3,2,0,1:T(8,128)(2,1)S(1)}, bf16[2,2,96,192]{3,2,0,1:T(8,128)(2,1)S(1)}, u32[]{:S(2)}, u32[]{:S(2)}) collective-permute-start(bf16[2,2,96,192]{3,2,0,1:T(8,128)(2,1)S(1)} %dynamic-slice_bitcast_fusion.12), channel_id=1, source_target_pairs={{0,16},{16,0},{1,17},{17,1},{2,18},{18,2},{3,19},{19,3},{4,20},{20... | collective-permute-start | bytes 442376 | tf_op jit(solution)/shard_map/ppermute | solution.py:44
  407.7 4.6 collective-permute-start.29
  419.0 6.3 %collective-permute-start.31 = (bf16[96,192]{1,0:T(8,128)(2,1)S(1)}, bf16[96,192]{1,0:T(8,128)(2,1)S(1)}, u32[]{:S(2)}, u32[]{:S(2)}) collective-permute-start(bf16[96,192]{1,0:T(8,128)(2,1)S(1)} %get-tuple-element.110), channel_id=1, source_target_pairs={{0,2},{1,3},{2,0},{3,1},{4,6},{5,7},{6,4},{7,5},{8,10},{9,11},{10,... | collective-permute-start | bytes 110600 | tf_op jit(solution)/shard_map/ppermute | solution.py:44
  421.2 5.9 %collective-permute-start.32 = (bf16[96,192]{1,0:T(8,128)(2,1)S(1)}, bf16[96,192]{1,0:T(8,128)(2,1)S(1)}, u32[]{:S(2)}, u32[]{:S(2)}) collective-permute-start(bf16[96,192]{1,0:T(8,128)(2,1)S(1)} %get-tuple-element.111), channel_id=1, source_target_pairs={{0,3},{1,2},{2,1},{3,0},{4,7},{5,6},{6,5},{7,4},{8,11},{9,10},{10,... | collective-permute-start | bytes 110600 | tf_op jit(solution)/shard_map/ppermute | solution.py:44
  428.3 20.5 %collective-permute-start.7 = (bf16[2,256,768]{2,1,0:T(8,128)(2,1)S(1)}, bf16[2,256,768]{2,1,0:T(8,128)(2,1)S(1)}, u32[]{:S(2)}, u32[]{:S(2)}) collective-permute-start(bf16[2,256,768]{2,1,0:T(8,128)(2,1)S(1)} %dynamic-slice_bitcast_fusion.3), channel_id=1, source_target_pairs={{0,8},{4,12},{8,0},{12,4},{1,9},{5,13},{9,1},{13,5},{2,10},{6,14},... | collective-permute-start | bytes 2359304 | tf_op jit(solution)/shard_map/ppermute | solution.py:44
  430.8 30.7 %collective-permute-start.49 = (bf16[2,2,96,768]{3,2,1,0:T(8,128)(2,1)S(1)}, bf16[2,2,96,768]{3,2,1,0:T(8,128)(2,1)S(1)}, u32[]{:S(2)}, u32[]{:S(2)}) collective-permute-start(bf16[2,2,96,768]{3,2,1,0:T(8,128)(2,1)S(1)} %dynamic-slice_bitcast_fusion.4), channel_id=1, source_target_pairs={{0,8},{4,12},{8,0},{12,4},{1,9},{5,13},{9,1},{13,5},{2,10},{6,14},... | collective-permute-start | bytes 1769480 | tf_op jit(solution)/shard_map/ppermute | solution.py:44
  431.6 30.5 %collective-permute-start.47 = (bf16[2,2,96,768]{3,2,0,1:T(8,128)(2,1)S(1)}, bf16[2,2,96,768]{3,2,0,1:T(8,128)(2,1)S(1)}, u32[]{:S(2)}, u32[]{:S(2)}) collective-permute-start(bf16[2,2,96,768]{3,2,0,1:T(8,128)(2,1)S(1)} %bitcast.334), channel_id=1, source_target_pairs={{0,16},{16,0},{1,17},{17,1},{2,18},{18,2},{3,19},{19,3},{4,20},{20... | collective-permute-start | bytes 1769480 | tf_op jit(solution)/shard_map/ppermute | solution.py:44
  449.2 7.0 %collective-permute-start.8 = (bf16[128,768]{1,0:T(8,128)(2,1)S(1)}, bf16[128,768]{1,0:T(8,128)(2,1)S(1)}, u32[]{:S(2)}, u32[]{:S(2)}) collective-permute-start(bf16[128,768]{1,0:T(8,128)(2,1)S(1)} %dynamic-slice_bitcast_fusion.13), channel_id=1, source_target_pairs={{0,1},{1,0},{2,3},{3,2},{4,5},{5,4},{6,7},{7,6},{8,9},{9,8},{10,11... | collective-permute-start | bytes 589832 | tf_op jit(solution)/shard_map/ppermute | solution.py:44
  449.3 22.1 %collective-permute-start.41 = (bf16[2,2,96,768]{3,2,1,0:T(8,128)(2,1)S(1)}, bf16[2,2,96,768]{3,2,1,0:T(8,128)(2,1)S(1)}, u32[]{:S(2)}, u32[]{:S(2)}) collective-permute-start(bf16[2,2,96,768]{3,2,1,0:T(8,128)(2,1)S(1)} %dynamic-slice_bitcast_fusion.5), channel_id=1, source_target_pairs={{0,8},{4,12},{8,0},{12,4},{1,9},{5,13},{9,1},{13,5},{2,10},{6,14},... | collective-permute-start | bytes 1769480 | tf_op jit(solution)/shard_map/ppermute | solution.py:44
  450.9 13.4 %collective-permute-start.39 = (bf16[2,2,96,768]{3,2,0,1:T(8,128)(2,1)S(1)}, bf16[2,2,96,768]{3,2,0,1:T(8,128)(2,1)S(1)}, u32[]{:S(2)}, u32[]{:S(2)}) collective-permute-start(bf16[2,2,96,768]{3,2,0,1:T(8,128)(2,1)S(1)} %bitcast.335), channel_id=1, source_target_pairs={{0,16},{16,0},{1,17},{17,1},{2,18},{18,2},{3,19},{19,3},{4,20},{20... | collective-permute-start | bytes 1769480 | tf_op jit(solution)/shard_map/ppermute | solution.py:44
  456.4 32.2 %collective-permute-start.9 = (bf16[384,768]{1,0:T(8,128)(2,1)S(1)}, bf16[384,768]{1,0:T(8,128)(2,1)S(1)}, u32[]{:S(2)}, u32[]{:S(2)}) collective-permute-start(bf16[384,768]{1,0:T(8,128)(2,1)S(1)} %get-tuple-element.74), channel_id=1, source_target_pairs={{0,1},{1,0},{2,3},{3,2},{4,5},{5,4},{6,7},{7,6},{8,9},{9,8},{10,11... | collective-permute-start | bytes 1769480 | tf_op jit(solution)/shard_map/ppermute | solution.py:44
  461.5 40.2 %collective-permute-start.10 = (bf16[384,768]{1,0:T(8,128)(2,1)S(1)}, bf16[384,768]{1,0:T(8,128)(2,1)S(1)}, u32[]{:S(2)}, u32[]{:S(2)}) collective-permute-start(bf16[384,768]{1,0:T(8,128)(2,1)S(1)} %get-tuple-element.74), channel_id=1, source_target_pairs={{0,2},{1,3},{2,0},{3,1},{4,6},{5,7},{6,4},{7,5},{8,10},{9,11},{10,... | collective-permute-start | bytes 1769480 | tf_op jit(solution)/shard_map/ppermute | solution.py:44
  462.2 39.8 %collective-permute-start.11 = (bf16[384,768]{1,0:T(8,128)(2,1)S(1)}, bf16[384,768]{1,0:T(8,128)(2,1)S(1)}, u32[]{:S(2)}, u32[]{:S(2)}) collective-permute-start(bf16[384,768]{1,0:T(8,128)(2,1)S(1)} %get-tuple-element.74), channel_id=1, source_target_pairs={{0,3},{1,2},{2,1},{3,0},{4,7},{5,6},{6,5},{7,4},{8,11},{9,10},{10,... | collective-permute-start | bytes 1769480 | tf_op jit(solution)/shard_map/ppermute | solution.py:44
  464.3 8.6 %collective-permute-start.50 = (bf16[2,96,768]{2,1,0:T(8,128)(2,1)S(1)}, bf16[2,96,768]{2,1,0:T(8,128)(2,1)S(1)}, u32[]{:S(2)}, u32[]{:S(2)}) collective-permute-start(bf16[2,96,768]{2,1,0:T(8,128)(2,1)S(1)} %dynamic-slice_bitcast_fusion.7), channel_id=1, source_target_pairs={{0,16},{16,0},{1,17},{17,1},{2,18},{18,2},{3,19},{19,3},{4,20},{20... | collective-permute-start | bytes 884744 | tf_op jit(solution)/shard_map/ppermute | solution.py:44
  471.4 9.2 %collective-permute-start.48 = (bf16[2,96,768]{2,1,0:T(8,128)(2,1)S(1)}, bf16[2,96,768]{2,1,0:T(8,128)(2,1)S(1)}, u32[]{:S(2)}, u32[]{:S(2)}) collective-permute-start(bf16[2,96,768]{2,1,0:T(8,128)(2,1)S(1)} %dynamic-slice_bitcast_fusion.8), channel_id=1, source_target_pairs={{0,8},{4,12},{8,0},{12,4},{1,9},{5,13},{9,1},{13,5},{2,10},{6,14},... | collective-permute-start | bytes 884744 | tf_op jit(solution)/shard_map/ppermute | solution.py:44
  473.0 8.9 %collective-permute-start.42 = (bf16[2,96,768]{2,1,0:T(8,128)(2,1)S(1)}, bf16[2,96,768]{2,1,0:T(8,128)(2,1)S(1)}, u32[]{:S(2)}, u32[]{:S(2)}) collective-permute-start(bf16[2,96,768]{2,1,0:T(8,128)(2,1)S(1)} %dynamic-slice_bitcast_fusion.9), channel_id=1, source_target_pairs={{0,16},{16,0},{1,17},{17,1},{2,18},{18,2},{3,19},{19,3},{4,20},{20... | collective-permute-start | bytes 884744 | tf_op jit(solution)/shard_map/ppermute | solution.py:44
  480.6 6.7 %collective-permute-start.40 = (bf16[2,96,768]{2,1,0:T(8,128)(2,1)S(1)}, bf16[2,96,768]{2,1,0:T(8,128)(2,1)S(1)}, u32[]{:S(2)}, u32[]{:S(2)}) collective-permute-start(bf16[2,96,768]{2,1,0:T(8,128)(2,1)S(1)} %dynamic-slice_bitcast_fusion.10), channel_id=1, source_target_pairs={{0,8},{4,12},{8,0},{12,4},{1,9},{5,13},{9,1},{13,5},{2,10},{6,14},... | collective-permute-start | bytes 884744 | tf_op jit(solution)/shard_map/ppermute | solution.py:44
  481.9 37.2 %collective-permute-start.51 = (bf16[96,768]{1,0:T(8,128)(2,1)S(1)}, bf16[96,768]{1,0:T(8,128)(2,1)S(1)}, u32[]{:S(2)}, u32[]{:S(2)}) collective-permute-start(bf16[96,768]{1,0:T(8,128)(2,1)S(1)} %get-tuple-element.99), channel_id=1, source_target_pairs={{0,1},{1,0},{2,3},{3,2},{4,5},{5,4},{6,7},{7,6},{8,9},{9,8},{10,11... | collective-permute-start | bytes 442376 | tf_op jit(solution)/shard_map/ppermute | solution.py:44
  487.4 33.4 %collective-permute-start.52 = (bf16[96,768]{1,0:T(8,128)(2,1)S(1)}, bf16[96,768]{1,0:T(8,128)(2,1)S(1)}, u32[]{:S(2)}, u32[]{:S(2)}) collective-permute-start(bf16[96,768]{1,0:T(8,128)(2,1)S(1)} %get-tuple-element.100), channel_id=1, source_target_pairs={{0,2},{1,3},{2,0},{3,1},{4,6},{5,7},{6,4},{7,5},{8,10},{9,11},{10,... | collective-permute-start | bytes 442376 | tf_op jit(solution)/shard_map/ppermute | solution.py:44
  488.7 32.1 %collective-permute-start.53 = (bf16[96,768]{1,0:T(8,128)(2,1)S(1)}, bf16[96,768]{1,0:T(8,128)(2,1)S(1)}, u32[]{:S(2)}, u32[]{:S(2)}) collective-permute-start(bf16[96,768]{1,0:T(8,128)(2,1)S(1)} %get-tuple-element.101), channel_id=1, source_target_pairs={{0,3},{1,2},{2,1},{3,0},{4,7},{5,6},{6,5},{7,4},{8,11},{9,10},{10,... | collective-permute-start | bytes 442376 | tf_op jit(solution)/shard_map/ppermute | solution.py:44
  501.8 19.8 %collective-permute-start.43 = (bf16[96,768]{1,0:T(8,128)(2,1)S(1)}, bf16[96,768]{1,0:T(8,128)(2,1)S(1)}, u32[]{:S(2)}, u32[]{:S(2)}) collective-permute-start(bf16[96,768]{1,0:T(8,128)(2,1)S(1)} %get-tuple-element.102), channel_id=1, source_target_pairs={{0,1},{1,0},{2,3},{3,2},{4,5},{5,4},{6,7},{7,6},{8,9},{9,8},{10,11... | collective-permute-start | bytes 442376 | tf_op jit(solution)/shard_map/ppermute | solution.py:44
  502.0 25.6 %collective-permute-start.44 = (bf16[96,768]{1,0:T(8,128)(2,1)S(1)}, bf16[96,768]{1,0:T(8,128)(2,1)S(1)}, u32[]{:S(2)}, u32[]{:S(2)}) collective-permute-start(bf16[96,768]{1,0:T(8,128)(2,1)S(1)} %get-tuple-element.103), channel_id=1, source_target_pairs={{0,2},{1,3},{2,0},{3,1},{4,6},{5,7},{6,4},{7,5},{8,10},{9,11},{10,... | collective-permute-start | bytes 442376 | tf_op jit(solution)/shard_map/ppermute | solution.py:44
  519.1 8.5 %collective-permute-start.45 = (bf16[96,768]{1,0:T(8,128)(2,1)S(1)}, bf16[96,768]{1,0:T(8,128)(2,1)S(1)}, u32[]{:S(2)}, u32[]{:S(2)}) collective-permute-start(bf16[96,768]{1,0:T(8,128)(2,1)S(1)} %get-tuple-element.104), channel_id=1, source_target_pairs={{0,3},{1,2},{2,1},{3,0},{4,7},{5,6},{6,5},{7,4},{8,11},{9,10},{10,... | collective-permute-start | bytes 442376 | tf_op jit(solution)/shard_map/ppermute | solution.py:44
  (59 other events, 665.1 us)

commit v2 on v1

--- a/solution.py
+++ b/solution.py
@@ -67,61 +67,12 @@
     return parts
 
 
-def gather_weight(shard, sizes, me):
-    nd, nc, nt = sizes
-    d, c, z = me
-    zset = gather_axis(shard, "tp", nt, z)
-    if nd != 2:
-        full = lax.all_gather(zset, ("dp", "ctx"), axis=1, tiled=False)
-        return full
-    half = nt // 2
-    px = swap_with(zset, "dp", nd, 1)
-    py = swap_with(zset, "ctx", nc, 2)
-    pd = jnp.concatenate(
-        [swap_with(px[:half], "ctx", nc, 2), swap_with(py[half:], "dp", nd, 1)], 0
-    )
-    own = [zset, px, py, pd]
-    other = [swap_with(v, "ctx", nc, 1) for v in own]
-    row = d * nc + c
-    out = jnp.zeros((nt, nd * nc) + shard.shape, shard.dtype)
-    for core, group in ((0, own), (1, other)):
-        for k, part in enumerate(group):
-            at = row ^ (core + (nc if k in (1, 3) else 0) + (2 if k in (2, 3) else 0))
-            out = lax.dynamic_update_index_in_dim(out, part, at, 1)
-    return out
-
-
-def add_low(a, b):
-    return (a.astype(F32) + b.astype(F32)).astype(BF)
-
-
 def scatter_weight(grad, sizes, me):
     nd, nc, nt = sizes
-    d, c, z = me
-    if nd != 2:
-        part = lax.psum_scatter(
-            grad.astype(F32), ("dp", "ctx"), scatter_dimension=1, tiled=False
-        ).astype(BF)
-    else:
-        rows, cols = grad.shape[2:]
-        view = grad.reshape(nt, nd, nc // 2, 2, rows, cols)
-        core = c % 2
-        y = c // 2
-        keep = lax.dynamic_index_in_dim(view, core, 3, keepdims=False)
-        send = lax.dynamic_index_in_dim(view, 1 - core, 3, keepdims=False)
-        a = add_low(keep, swap_with(send, "ctx", nc, 1))
-        half = nt // 2
-        one, two = a[:half], a[half:]
-        r1 = swap_with(lax.dynamic_index_in_dim(one, 1 - d, 1, keepdims=False), "dp", nd, 1)
-        r2 = swap_with(lax.dynamic_index_in_dim(two, 1 - y, 2, keepdims=False), "ctx", nc, 2)
-        one = add_low(lax.dynamic_index_in_dim(one, d, 1, keepdims=False), r1)
-        two = add_low(lax.dynamic_index_in_dim(two, y, 2, keepdims=False), r2)
-        r1 = swap_with(lax.dynamic_index_in_dim(one, 1 - y, 1, keepdims=False), "ctx", nc, 2)
-        r2 = swap_with(lax.dynamic_index_in_dim(two, 1 - d, 1, keepdims=False), "dp", nd, 1)
-        one = add_low(lax.dynamic_index_in_dim(one, y, 1, keepdims=False), r1)
-        two = add_low(lax.dynamic_index_in_dim(two, d, 1, keepdims=False), r2)
-        part = jnp.concatenate([one, two], 0)
-    parts = exchange_axis(part, "tp", nt, z)
+    part = lax.psum_scatter(
+        grad.astype(F32), ("dp", "ctx"), scatter_dimension=1, tiled=False
+    ).astype(BF)
+    parts = exchange_axis(part, "tp", nt, me[2])
     return sum(p.astype(F32) for p in parts)
 
 
@@ -130,62 +81,18 @@
     return lax.ppermute(value, ("ctx", "tp"), pairs)
 
 
-def pair_perm(value, sizes, kd, kt):
-    nd, _, nt = sizes
-    pairs = [
-        (a * nt + b, (a ^ kd) * nt + (b ^ kt)) for a in range(nd) for b in range(nt)
-    ]
-    return lax.ppermute(value, ("dp", "tp"), pairs)
-
-
 def gather_heads(shard, sizes, me):
-    nd, nc, nt = sizes
-    d, c, z = me
-    mine = transpose_ctx_tp(shard, nc)
-    if nd != 2:
-        return lax.all_gather(mine, ("dp", "tp"), axis=0, tiled=True)
-    out = jnp.zeros((nd * nt,) + shard.shape, shard.dtype)
-    for kd in range(nd):
-        for kt in range(nt):
-            part = pair_perm(mine, sizes, kd, kt) if kd or kt else mine
-            out = lax.dynamic_update_index_in_dim(out, part, (d ^ kd) * nt + (z ^ kt), 0)
-    return out.reshape((nd * nt * shard.shape[0],) + shard.shape[1:])
+    mine = transpose_ctx_tp(shard, sizes[1])
+    return lax.all_gather(mine, ("dp", "tp"), axis=0, tiled=True)
 
 
 def scatter_heads(grad, sizes, me):
     nd, nc, nt = sizes
-    d, c, z = me
     blocks = grad.reshape((nd * nt, grad.shape[0] // (nd * nt)) + grad.shape[1:])
-    if nd != 2:
-        total = lax.psum_scatter(
-            blocks.astype(F32), ("dp", "tp"), scatter_dimension=0, tiled=False
-        )
-    else:
-        total = 0.0
-        for kd in range(nd):
-            for kt in range(nt):
-                block = lax.dynamic_index_in_dim(
-                    blocks, (d ^ kd) * nt + (z ^ kt), 0, keepdims=False
-                )
-                if kd or kt:
-                    block = pair_perm(block, sizes, kd, kt)
-                total = total + block.astype(F32)
+    total = lax.psum_scatter(
+        blocks.astype(F32), ("dp", "tp"), scatter_dimension=0, tiled=False
+    )
     return transpose_ctx_tp(total, nc)
-
-
-def sum_all(value, sizes):
-    nd, nc, nt = sizes
-    if nd != 2:
-        return lax.psum(value, ALL)
-    for axis, size, mask in (
-        ("ctx", nc, 1),
-        ("ctx", nc, 2),
-        ("dp", nd, 1),
-        ("tp", nt, 1),
-        ("tp", nt, 2),
-    ):
-        value = value + swap_with(value, axis, size, mask)
-    return value
 
 
 def block_rows(qb, half, ln):
@@ -410,18 +317,29 @@
             device_id_type=MESH,
         )
 
-    def start(self, i, src, dst, device):
-        copy = self.make(i, src, dst, device)
-        copy.start()
-        self.open.append(copy)
+    def start(self, i, parts, when=None):
+        if when is None:
+            self.make(i, *parts()).start()
+        else:
+
+            @pl.when(when())
+            def _():
+                self.make(i, *parts()).start()
+
+        self.open.append((i, parts, when))
 
     def arrived(self, i, dst, device):
         self.make(i, dst, dst, device).wait_recv()
 
     def sent(self):
-        for copy in self.open:
-            copy.wait_send()
-        self.open = []
+        for i, parts, when in self.open:
+            if when is None:
+                self.make(i, *parts()).wait_send()
+            else:
+
+                @pl.when(when())
+                def _():
+                    self.make(i, *parts()).wait_send()
 
 
 def forward_kernel(
@@ -436,7 +354,7 @@
     w_i,
     w_b,
     ctx_all,
-    x_out,
+    xt_out,
     q_out,
     kv_out,
     wh_out,
@@ -448,6 +366,7 @@
     ctx_t,
     seg,
     x2,
+    xt,
     wh,
     bh,
     q_scr,
@@ -499,7 +418,7 @@
 
     n_ty, n_tc, n_tf = next(number), next(number), next(number)
     tok_at = lambda i: x2.at[pl.ds(2 * i, 2)]
-    rc.start(n_ty, tok2, tok_at(c), at_c(2))
+    rc.start(n_ty, lambda: (tok2, tok_at(c), at_c(2)))
     n_wa, n_ba = next(number), next(number)
     wh_at = lambda r: wh.at[pl.ds(pl.multiple_of(r * wr, wr), wr)]
 
@@ -525,10 +444,10 @@
         for copy in here:
             copy.start()
 
-    rc.start(n_tc, tok2, tok_at(c), at_c(1))
+    rc.start(n_tc, lambda: (tok2, tok_at(c), at_c(1)))
     n_seg = [next(number) for _ in range(3)]
     for k in (1, 2, 3):
-        rc.start(n_seg[k - 1], seg2, seg.at[c], at_c(k))
+        rc.start(n_seg[k - 1], lambda k=k: (seg2, seg.at[c], at_c(k)))
     seg_here = copy_here(seg2, seg.at[c])
     bu_here = copy_here(b_unit, bu_full.at[z])
     i_at = lambda r, t: i_full.at[r, :, pl.ds(pl.multiple_of(t * units, 128), units)]
@@ -554,19 +473,19 @@
 
     n_wx = [next(number) for _ in pairs]
     for i, p in zip(n_wx, pairs):
-        rc.start(i, wh_at(row_w), wh_at(row_w), at_xz(*p))
+        rc.start(i, lambda p=p: (wh_at(row_w), wh_at(row_w), at_xz(*p)))
 
     n_bu = [next(number) for _ in range(3)]
     n_z = [[next(number) for _ in range(3)] for _ in range(3)]
     full_at = (o_at, i_at, b_at)
     for k in (1, 2, 3):
-        rc.start(n_bu[k - 1], b_unit, bu_full.at[z], at_xz(0, k))
+        rc.start(n_bu[k - 1], lambda k=k: (b_unit, bu_full.at[z], at_xz(0, k)))
     for w, src in enumerate((w_o, w_i, w_b)):
         for k in (1, 2, 3):
-            rc.start(n_z[w][k - 1], src, full_at[w](row, z), at_xz(0, k))
+            rc.start(n_z[w][k - 1], lambda k=k, w=w, src=src: (src, full_at[w](row, z), at_xz(0, k)))
 
     rc.arrived(n_ty, tok_at(c ^ 2), at_c(2))
-    rc.start(n_tf, tok_at(c ^ 2), tok_at(c ^ 2), at_c(1))
+    rc.start(n_tf, lambda: (tok_at(c ^ 2), tok_at(c ^ 2), at_c(1)))
     for k in (1, 2, 3):
         rc.arrived(n_seg[k - 1], seg.at[c ^ k], at_c(k))
     seg_here.wait()
@@ -581,7 +500,6 @@
     mine.wait()
     rc.arrived(n_tc, tok_at(c ^ 1), at_c(1))
     rc.arrived(n_tf, tok_at(c ^ 3), at_c(1))
-    x_here = copy_here(x2, x_out)
     wh_here = copy_here(wh, wh_out)
     wide = heads * 128
 
@@ -589,12 +507,14 @@
     def _(i):
         x = x2[i]
         rows = pl.ds(pl.multiple_of(i * ln, ln), ln)
+        xt[:, rows] = x.T
         got = (dot_nn(x, wh[:, :wide]) + bh[0:1, :wide]).astype(BF)
         kv[rows, :] = got
         qp = ((dot_nn(x, wh[:, wide:]) + bh[0:1, wide:]).astype(BF).astype(F32) * 0.125).astype(BF)
         for h in range(heads):
             q_scr[rows, 128 * h : 128 * h + HEAD] = qp[:, HEAD * h : HEAD * h + HEAD]
 
+    x_here = copy_here(xt, xt_out)
     q_here = copy_here(q_scr, q_out)
     kv_here = copy_here(kv, kv_out)
 
@@ -627,24 +547,24 @@
         w_here[w].wait()
         for k in (1, 2, 3):
             rc.arrived(n_z[w][k - 1], full_at[w](row, z ^ k), at_xz(0, k))
-        rc.start(n_x[w], row_at[w](row), row_at[w](row), at_x)
-        rc.start(n_y[w], row_at[w](row), row_at[w](row), at_c(2))
-        rc.start(n_c[w][0], row_at[w](row), row_at[w](row), at_c(1))
+        rc.start(n_x[w], lambda w=w: (row_at[w](row), row_at[w](row), at_x))
+        rc.start(n_y[w], lambda w=w: (row_at[w](row), row_at[w](row), at_c(2)))
+        rc.start(n_c[w][0], lambda w=w: (row_at[w](row), row_at[w](row), at_c(1)))
 
     row_x, row_y, row_d = row ^ 4, row ^ 2, row ^ 6
 
     def stage_corner(w):
         rc.arrived(n_x[w], row_at[w](row_x), at_x)
-        rc.start(n_d1[w], low_at[w](row_x), low_at[w](row_x), at_c(2))
-        rc.start(n_c[w][1], row_at[w](row_x), row_at[w](row_x), at_c(1))
+        rc.start(n_d1[w], lambda w=w: (low_at[w](row_x), low_at[w](row_x), at_c(2)))
+        rc.start(n_c[w][1], lambda w=w: (row_at[w](row_x), row_at[w](row_x), at_c(1)))
         rc.arrived(n_y[w], row_at[w](row_y), at_c(2))
-        rc.start(n_d2[w], high_at[w](row_y), high_at[w](row_y), at_x)
-        rc.start(n_c[w][2], row_at[w](row_y), row_at[w](row_y), at_c(1))
+        rc.start(n_d2[w], lambda w=w: (high_at[w](row_y), high_at[w](row_y), at_x))
+        rc.start(n_c[w][2], lambda w=w: (row_at[w](row_y), row_at[w](row_y), at_c(1)))
 
     def stage_core(w):
         rc.arrived(n_d1[w], low_at[w](row_d), at_c(2))
         rc.arrived(n_d2[w], high_at[w](row_d), at_x)
-        rc.start(n_c[w][3], row_at[w](row_d), row_at[w](row_d), at_c(1))
+        rc.start(n_c[w][3], lambda w=w: (row_at[w](row_d), row_at[w](row_d), at_c(1)))
 
     def stage_end(w):
         for i, r in zip(n_c[w], (row, row_x, row_y, row_d)):
@@ -708,17 +628,24 @@
 
     stage_plane(0)
     stage_plane(1)
-    pl.loop(0, 2)(block)
-    stage_plane(2)
-    pl.loop(2, 4)(block)
-    stage_corner(0)
-    stage_corner(1)
-    pl.loop(4, 6)(block)
+
+    @pl.loop(0, 6)
+    def _(qb):
+        block(qb)
+
+        @pl.when(qb == 1)
+        def _():
+            stage_plane(2)
+
+        @pl.when(qb == 3)
+        def _():
+            stage_corner(0)
+            stage_corner(1)
 
     n_ctx = [next(number) for _ in range(3)]
     ctx_at = lambda i: context.at[pl.ds(pl.multiple_of(i * own, 128), own)]
     for k in (1, 2, 3):
-        rc.start(n_ctx[k - 1], ctx_at(c ^ k), ctx_all.at[c], at_c(k))
+        rc.start(n_ctx[k - 1], lambda k=k: (ctx_at(c ^ k), ctx_all.at[c], at_c(k)))
     ctx_here = copy_here(ctx_at(c), ctx_all.at[c])
     stage_corner(2)
     stage_core(0)
@@ -752,7 +679,7 @@
         functools.partial(forward_kernel, heads, ln),
         out_shape=(
             sds((nc, 3 * ln // 2, group), BF),
-            sds((2 * nc, ln, width), BF),
+            sds((width, 2 * nc * ln), BF),
             sds((2 * nc * ln, heads * 128), BF),
             sds((2 * nc * ln, heads * 128), BF),
             sds((nr * wr, 3 * group), BF),
@@ -768,6 +695,7 @@
         out_specs=(hb,) * 9 + (vm,) * 3,
         scratch_shapes=[
             pltpu.VMEM((2 * nc, ln, width), BF),
+            pltpu.VMEM((width, 2 * nc * ln), BF),
             pltpu.VMEM((nr * wr, 3 * group), BF),
             pltpu.VMEM((8, 3 * group), F32),
             pltpu.VMEM((2 * nc * ln, heads * 128), BF),
@@ -787,6 +715,655 @@
         ),
         name="forward",
     )(tok2, seg2, w_head, b_head, b_unit, w_o, w_i, w_b)
+
+
+def add_into(dst, other, rows):
+    @pl.loop(0, rows // 16)
+    def _(i):
+        at = pl.ds(pl.multiple_of(i * 16, 16), 16)
+        for a, b in zip(dst, other):
+            a[at, :] = (a[at, :].astype(F32) + b[at, :].astype(F32)).astype(a.dtype)
+
+
+def backward_kernel(
+    heads,
+    ln,
+    d_ctx,
+    g_b,
+    g_i,
+    g_o,
+    out_low,
+    d_first,
+    small_in,
+    q_in,
+    kv_in,
+    xt_in,
+    wh_in,
+    lse,
+    ctx_t,
+    seg,
+    output,
+    d_tokens,
+    gf_b,
+    gf_i,
+    gf_o,
+    gf_h,
+    small,
+    bias,
+    q_scr,
+    kv,
+    xt,
+    wh,
+    d_got,
+    d_o,
+    kvt,
+    dkv,
+    dqt,
+    d_proj,
+    segc,
+    segr,
+    part,
+    got_c,
+    got_y,
+    got_z,
+    send_y,
+    send_z,
+    mine,
+    done,
+    o_b,
+    o_i,
+    o_o,
+    r_b,
+    r_i,
+    r_o,
+    x_b,
+    x_i,
+    x_o,
+    y_b,
+    y_i,
+    y_o,
+    z_b,
+    z_i,
+    z_o,
+    acc_h,
+    o_h,
+    x_h,
+    z_h,
+    send_h,
+    small_got,
+    bias_sum,
+    bias_got,
+    h_got,
+    bias_fin,
+    send,
+    recv,
+    local,
+):
+    d, c, z = (lax.axis_index(n) for n in ALL)
+    nc = 4
+    hl = ln // 2
+    own = ln + hl
+    half = z % 2
+    core, y = c % 2, c // 2
+    wr = gf_b.shape[0]
+    units = gf_b.shape[1]
+    width = out_low.shape[1]
+    wide = heads * 128
+    rc = Copies(send, recv)
+    at_c = lambda k: (d, c ^ k, z)
+    at_x = (1 - d, c, z)
+    at_z = lambda k: (d, c, z ^ k)
+    across = (d, z, c)
+
+    barrier = pltpu.get_barrier_semaphore()
+    everyone = [at_c(k) for k in (1, 2, 3)] + [at_z(k) for k in (1, 2, 3)] + [at_x]
+    for device in everyone:
+        pl.semaphore_signal(barrier, inc=1, device_id=device, device_id_type=MESH)
+
+    @pl.when(c != z)
+    def _():
+        pl.semaphore_signal(barrier, inc=1, device_id=across, device_id_type=MESH)
+
+    pl.semaphore_wait(barrier, len(everyone) + jnp.where(c != z, 1, 0))
+
+    number = iter(range(200))
+    local_number = iter(range(40))
+
+    def copy_here(src, dst):
+        copy = pltpu.make_async_copy(src, dst, local.at[next(local_number)])
+        copy.start()
+        return copy
+
+    flat = lambda ref: (lambda xy, h: (ref.at[xy, :, pl.ds(1536 * h, 1536)],))
+    weights = []
+    for own_b, got_b, x_buf, y_buf, z_buf, grad, final, is_o in (
+        (o_b, r_b, x_b, y_b, z_b, g_b, gf_b, False),
+        (o_i, r_i, x_i, y_i, z_i, g_i, gf_i, False),
+        (o_o, r_o, x_o, y_o, z_o, g_o, gf_o, True),
+    ):
+        n = [next(number) for _ in range(12)]
+        weights.append((own_b, got_b, x_buf, y_buf, z_buf, grad, final, is_o, n))
+    half_units = 2 * units
+
+    def of_core(w, which):
+        grad, is_o = w[5], w[7]
+        return grad.at[:, :, which] if is_o else grad.at[:, which]
+
+    def part_of(w, xy, h):
+        if w[7]:
+            return w[0].at[pl.ds(2 * h, 2), xy]
+        return w[0].at[xy, :, pl.ds(half_units * h, half_units)]
+
+    def views(w, xy, h):
+        if w[7]:
+            return [w[0].at[2 * h, xy], w[0].at[2 * h + 1, xy]]
+        return [w[0].at[xy, :, pl.ds(half_units * h, half_units)]]
+
+    def buf_views(w, ref, i):
+        return [ref.at[i, 0], ref.at[i, 1]] if w[7] else [ref.at[i]]
+
+    def unit_at(w, t):
+        xy = 2 * d + y
+        if w[7]:
+            return w[0].at[t, xy]
+        return w[0].at[xy, :, pl.ds(pl.multiple_of(t * units, 128), units)]
+
+    w_here = [copy_here(of_core(w, core), w[0]) for w in weights]
+    blk = lambda x_, y_: 2 * x_ + y_
+
+    def w_core_send(w):
+        rc.start(w[8][0], lambda: (of_core(w, 1 - core), w[1], at_c(1)))
+
+    def w_core_add(i):
+        w = weights[i]
+        w_here[i].wait()
+        rc.arrived(w[8][0], w[1], at_c(1))
+
+        @pl.loop(0, 4)
+        def _(xy):
+            if w[7]:
+                add_into([w[0].at[t, xy] for t in range(4)], [w[1].at[t, xy] for t in range(4)], wr)
+            else:
+                add_into([w[0].at[xy]], [w[1].at[xy]], wr)
+
+        n = w[8]
+        for j in range(2):
+            rc.start(n[1 + j], lambda j=j: (part_of(w, blk(1 - d, j), 0), w[2].at[j], at_x))
+            rc.start(n[3 + j], lambda j=j: (part_of(w, blk(j, 1 - y), 1), w[3].at[j], at_c(2)))
+
+    def w_plane(i):
+        w = weights[i]
+        n = w[8]
+        for j in range(2):
+            rc.arrived(n[1 + j], w[2].at[j], at_x)
+        for j in range(2):
+            add_into(views(w, blk(d, j), 0), buf_views(w, w[2], j), wr)
+        rc.start(n[5], lambda: (part_of(w, blk(d, 1 - y), 0), w[3].at[2], at_c(2)))
+        for j in range(2):
+            rc.arrived(n[3 + j], w[3].at[j], at_c(2))
+        for j in range(2):
+            add_into(views(w, blk(j, y), 1), buf_views(w, w[3], j), wr)
+        rc.start(n[6], lambda: (part_of(w, blk(1 - d, y), 1), w[2].at[2], at_x))
+
+    def w_corner(i):
+        w = weights[i]
+        n = w[8]
+        rc.arrived(n[5], w[3].at[2], at_c(2))
+        add_into(views(w, blk(d, y), 0), buf_views(w, w[3], 2), wr)
+        rc.arrived(n[6], w[2].at[2], at_x)
+        add_into(views(w, blk(d, y), 1), buf_views(w, w[2], 2), wr)
+        rc.start(n[7], lambda: (unit_at(w, z ^ 1), w[4].at[0], at_z(1)))
+        rc.start(n[8], lambda: (unit_at(w, z ^ 3), w[4].at[1], at_z(1)))
+
+    def w_line(i):
+        w = weights[i]
+        n = w[8]
+        rc.arrived(n[8], w[4].at[1], at_z(1))
+        add_into([unit_at(w, z ^ 2)], [w[4].at[1]], wr)
+        rc.start(n[9], lambda: (unit_at(w, z ^ 2), w[4].at[2], at_z(2)))
+        rc.arrived(n[7], w[4].at[0], at_z(1))
+        add_into([unit_at(w, z)], [w[4].at[0]], wr)
+
+    def w_end(i):
+        w = weights[i]
+        rc.arrived(w[8][9], w[4].at[2], at_z(2))
+        w[6][...] = unit_at(w, z)[...].astype(F32) + w[4].at[2][...].astype(F32)
+
+    whole_of = lambda t: (3 * t + 1) // 2
+    shared_of = lambda t: 1 + 3 * (t // 2)
+
+    class Line:
+        def __init__(self, at):
+            self.at = at
+            self.left = [next(number) for _ in range(3)]
+            self.right = [next(number) for _ in range(3)]
+
+        def begin(self, src):
+            rc.start(self.left[0], lambda: (src, self.at(z), (d, c, z + 1)), lambda: z < 3)
+            rc.start(self.right[0], lambda: (src, self.at(z), (d, c, z - 1)), lambda: z > 0)
+
+        def step(self, j):
+            from_left, from_right = z - j, z + j
+
+            @pl.when(z >= j)
+            def _():
+                rc.arrived(self.left[j - 1], self.at(from_left), (d, c, z - 1))
+
+            if j < 3:
+                rc.start(
+                    self.left[j],
+                    lambda: (self.at(z - j), self.at(z - j), (d, c, z + 1)),
+                    lambda: (z >= j) & (z < 3),
+                )
+
+            @pl.when(z + j <= 3)
+            def _():
+                rc.arrived(self.right[j - 1], self.at(from_right), (d, c, z + 1))
+
+            if j < 3:
+                rc.start(
+                    self.right[j],
+                    lambda: (self.at(z + j), self.at(z + j), (d, c, z - 1)),
+                    lambda: (z + j <= 3) & (z > 0),
+                )
+
+    whole_rows = lambda ref, a, n: (lambda t: ref.at[whole_of(t), pl.ds(a, n)])
+    shared_rows = lambda ref: (
+        lambda t: ref.at[shared_of(t), pl.ds(pl.multiple_of((t % 2) * hl, 128), hl)]
+    )
+    out_lines = [Line(whole_rows(output, 0, ln)), Line(shared_rows(output))]
+    tok_lines = [
+        Line(whole_rows(d_tokens, 0, hl)),
+        Line(whole_rows(d_tokens, hl, hl)),
+        Line(shared_rows(d_tokens)),
+    ]
+
+    n_ctx = [next(number) for _ in range(3)]
+    for k in (1, 2, 3):
+        rc.start(n_ctx[k - 1], lambda k=k: (d_ctx.at[c ^ k], d_got.at[c], at_c(k)))
+    ctx_here = copy_here(d_ctx.at[c], d_got.at[c])
+    for w in weights:
+        w_core_send(w)
+    kv_here = copy_here(kv_in, kv)
+    q_here = copy_here(q_in, q_scr)
+    n_small = [next(number) for _ in range(5)]
+    small_to = (at_c(1), at_c(2), at_x, at_z(1), at_z(2))
+    small[...] = small_in[...]
+
+    def small_send(i):
+        rc.start(n_small[i], lambda: (small_got.at[i, 1], small_got.at[i, 0], small_to[i]))
+
+    def small_step(i):
+        rc.arrived(n_small[i], small_got.at[i, 0], small_to[i])
+        small[...] += small_got[i, 0]
+        if i < 4:
+            small_got[i + 1, 1] = small[...]
+            small_send(i + 1)
+
+    small_got[0, 1] = small_in[...]
+    small_send(0)
+    wh_here = copy_here(wh_in, wh)
+    xt_here = copy_here(xt_in, xt)
+    out_lines[0].begin(out_low.at[pl.ds(0, ln)])
+    out_lines[1].begin(out_low.at[pl.ds(ln, hl)])
+    out_here = [
+        copy_here(out_low.at[pl.ds(0, ln)], out_lines[0].at(z)),
+        copy_here(out_low.at[pl.ds(ln, hl)], out_lines[1].at(z)),
+    ]
+
+    for i in range(nc):
+        for s in range(2):
+            line = seg[i, s : s + 1, :].astype(F32)
+            segr[2 * i + s, 0:1, :] = line
+            segc[2 * i + s] = jnp.broadcast_to(line, (128, ln)).T
+    dkv[...] = jnp.zeros_like(dkv)
+    d_o[...] = jnp.zeros_like(d_o)
+    d_proj[...] = jnp.zeros_like(d_proj)
+    bias_sum[...] = jnp.zeros_like(bias_sum)
+    kv_here.wait()
+
+    @pl.loop(0, nc)
+    def _(j):
+        for s in range(2):
+            rows = pl.ds(pl.multiple_of((2 * j + s) * ln, ln), ln)
+            for h in range(heads):
+                kvt[s * heads + h, :, pl.ds(pl.multiple_of(j * ln, ln), ln)] = kv[
+                    rows, 128 * h : 128 * h + 128
+                ].T
+
+    w_core_add(0)
+    small_step(0)
+    for k in (1, 2, 3):
+        rc.arrived(n_ctx[k - 1], d_got.at[c ^ k], at_c(k))
+    ctx_here.wait()
+
+    @pl.loop(0, nc)
+    def _(i):
+        rows = pl.ds(pl.multiple_of(i * own, 128), own)
+        for h in range(heads):
+            d_o[rows, 128 * h + HEAD : 128 * h + 128] = d_got[i, :, HEAD * h : HEAD * h + HEAD]
+
+    q_here.wait()
+    w_core_add(1)
+    w_core_add(2)
+    small_step(1)
+
+    def block(qb):
+        r0, r1, o0, o1, seq = block_rows(qb, half, ln)
+        b0 = jnp.where(qb < 4, qb, 2 * (qb - 4))
+        b1 = jnp.where(qb < 4, qb, 2 * (qb - 4) + 1)
+        s0 = pl.multiple_of(jnp.where(qb < 4, 0, hl * half), 128)
+        s1 = pl.multiple_of(jnp.where(qb < 4, hl, hl * half), 128)
+        sq = jnp.concatenate(
+            [
+                segr[2 * b0 + seq, 0:1, pl.ds(s0, hl)],
+                segr[2 * b1 + seq, 0:1, pl.ds(s1, hl)],
+            ],
+            1,
+        )
+        q, do, line, delta = [], [], [], []
+        for h in range(heads):
+            q.append(two(q_scr, r0, r1, hl, slice(128 * h, 128 * h + 128)))
+            do.append(two(d_o, o0, o1, hl, slice(128 * h, 128 * h + 128)))
+            line.append(two_lanes(lse, slice(h, h + 1), o0, o1, hl))
+            turned = do[h].astype(F32).T[HEAD:, :]
+            kept = two_lanes(ctx_t, slice(HEAD * h, HEAD * h + HEAD), o0, o1, hl)
+            delta.append(jnp.sum(turned * kept, 0, keepdims=True))
+        dqt[...] = jnp.zeros_like(dqt)
+
+        @pl.loop(0, nc)
+        def _(j):
+            rows = pl.ds(pl.multiple_of((2 * j + seq) * ln, ln), ln)
+            keys = pl.ds(pl.multiple_of(j * ln, ln), ln)
+            key_seg = segc[2 * j + seq]
+            same = jnp.concatenate([key_seg, key_seg], 1) == sq
+            for h in range(heads):
+                kvh = kv[rows, 128 * h : 128 * h + 128]
+                p = jnp.where(same, jnp.exp(dot_nt(kvh, q[h]) - line[h]), 0.0)
+                ds = (p * (dot_nt(kvh, do[h]) - delta[h])).astype(BF)
+                dkv[rows, 128 * h : 128 * h + 128] += dot_nn(ds, q[h]) + dot_nn(
+                    p.astype(BF), do[h]
+                )
+                dqt[h] += dot_nn(kvt[seq * heads + h, :, keys], ds)
+
+        turned = jnp.concatenate([dqt[h, :HEAD, :] for h in range(heads)], 0).T * 0.125
+        bias_sum[0:1, wide:] += jnp.sum(turned, 0, keepdims=True)
+        low = turned.astype(BF)
+        d_proj[pl.ds(r0, hl), wide:] = low[:hl]
+        d_proj[pl.ds(r1, hl), wide:] = low[hl:]
+
+    n_tc = [[next(number), next(number)] for _ in range(2)]
+    n_ty = [[next(number), next(number)] for _ in range(2)]
+    n_tz = next(number)
+
+    def rows_of(cb, s):
+        rows = pl.ds(pl.multiple_of((2 * cb + s) * ln, ln), ln)
+        got = dkv[rows, :]
+        bias_sum[0:1, :wide] += jnp.sum(got, 0, keepdims=True)
+        d_proj[rows, :wide] = got.astype(BF)
+        part[cb, s] = dot_nt(d_proj[rows, :], wh[...]).astype(BF)
+
+    def t_partial(s):
+        rows_of(c ^ 3, s)
+        rc.start(n_tc[s][0], lambda: (part.at[c ^ 3, s], got_c.at[s, 0], at_c(1)))
+        rows_of(c ^ 1, s)
+        rc.start(n_tc[s][1], lambda: (part.at[c ^ 1, s], got_c.at[s, 1], at_c(1)))
+        rows_of(c ^ 2, s)
+        rows_of(c, s)
+
+    def t_core(s):
+        rc.arrived(n_tc[s][0], got_c.at[s, 0], at_c(1))
+        for k in range(2):
+            at = slice(k * hl, k * hl + hl)
+            send_y[s, at] = (part[c ^ 2, s, at].astype(F32) + got_c[s, 0, at].astype(F32)).astype(BF)
+            rc.start(
+                n_ty[s][k],
+                lambda k=k: (
+                    send_y.at[s, pl.ds(k * hl, hl)],
+                    got_y.at[s, pl.ds(k * hl, hl)],
+                    at_c(2),
+                ),
+            )
+        rc.arrived(n_tc[s][1], got_c.at[s, 1], at_c(1))
+        mine[s] = part[c, s].astype(F32) + got_c[s, 1].astype(F32)
+
+    def t_shared():
+        for k in range(2):
+            rc.arrived(n_ty[1][k], got_y.at[1, pl.ds(k * hl, hl)], at_c(2))
+        mine[1] += got_y[1].astype(F32)
+        send_z[...] = mine[1, pl.ds(pl.multiple_of((1 - half) * hl, 128), hl)].astype(BF)
+        rc.start(n_tz, lambda: (send_z, got_z, at_z(1)))
+
+    def t_shared_end():
+        rc.arrived(n_tz, got_z, at_z(1))
+        mine_half = mine[1, pl.ds(pl.multiple_of(half * hl, 128), hl)]
+        done[ln:, :] = (mine_half + got_z[...].astype(F32) + d_first[ln:, :]).astype(BF)
+        tok_lines[2].begin(done.at[pl.ds(ln, hl)])
+
+    def t_whole(k):
+        at = slice(k * hl, k * hl + hl)
+        rc.arrived(n_ty[0][k], got_y.at[0, pl.ds(k * hl, hl)], at_c(2))
+        done[at, :] = (mine[0, at] + got_y[0, at].astype(F32) + d_first[at, :]).astype(BF)
+        tok_lines[k].begin(done.at[pl.ds(k * hl, hl)])
+
+    n_h = [next(number) for _ in range(8)]
+
+    def h_partial():
+        @pl.loop(0, 2 * nc)
+        def _(i):
+            rows = pl.ds(pl.multiple_of(i * ln, ln), ln)
+            acc_h[...] += dot_nn(xt[:, rows], d_proj[rows, :])
+
+        o_h[...] = acc_h[...].astype(BF)
+        rows_x = lambda x_: pl.ds(pl.multiple_of(x_ * 4 * wr, wr), 4 * wr)
+        rc.start(n_h[0], lambda: (o_h.at[rows_x(1 - d)], x_h, at_x))
+
+    h_at = lambda t: o_h.at[pl.ds(pl.multiple_of((4 * d + t) * wr, wr), wr)]
+
+    def h_plane():
+        rc.arrived(n_h[0], x_h, at_x)
+        add_into([o_h.at[pl.ds(pl.multiple_of(d * 4 * wr, wr), 4 * wr)]], [x_h], 4 * wr)
+        rc.start(n_h[1], lambda: (h_at(z ^ 3), z_h.at[1], at_z(1)))
+        rc.start(n_h[2], lambda: (h_at(z ^ 1), z_h.at[0], at_z(1)))
+
+    def h_line():
+        rc.arrived(n_h[1], z_h.at[1], at_z(1))
+        add_into([h_at(z ^ 2)], [z_h.at[1]], wr)
+        rc.start(n_h[3], lambda: (h_at(z ^ 2), z_h.at[2], at_z(2)))
+        rc.arrived(n_h[2], z_h.at[0], at_z(1))
+        add_into([h_at(z)], [z_h.at[0]], wr)
+
+    def h_end():
+        rc.arrived(n_h[3], z_h.at[2], at_z(2))
+        send_h[...] = h_at(z)[...].astype(F32) + z_h[2].astype(F32)
+        rc.start(n_h[4], lambda: (send_h, h_got, across), lambda: c != z)
+
+        @pl.when(c == z)
+        def _():
+            h_got[...] = send_h[...]
+
+    n_bias = [next(number) for _ in range(4)]
+    bias_to = (at_x, at_z(1), at_z(2))
+
+    def bias_send(i):
+        bias_got[i, 1] = bias_sum[...]
+        rc.start(n_bias[i], lambda: (bias_got.at[i, 1], bias_got.at[i, 0], bias_to[i]))
+
+    def bias_step(i):
+        rc.arrived(n_bias[i], bias_got.at[i, 0], bias_to[i])
+        bias_sum[...] += bias_got[i, 0]
+        if i < 2:
+            bias_send(i + 1)
+            return
+        rc.start(n_bias[3], lambda: (bias_sum, bias_fin, across), lambda: c != z)
+
+        @pl.when(c == z)
+        def _():
+            bias_fin[...] = bias_sum[...]
+
+    wh_here.wait()
+
+    @pl.loop(0, 6)
+    def _(i):
+        block(jnp.where(i < 2, i + 4, i - 2))
+
+        @pl.when(i == 1)
+        def _():
+            t_partial(1)
+            w_plane(0)
+            for line in out_lines:
+                line.step(1)
+            small_step(2)
+            t_core(1)
+
+        @pl.when(i == 3)
+        def _():
+            w_plane(1)
+            w_plane(2)
+            small_step(3)
+            for line in out_lines:
+                line.step(2)
+            t_shared()
+
+        @pl.when(i == 4)
+        def _():
+            w_corner(0)
+            small_step(4)
+            t_shared_end()
+
+    t_partial(0)
+    t_core(0)
+    bias_send(0)
+    acc_h[...] = jnp.zeros_like(acc_h)
+    xt_here.wait()
+    h_partial()
+    w_corner(1)
+    w_corner(2)
+    t_whole(0)
+    t_whole(1)
+    for line in out_lines:
+        line.step(3)
+    tok_lines[2].step(1)
+    h_plane()
+    bias_step(0)
+    w_line(0)
+    tok_lines[0].step(1)
+    tok_lines[1].step(1)
+    tok_lines[2].step(2)
+    w_line(1)
+    w_line(2)
+    bias_step(1)
+    h_line()
+    tok_lines[0].step(2)
+    tok_lines[1].step(2)
+    bias_step(2)
+    h_end()
+    w_end(0)
+    w_end(1)
+    w_end(2)
+    tok_here = [
+        copy_here(done.at[pl.ds(0, hl)], tok_lines[0].at(z)),
+        copy_here(done.at[pl.ds(hl, hl)], tok_lines[1].at(z)),
+        copy_here(done.at[pl.ds(ln, hl)], tok_lines[2].at(z)),
+    ]
+    for line in tok_lines:
+        line.step(3)
+
+    @pl.when(c != z)
+    def _():
+        rc.arrived(n_h[4], h_got, across)
+        rc.arrived(n_bias[3], bias_fin, across)
+
+    gf_h[...] = h_got[...]
+    bias[...] = bias_fin[...]
+
+    for copy in out_here + tok_here:
+        copy.wait()
+    rc.sent()
+
+
+def backward(d_ctx, g_b, g_i, g_o, out_low, d_first, small, q, kv, xt, wh, lse, ctx_t, seg, heads, seqs):
+    nc, own, group = d_ctx.shape
+    ln = own * 2 // 3
+    hl = ln // 2
+    width = out_low.shape[1]
+    wr, all_units = g_b.shape[2:]
+    units = all_units // 4
+    hb = pl.BlockSpec(memory_space=pl.ANY)
+    vm = pl.BlockSpec(memory_space=pltpu.VMEM)
+    sds = jax.ShapeDtypeStruct
+    v = pltpu.VMEM
+    rows = nc * own
+    n2 = 2 * nc * ln
+    return pl.pallas_call(
+        functools.partial(backward_kernel, heads, ln),
+        out_shape=(
+            sds((seqs, ln, width), BF),
+            sds((seqs, ln, width), BF),
+            sds((wr, units), F32),
+            sds((wr, units), F32),
+            sds((wr, group), F32),
+            sds((wr, 3 * group), F32),
+            sds(small.shape, F32),
+            sds((8, 3 * group), F32),
+        ),
+        in_specs=[hb] * 5 + [vm, vm] + [hb] * 4 + [vm] * 3,
+        out_specs=(hb, hb) + (vm,) * 6,
+        scratch_shapes=[
+            v((n2, heads * 128), BF),
+            v((n2, heads * 128), BF),
+            v((width, n2), BF),
+            v((width, 3 * group), BF),
+            v((nc, own, group), BF),
+            v((rows, heads * 128), BF),
+            v((2 * heads, 128, nc * ln), BF),
+            v((n2, heads * 128), F32),
+            v((heads, 128, ln), F32),
+            v((n2, 3 * group), BF),
+            v((2 * nc, ln, 128), F32),
+            v((2 * nc, 8, ln), F32),
+            v((nc, 2, ln, width), BF),
+            v((2, 2, ln, width), BF),
+            v((2, ln, width), BF),
+            v((hl, width), BF),
+            v((2, ln, width), BF),
+            v((hl, width), BF),
+            v((2, ln, width), F32),
+            v((own, width), BF),
+            v((4, wr, all_units), BF),
+            v((4, wr, all_units), BF),
+            v((4, 4, wr, group), BF),
+            v((4, wr, all_units), BF),
+            v((4, wr, all_units), BF),
+            v((4, 4, wr, group), BF),
+            v((3, wr, 2 * units), BF),
+            v((3, wr, 2 * units), BF),
+            v((3, 2, wr, group), BF),
+            v((3, wr, 2 * units), BF),
+            v((3, wr, 2 * units), BF),
+            v((3, 2, wr, group), BF),
+            v((3, wr, units), BF),
+            v((3, wr, units), BF),
+            v((3, wr, group), BF),
+            v((width, 3 * group), F32),
+            v((width, 3 * group), BF),
+            v((4 * wr, 3 * group), BF),
+            v((3, wr, 3 * group), BF),
+            v((wr, 3 * group), F32),
+            v((5, 2) + small.shape, F32),
+            v((8, 3 * group), F32),
+            v((3, 2, 8, 3 * group), F32),
+            v((wr, 3 * group), F32),
+            v((8, 3 * group), F32),
+            pltpu.SemaphoreType.DMA((130,)),
+            pltpu.SemaphoreType.DMA((130,)),
+            pltpu.SemaphoreType.DMA((40,)),
+        ],
+        compiler_params=pltpu.CompilerParams(
+            vmem_limit_bytes=58 << 20, collective_id=1, has_side_effects=True
+        ),
+        name="backward",
+    )(d_ctx, g_b, g_i, g_o, out_low, d_first, small, q, kv, xt, wh, lse, ctx_t, seg)
 
 
 def head_order(kinds, heads):
@@ -828,7 +1405,7 @@
     ctx_all = in_order(exchange_axis(context.reshape(nc, ln + hl, group), "ctx", nc, c), c)
     return (
         ctx_all,
-        x2,
+        x2.reshape(-1, width).T,
         q,
         kv,
         wh,
@@ -860,6 +1437,62 @@
     info = jnp.concatenate([lo, hi, half[None]]).astype(jnp.int32)
     seg_flat = seg2.reshape(2 * nc * ln)
     return info, seg_flat[:, None], seg_flat[None, :]
+
+
+def backward_plain(
+    sizes, me, d_ctx, low, out_low, d_first, small, q, kv, xt, wh, lse, ctx_t, seg_all, heads, seqs
+):
+    nd, nc, nt = sizes
+    d, c, z = me
+    own, group = d_ctx.shape[1:]
+    ln = own * 2 // 3
+    hl = ln // 2
+    half = z % 2
+    width = out_low.shape[1]
+    units = low[0].shape[1] // nt
+    nr = nd * nc
+    wr = width // nr
+    info, seg_col, seg_row = key_blocks(seg_all, half, ln, nc)
+
+    def spread_rows(rows_low, dtype):
+        out = jnp.zeros((seqs, ln, width), dtype)
+        parts = [rows_low] + [swap_with(rows_low, "tp", nt, k) for k in range(1, nt)]
+        for k, part in enumerate(parts):
+            t = z ^ k
+            part = part.astype(dtype)
+            out = lax.dynamic_update_slice(out, part[None, :ln], ((3 * t + 1) // 2, 0, 0))
+            out = lax.dynamic_update_slice(
+                out, part[None, ln:], (1 + 3 * (t // 2), (t % 2) * hl, 0)
+            )
+        return out
+
+    by_unit = lambda g: jnp.transpose(g.reshape(nr, wr, nt, units), (2, 0, 1, 3))
+    g_back = scatter_weight(by_unit(low[0]), sizes, me)
+    g_in = scatter_weight(by_unit(low[1]), sizes, me)
+    g_out = scatter_weight(low[2].reshape(nt, nr, wr, group), sizes, me)
+    output = spread_rows(out_low, BF)
+    small = lax.psum(small, ALL)
+    d_ctx = in_order(exchange_axis(d_ctx, "ctx", nc, c), c).reshape(nc * own, heads, HEAD)
+    d_ctx = jnp.concatenate([jnp.zeros_like(d_ctx), d_ctx], -1).reshape(nc * own, heads * 128)
+    d_q, d_kv, d_bias = attend_back(
+        info, q, kv, d_ctx, seg_col, seg_row, lse, ctx_t, heads, ln, nc
+    )
+    d_proj = jnp.concatenate([d_kv, d_q], -1)
+    part = jnp.einsum("tf,df->td", d_proj, wh, preferred_element_type=F32)
+    part = lax.psum_scatter(
+        part.reshape(nc, 2 * ln, width), "ctx", scatter_dimension=0, tiled=False
+    ).reshape(2, ln, width)
+    shared = part[1].reshape(2, hl, width)
+    shared = lax.dynamic_index_in_dim(shared, half, 0, keepdims=False) + swap_with(
+        lax.dynamic_index_in_dim(shared, 1 - half, 0, keepdims=False), "tp", nt, 1
+    )
+    d_own = (jnp.concatenate([part[0], shared], 0) + d_first).astype(BF)
+    d_tokens = spread_rows(d_own, F32)
+    g_h = scatter_heads(jnp.dot(xt, d_proj, preferred_element_type=F32).astype(BF), sizes, me)
+    slots = jnp.zeros((nc,) + d_bias[0].shape, F32)
+    slots = lax.psum(lax.dynamic_update_index_in_dim(slots, d_bias[0], c, 0), ALL)
+    d_bias = lax.dynamic_index_in_dim(slots, z, 0, keepdims=False)
+    return output, d_tokens, g_back, g_in, g_out, g_h, small, d_bias
 
 
 def per_device(
@@ -917,13 +1550,11 @@
     b_unit = jnp.broadcast_to(in_bias[None], (8, units))
     args = (tok2, seg2, w_head, b_head, b_unit, w_out, w_in, w_back, heads)
     got = forward(*args) if sizes == (2, 4, 4) else forward_plain(sizes, me, *args)
-    ctx_all, x2, q, kv, wh, w_o, w_i, w_b, b_in, lse, ctx_t, seg_all = got
-    x2 = x2.reshape(2 * nc * ln, width)
+    ctx_all, xt, q, kv, wh, w_o, w_i, w_b, b_in, lse, ctx_t, seg_all = got
     w_o = w_o.reshape(nt, width, group)
     w_i = w_i.reshape(width, nt * units)
     w_b = w_b.reshape(width, nt * units)
     b_in = b_in[:, 0].reshape(nt * units)
-    info, seg_col, seg_row = key_blocks(seg_all, half, ln, nc)
     own = ln + hl
 
     x_own = own_rows(tokens).astype(F32)
@@ -937,18 +1568,6 @@
     second = normed + branch + back_bias
     normal_two, rstd_two = norm_parts(second)
     out_low = (normal_two * gain_two + shift_two).astype(BF)
-
-    def spread_rows(rows_low, dtype):
-        out = jnp.zeros((seqs, ln, width), dtype)
-        parts = [rows_low] + [swap_with(rows_low, "tp", nt, k) for k in range(1, nt)]
-        for k, part in enumerate(parts):
-            t = z ^ k
-            part = part.astype(dtype)
-            out = lax.dynamic_update_slice(out, part[None, :ln], (whole_of(t), 0, 0))
-            out = lax.dynamic_update_slice(
-                out, part[None, ln:], (shared_of(t), half_of(t) * hl, 0)
-            )
-        return out
 
     d_second, d_gain_two, d_shift_two = norm_back(
         own_rows(cotangent).astype(F32), normal_two, rstd_two, gain_two
@@ -967,59 +1586,43 @@
     d_out_bias = jnp.sum(d_first, 0)
     d_w_out = jnp.einsum("td,gtf->gdf", d_first_low, ctx_all, preferred_element_type=F32)
     d_ctx = jnp.einsum("td,gdf->gtf", d_first_low, w_o, preferred_element_type=F32).astype(BF)
-    d_ctx = in_order(exchange_axis(d_ctx, "ctx", nc, c), c).reshape(nc * own, heads, HEAD)
-    d_ctx = jnp.concatenate([jnp.zeros_like(d_ctx), d_ctx], -1).reshape(nc * own, heads * 128)
-
-    nr = nd * nc
-    by_unit = lambda g: jnp.transpose(g.astype(BF).reshape(nr, wr, nt, units), (2, 0, 1, 3))
-    g_back = scatter_weight(by_unit(d_w_back), sizes, me)
-    g_in = scatter_weight(by_unit(d_w_in), sizes, me)
-    g_out = scatter_weight(d_w_out.astype(BF).reshape(nt, nr, wr, group), sizes, me)
-    output = spread_rows(out_low, BF)
-    small = sum_all(
-        jnp.concatenate(
-            [
-                jnp.stack(
-                    [d_out_bias, d_gain_one, d_shift_one, d_back_bias, d_gain_two, d_shift_two]
-                ).reshape(-1),
-                d_in_bias.reshape(-1),
-            ]
-        ),
-        sizes,
+    small = jnp.concatenate(
+        [d_out_bias, d_gain_one, d_shift_one, d_back_bias, d_gain_two, d_shift_two, d_in_bias]
     )
-
-    d_q, d_kv, d_bias = attend_back(
-        info, q, kv, d_ctx, seg_col, seg_row, lse, ctx_t, heads, ln, nc
-    )
-    d_proj = jnp.concatenate([d_kv, d_q], -1)
-    part = jnp.einsum("tf,df->td", d_proj, wh, preferred_element_type=F32).astype(BF)
-    part = part.reshape(nc // 2, 2, 2, ln, width)
-    core, y = c % 2, c // 2
-    part = add_low(
-        lax.dynamic_index_in_dim(part, core, 1, keepdims=False),
-        swap_with(lax.dynamic_index_in_dim(part, 1 - core, 1, keepdims=False), "ctx", nc, 1),
-    )
-    part = add_low(
-        lax.dynamic_index_in_dim(part, y, 0, keepdims=False),
-        swap_with(lax.dynamic_index_in_dim(part, 1 - y, 0, keepdims=False), "ctx", nc, 2),
-    )
-    shared = part[1].reshape(2, hl, width)
-    shared = lax.dynamic_index_in_dim(shared, half, 0, keepdims=False).astype(F32) + swap_with(
-        lax.dynamic_index_in_dim(shared, 1 - half, 0, keepdims=False), "tp", nt, 1
-    ).astype(F32)
-    d_own = (jnp.concatenate([part[0].astype(F32), shared], 0) + d_first).astype(BF)
-    d_tokens = spread_rows(d_own, F32)
-
-    d_wh = jnp.einsum("td,tf->df", x2, d_proj, preferred_element_type=F32).astype(BF)
-    g_qkv = jnp.stack(head_kinds(scatter_heads(d_wh, sizes, me), heads), 1)
-    d_qb, _, d_vb = head_kinds(d_bias[0], heads)
+    low = (d_w_back.astype(BF), d_w_in.astype(BF), d_w_out.astype(BF))
+    if sizes == (2, 4, 4):
+        small = jnp.concatenate([small, jnp.zeros((-small.shape[0] % 1024,), F32)])
+        output, d_tokens, g_back, g_in, g_out, g_h, small, d_bias = backward(
+            d_ctx,
+            low[0].reshape(4, 2, wr, nt * units),
+            low[1].reshape(4, 2, wr, nt * units),
+            low[2].reshape(nt, 4, 2, wr, group),
+            out_low,
+            d_first,
+            small.reshape(-1, 128),
+            q,
+            kv,
+            xt,
+            wh,
+            lse,
+            ctx_t,
+            seg_all,
+            heads,
+            seqs,
+        )
+        d_tokens = d_tokens.astype(F32)
+        small = small.reshape(-1)
+        d_bias = d_bias[0]
+    else:
+        output, d_tokens, g_back, g_in, g_out, g_h, small, d_bias = backward_plain(
+            sizes, me, d_ctx, low, out_low, d_first, small, q, kv, xt, wh, lse, ctx_t, seg_all, heads, seqs
+        )
+    g_qkv = jnp.stack(head_kinds(g_h, heads), 1)
+    d_qb, _, d_vb = head_kinds(d_bias, heads)
     qv = jnp.concatenate([d_qb, d_vb])
-    slots = lax.dynamic_update_index_in_dim(jnp.zeros((nc, 2 * group), F32), qv, c, 0)
-    slots = sum_all(slots, sizes)
-    qv = lax.dynamic_index_in_dim(slots, z, 0, keepdims=False)
     wide = small[: 6 * width].reshape(6, width)
     g_in_bias = lax.dynamic_index_in_dim(
-        small[6 * width :].reshape(nt, units), z, 0, keepdims=False
+        small[6 * width : 6 * width + nt * units].reshape(nt, units), z, 0, keepdims=False
     )
     return (
         output,

time: 534 us -> 344 us (0.64)
  starting transfers between devices: 142 us -> 0 us
  Pallas kernels: 128 us -> 262 us
  local copies, waits for them, and re-layouts: 117 us -> 28.8 us
  waiting for transfers between devices: 77.1 us -> 0 us
  matrix products: 45.6 us -> 37.6 us
  other arithmetic: 16.5 us -> 9.24 us
    ppermute x54 -> x0, starting transfers between devices: 142 us -> none  [the longest x46 130 us: swap_with(): return lax.ppermute(value, axis, [(i, i ^ mask) for i in range(size)])]
    pallas_call x1, Pallas kernels: 21.4 us -> 156 us  [backward(): pl.pallas_call(functools.partial(backward_kernel, heads, ln), out_shape=(...]
    ppermute x54 -> x0, waiting for transfers between devices: 77.1 us -> none  [the longest x46 74.2 us: swap_with(): return lax.ppermute(value, axis, [(i, i ^ mask) for i in range(size)])]
    dynamic_update_slice x21 -> x0, local copies, waits for them, and re-layouts: 29.7 us -> none  [the longest x4 15.5 us: in_order(): out = lax.dynamic_update_index_in_dim(out, part, me ^ k, axis)]
    reshape x7 -> x1, local copies, waits for them, and re-layouts: 27 us -> 0.01 us  [per_device(): small[6 * width:6 * width + nt * units].reshape(nt, units)]
    dynamic_slice x7 -> x1, local copies, waits for them, and re-layouts: 10.4 us -> 0.61 us  [per_device(): lax.dynamic_index_in_dim(small[6 * width:6 * width + nt * units].reshape(...]
    another operation x13 -> x3, local copies, waits for them, and re-layouts: 9.46 us -> 1.07 us  [per_device(): g_qkv = jnp.stack(head_kinds(g_h, heads), 1)]
    unnamed x114 -> x91, local copies, waits for them, and re-layouts: 20.7 us -> 12.6 us
  transfers between devices with their start and end apart: 54 -> 0, of which waited for: 20 -> 0; matrix products, arithmetic and copies ran while one was open for 25% -> 0% of each run, Pallas kernels for 4% -> 0%
where the time goes in v2:
time: 344 us; the launch traced here: 339 us
  Pallas kernels  262 us (76%)
  matrix products  37.6 us (11%)
  local copies, waits for them, and re-layouts  28.8 us (8%)
  other arithmetic  9.24 us (3%)
    pallas_call x1, Pallas kernels, backward(): pl.pallas_call(functools.partial(backward_kernel, heads, ln), out_shape=(...  156 us
    pallas_call x1, Pallas kernels, forward(): pl.pallas_call(functools.partial(forward_kernel, heads, ln), out_shape=(s...  106 us
    unnamed x91, local copies, waits for them, and re-layouts  12.6 us
    dot_general x1, matrix products, per_device(): inner = jnp.dot(normed_low, w_i, preferred_element_type=F32) + b_in  12 us

profile of v2, /device:TPU:0, one launch (start us, length us, event | category | flops | bytes accessed | tf_op | source)
XLA Modules:
  0.0 339.4 jit_solution(8592904569253591601)
XLA Ops:
  0.7 1.3 constant_dynamic-slice_fusion.3
  2.1 0.8 constant_dynamic-slice_fusion.1
  3.2 0.1 copy.67
  3.4 0.1 copy.65
  3.8 0.9 copy-done.6
  4.7 106.3 %forward.1 = (bf16[4,384,192]{2,1,0:T(8,128)(2,1)S(1)}, bf16[768,2048]{1,0:T(8,128)(2,1)S(1)}, bf16[2048,384]{1,0:T(8,128)(2,1)S(1)}, bf16[2048,384]{1,0:T(8,128...) custom-call(bf16[2,256,768]{2,1,0:T(8,128)(2,1)S(1)} %pad_maximum_fu, ...), custom_call_target="tpu_custom_call" | custom-call | tf_op jit(solution)/shard_map/forward/pallas_call | solution.py:678
  111.0 1.6 copy-done
  112.6 1.2 copy-done.1
  113.8 1.1 copy-done.2
  115.0 1.0 copy-done.3
  116.0 1.0 copy-done.4
  117.0 0.6 copy-done.7
  117.6 0.6 copy-done.9
  118.2 0.6 copy-done.10
  118.8 1.1 dynamic-slice_bitcast_fusion.1
  120.0 2.1 fusion.43
  122.1 0.3 multiply_reduce_fusion.3
  122.4 1.7 slice.79
  124.1 12.0 %fusion.2 = (bf16[384,3072]{1,0:T(8,128)(2,1)S(1)}, f32[384,3072]{1,0:T(8,128)S(1)}) fusion(f32[3072]{0:T(1024)S(1)} %bitcast.80, bf16[768,3072]{1,0:T(8,128)(2,1)S(1)} %bitcast.83, f32[384,768]{1,0:T(8,128)S(1)} %get-tuple-element.84, f32[768]{0:T(1024)S(1)} %copy-done.33, f32[768]{0:T(1024)S(1)} %copy-done.26, f32[384]{0:T(512)S(1)} %add_rsqrt_fusion.1, ...), kind=kOutput, calls=%fused_computation.6 | convolution fusion | flops 1891270656 | bytes 12997632 | tf_op jit(solution)/shard_map/dot_general | solution.py:1565
  136.2 2.2 fusion.44
  138.4 0.3 multiply_reduce_fusion.2
  138.7 1.0 dynamic-slice_bitcast_fusion
  139.8 1.5 fusion.25
  141.3 0.4 fusion.38
  141.7 3.8 %fusion.45 = (f32[3072]{0:T(1024)S(1)}, bf16[384,3072]{1,0:T(8,128)(2,1)S(1)}) fusion(f32[384,3072]{1,0:T(8,128)S(1)} %get-tuple-element.86, f32[3072]{0:T(1024)S(1)} %bitcast.81, bf16[768,3072]{1,0:T(8,128)(2,1)S(1)} %bitcast.88, f32[384,768]{1,0:T(8,128)S(1)} %get-tuple-element.64), kind=kOutput, calls=%fused_computation.114 | convolution fusion | flops 1826386944 | bytes 13000704 | tf_op jit(solution)/shard_map/dot_general | solution.py:1578
  145.6 2.4 multiply_reduce_fusion
  148.0 1.4 fusion.40
  149.5 3.1 fusion.18
  152.7 2.6 copy.57
  155.3 6.4 %convolution_convert_fusion = bf16[768,3072]{1,0:T(8,128)(2,1)} fusion(bf16[384,3072]{1,0:T(8,128)(2,1)} %copy-done.36, f32[384,768]{1,0:T(8,128)S(1)} %copy-done.13, f32[768]{0:T(1024)S(1)} %copy-done.33, f32[768]{0:T(1024)S(1)} %copy-done.26, f32[384]{0:T(512)S(1)} %add_rsqrt_fusion.1, f32[384]{0:T(512)S(1)} %broadcast_multiply_fusion.5), kind=kOutput, calls=%fused_computation.2 | convolution fusion | flops 1815773184 | bytes 8266752 | tf_op jit(solution)/shard_map/td,tf->df/dot_general | solution.py:1582
  161.7 4.5 %convolution_convert_fusion.1 = bf16[768,3072]{1,0:T(8,128)(2,1)} fusion(bf16[384,3072]{1,0:T(8,128)(2,1)S(1)} %copy-done.35, f32[384,768]{1,0:T(8,128)S(1)} %copy-done.17), kind=kOutput, calls=%fused_computation.3 | convolution fusion | flops 1814593536 | bytes 8257536 | tf_op jit(solution)/shard_map/td,tf->df/dot_general | solution.py:1577
  166.2 1.0 convolution_convert_fusion.3
  167.2 1.2 copy.55
  168.4 155.8 %backward.1 = (bf16[6,256,768]{2,1,0:T(8,128)(2,1)}, bf16[6,256,768]{2,1,0:T(8,128)(2,1)}, f32[96,768]{1,0:T(8,128)}, f32[96,768]{1,0:T(8,128)}, f32[96,192]{1,0...) custom-call(bf16[4,384,192]{2,1,0:T(8,128)(2,1)} %bitcast.71, ...), custom_call_target="tpu_custom_call" | custom-call | tf_op jit(solution)/shard_map/backward/pallas_call | solution.py:1298
  324.2 0.9 slice.81
  325.1 0.1 copy.58
  325.4 0.9 slice_bitcast_fusion
  326.3 0.7 pad_maximum_fusion.2
  327.1 4.4 %convert_element_type.58 = f32[6,256,768]{2,1,0:T(8,128)} convert(bf16[6,256,768]{2,1,0:T(8,128)(2,1)} %get-tuple-element.48) | non-fusion elementwise | flops 1179648 | bytes 7077888 | tf_op jit(solution)/shard_map/convert_element_type | solution.py:1613
  331.5 0.6 dynamic-slice_reduce_fusion
  332.1 0.6 slice_bitcast_fusion.2
  332.7 0.7 slice_reduce_fusion.1
  333.6 0.6 reshape_squeeze.11
  334.2 1.3 slice.84
  335.5 1.4 copy.80
  336.9 0.6 copy.81
  337.5 0.7 copy.82
  338.3 0.7 copy.83
  (107 shorter events, 1.1 us)
Async XLA Ops:
  0.6 2.4 copy-start.20
  0.7 2.8 copy-start.28
  0.7 3.0 copy-start.29
  0.7 3.0 copy-start.27
  0.7 3.0 copy-start.8
  0.7 3.0 copy-start.5
  2.0 1.7 copy-start.15
  2.0 117.9 %copy-start.31 = (f32[768]{0:T(1024)S(1)}, f32[768]{0:T(1024)}, u32[]{:S(2)}) copy-start(f32[768]{0:T(1024)} %param.22) | copy-start | bytes 9220
  3.7 0.9 copy-start.6
  111.0 1.6 copy-start
  112.6 1.2 copy-start.1
  113.8 1.2 copy-start.2
  115.0 1.0 copy-start.3
  116.0 1.0 copy-start.4
  117.0 0.6 copy-start.7
  117.6 0.6 copy-start.9
  118.2 0.6 copy-start.10
  118.8 5.2 %copy-start.33 = (f32[768]{0:T(1024)S(1)}, f32[768]{0:T(1024)}, u32[]{:S(2)}) copy-start(f32[768]{0:T(1024)} %param.24) | copy-start | bytes 9220
  120.0 4.1 %copy-start.26 = (f32[768]{0:T(1024)S(1)}, f32[768]{0:T(1024)}, u32[]{:S(2)}) copy-start(f32[768]{0:T(1024)} %param.23) | copy-start | bytes 9220
  120.0 4.1 %copy-start.30 = (bf16[8,96,3072]{2,1,0:T(8,128)(2,1)S(1)}, bf16[8,96,3072]{2,1,0:T(8,128)(2,1)}, u32[]{:S(2)}) copy-start(bf16[8,96,3072]{2,1,0:T(8,128)(2,1)} %get-tuple-element.37) | copy-start | bytes 14155780
  120.0 16.1 %slice-start = ((s8[4718592]{0:T(1024)(128)(4,1)}), s8[4194304]{0:T(1024)(128)(4,1)S(1)}, s32[]{:S(2)}) async-start(s8[4718592]{0:T(1024)(128)(4,1)} %bitcast.85), calls=%async_computation | async-start | bytes 8388608
  122.1 25.9 %copy-start.12 = (f32[384,768]{1,0:T(8,128)}, f32[384,768]{1,0:T(8,128)S(1)}, u32[]{:S(2)}) copy-start(f32[384,768]{1,0:T(8,128)S(1)} %get-tuple-element.84) | copy-start | bytes 3538948
  124.1 12.1 %slice-start.1 = ((s8[4718592]{0:T(1024)(128)(4,1)}), s8[524288]{0:T(1024)(128)(4,1)S(1)}, s32[]{:S(2)}) async-start(s8[4718592]{0:T(1024)(128)(4,1)} %bitcast.85), calls=%async_computation.1 | async-start | bytes 1048576
  124.1 12.1 %copy-start.32 = (f32[768]{0:T(1024)S(1)}, f32[768]{0:T(1024)}, u32[]{:S(2)}) copy-start(f32[768]{0:T(1024)} %param.28) | copy-start | bytes 9220
  136.1 2.3 copy-start.34
  136.2 3.6 %copy-start.24 = (f32[768]{0:T(1024)S(1)}, f32[768]{0:T(1024)}, u32[]{:S(2)}) copy-start(f32[768]{0:T(1024)} %param.29) | copy-start | bytes 9220
  136.2 3.6 %copy-start.25 = (f32[768]{0:T(1024)S(1)}, f32[768]{0:T(1024)}, u32[]{:S(2)}) copy-start(f32[768]{0:T(1024)} %param.30) | copy-start | bytes 9220
  141.7 3.9 %copy-start.16 = (f32[384,768]{1,0:T(8,128)}, f32[384,768]{1,0:T(8,128)S(1)}, u32[]{:S(2)}) copy-start(f32[384,768]{1,0:T(8,128)S(1)} %get-tuple-element.64) | copy-start | bytes 3538948
  145.5 2.4 copy-start.36
  149.5 5.7 %copy-start.23 = (f32[8192]{0:T(1024)}, f32[8192]{0:T(1024)S(1)}, u32[]{:S(2)}) copy-start(f32[8192]{0:T(1024)S(1)} %constant_dynamic-update-slice_fusion) | copy-start | bytes 98308
  152.7 2.6 copy-start.13
  155.3 6.4 %copy-start.17 = (f32[384,768]{1,0:T(8,128)S(1)}, f32[384,768]{1,0:T(8,128)}, u32[]{:S(2)}) copy-start(f32[384,768]{1,0:T(8,128)} %copy-done.16) | copy-start | bytes 3538948
  155.3 6.4 %copy-start.35 = (bf16[384,3072]{1,0:T(8,128)(2,1)S(1)}, bf16[384,3072]{1,0:T(8,128)(2,1)}, u32[]{:S(2)}) copy-start(bf16[384,3072]{1,0:T(8,128)(2,1)} %copy-done.34) | copy-start | bytes 7077892
  161.7 4.5 %copy-start.11 = (f32[384,768]{1,0:T(8,128)S(1)}, f32[384,768]{1,0:T(8,128)}, u32[]{:S(2)}) copy-start(f32[384,768]{1,0:T(8,128)} %get-tuple-element.66.d_first) | copy-start | bytes 3538948
  327.1 4.4 %copy-start.22 = (f32[64,128]{1,0:T(8,128)S(1)}, f32[64,128]{1,0:T(8,128)}, u32[]{:S(2)}) copy-start(f32[64,128]{1,0:T(8,128)} %get-tuple-element.52) | copy-start | bytes 98308
  327.1 8.4 %copy-start.14 = (bf16[6,256,768]{2,1,0:T(8,128)(2,1)S(1)}, bf16[6,256,768]{2,1,0:T(8,128)(2,1)}, u32[]{:S(2)}) copy-start(bf16[6,256,768]{2,1,0:T(8,128)(2,1)} %get-tuple-element.111) | copy-start | bytes 7077892
  335.5 1.4 copy-start.21
  335.5 2.1 copy-start.19
  335.5 2.8 copy-start.18

commit v3 on v2

--- a/solution.py
+++ b/solution.py
@@ -307,39 +307,51 @@
     def __init__(self, send, recv):
         self.send, self.recv, self.open = send, recv, []
 
-    def make(self, i, src, dst, device):
+    def make(self, i, src, dst, device, sent=None):
         return pltpu.make_async_remote_copy(
             src_ref=src,
             dst_ref=dst,
-            send_sem=self.send.at[i],
+            send_sem=self.send.at[i if sent is None else sent],
             recv_sem=self.recv.at[i],
             device_id=device,
             device_id_type=MESH,
         )
 
-    def start(self, i, parts, when=None):
+    def start(self, i, parts, when=None, sent=None):
+        number = (lambda: i) if not callable(i) else i
+
+        def go(wait):
+            copy = self.make(number(), *parts(), sent=sent)
+            copy.wait_send() if wait else copy.start()
+
+        self.run(go, when, False)
+        self.open.append((go, when))
+
+    def run(self, go, when, wait):
         if when is None:
-            self.make(i, *parts()).start()
+            go(wait)
         else:
 
             @pl.when(when())
             def _():
-                self.make(i, *parts()).start()
-
-        self.open.append((i, parts, when))
+                go(wait)
 
     def arrived(self, i, dst, device):
         self.make(i, dst, dst, device).wait_recv()
 
-    def sent(self):
-        for i, parts, when in self.open:
-            if when is None:
-                self.make(i, *parts()).wait_send()
-            else:
-
-                @pl.when(when())
-                def _():
-                    self.make(i, *parts()).wait_send()
+    def all_sent(self):
+        for go, when in self.open:
+            self.run(go, when, True)
+
+
+def line_order(z, i):
+    if i == 0:
+        return z
+    if i == 1:
+        return jnp.where(z == 0, 1, z - 1)
+    if i == 2:
+        return jnp.where(z == 0, 2, jnp.where(z == 3, 1, z + 1))
+    return jnp.where(z < 2, 3, 0)
 
 
 def forward_kernel(
@@ -359,8 +371,7 @@
     kv_out,
     wh_out,
     o_full,
-    i_full,
-    b_full,
+    w_full,
     bu_full,
     lse,
     ctx_t,
@@ -389,54 +400,41 @@
     wr = w_i.shape[0]
     units = w_i.shape[1]
     row = d * nc + c
+    row_x, row_y, row_d = row ^ 4, row ^ 2, row ^ 6
     rc = Copies(send, recv)
     at_c = lambda k: (d, c ^ k, z)
     at_x = (1 - d, c, z)
-    at_xz = lambda kd, kt: (d ^ kd, c, z ^ kt)
+    to_c = lambda k: (lambda: at_c(k))
+    to_x = lambda: at_x
+    at_z = lambda k: (d, c, z ^ k)
     across = (d, z, c)
-    pairs = [(kd, kt) for kd in range(2) for kt in range(4) if kd or kt]
-
-    barrier = pltpu.get_barrier_semaphore()
-    everyone = [at_c(k) for k in (1, 2, 3)] + [at_xz(*p) for p in pairs]
-    for device in everyone:
-        pl.semaphore_signal(barrier, inc=1, device_id=device, device_id_type=MESH)
-
-    @pl.when(c != z)
-    def _():
-        pl.semaphore_signal(barrier, inc=1, device_id=across, device_id_type=MESH)
-
-    pl.semaphore_wait(barrier, len(everyone) + jnp.where(c != z, 1, 0))
-
-    number = iter(range(100))
-    locals_ = []
+    order = [line_order(z, i) for i in range(4)]
+    number = iter(range(0, 400))
+    four = lambda: [next(number) for _ in range(4)][0]
+    local_number = iter(range(32))
 
     def copy_here(src, dst):
-        copy = pltpu.make_async_copy(src, dst, local.at[len(locals_)])
+        copy = pltpu.make_async_copy(src, dst, local.at[next(local_number)])
         copy.start()
-        locals_.append(copy)
         return copy
 
-    n_ty, n_tc, n_tf = next(number), next(number), next(number)
+    t_cols = lambda t: pl.ds(pl.multiple_of(t * units, 128), units)
+    w_at = lambda r, t: w_full.at[:, r, :, t_cols(t)]
+    o_at = lambda r, t: o_full.at[t, r]
+    wh_at = lambda r: wh.at[pl.ds(pl.multiple_of(r * wr, wr), wr)]
     tok_at = lambda i: x2.at[pl.ds(2 * i, 2)]
-    rc.start(n_ty, lambda: (tok2, tok_at(c), at_c(2)))
-    n_wa, n_ba = next(number), next(number)
-    wh_at = lambda r: wh.at[pl.ds(pl.multiple_of(r * wr, wr), wr)]
-
-    def across_copies():
-        return (
-            rc.make(n_wa, w_head, wh_at(row), across),
-            rc.make(n_ba, b_head, bh, across),
-        )
-
-    @pl.when(c != z)
-    def _():
-        for copy in across_copies():
-            copy.start()
-
+    w_here = [
+        copy_here(w_i, w_full.at[0, row, :, t_cols(z)]),
+        copy_here(w_b, w_full.at[1, row, :, t_cols(z)]),
+        copy_here(w_o, o_at(row, z)),
+    ]
     mine = copy_here(tok2, tok_at(c))
+    seg_here = copy_here(seg2, seg.at[c])
+    bu_here = copy_here(b_unit, bu_full.at[z])
+    here_sem = [local.at[next(local_number)] for _ in range(2)]
     here = [
-        pltpu.make_async_copy(w_head, wh_at(row), local.at[30]),
-        pltpu.make_async_copy(b_head, bh, local.at[31]),
+        pltpu.make_async_copy(w_head, wh_at(row), here_sem[0]),
+        pltpu.make_async_copy(b_head, bh, here_sem[1]),
     ]
 
     @pl.when(c == z)
@@ -444,59 +442,159 @@
         for copy in here:
             copy.start()
 
-    rc.start(n_tc, lambda: (tok2, tok_at(c), at_c(1)))
-    n_seg = [next(number) for _ in range(3)]
-    for k in (1, 2, 3):
-        rc.start(n_seg[k - 1], lambda k=k: (seg2, seg.at[c], at_c(k)))
-    seg_here = copy_here(seg2, seg.at[c])
-    bu_here = copy_here(b_unit, bu_full.at[z])
-    i_at = lambda r, t: i_full.at[r, :, pl.ds(pl.multiple_of(t * units, 128), units)]
-    b_at = lambda r, t: b_full.at[r, :, pl.ds(pl.multiple_of(t * units, 128), units)]
-    o_at = lambda r, t: o_full.at[t, r]
-    w_here = [
-        copy_here(w_o, o_at(row, z)),
-        copy_here(w_i, i_at(row, z)),
-        copy_here(w_b, b_at(row, z)),
-    ]
-
-    row_w = d * nc + z
+    barrier = pltpu.get_barrier_semaphore()
+    everyone = [at_c(k) for k in (1, 2, 3)] + [at_z(k) for k in (1, 2, 3)] + [at_x]
+    for device in everyone:
+        pl.semaphore_signal(barrier, inc=1, device_id=device, device_id_type=MESH)
 
     @pl.when(c != z)
     def _():
-        for copy in across_copies():
-            copy.wait_recv()
+        pl.semaphore_signal(barrier, inc=1, device_id=across, device_id_type=MESH)
+
+    pl.semaphore_wait(barrier, len(everyone) + jnp.where(c != z, 1, 0))
+
+    n_ty, n_tc, n_tf, n_wa, n_ba = (next(number) for _ in range(5))
+    rc.start(n_ty, lambda: (tok2, tok_at(c), at_c(2)))
+    not_here = lambda: c != z
+    rc.start(n_wa, lambda: (w_head, wh_at(row), across), not_here)
+    rc.start(n_ba, lambda: (b_head, bh, across), not_here)
+    rc.start(n_tc, lambda: (tok2, tok_at(c), at_c(1)))
+    n_seg = four()
+    for k in (1, 2, 3):
+        rc.start(n_seg + k, lambda k=k: (seg2, seg.at[c], at_c(k)))
+
+    class Line:
+        def __init__(self, at):
+            self.at = at
+            self.n = [next(number) for _ in range(5)][0]
+
+        def begin(self):
+            own_ = lambda: self.at(z)
+            rc.start(
+                lambda: self.n + z,
+                lambda: (own_(), own_(), (d, c, z + 1)),
+                lambda: z < 3,
+                self.n + 3,
+            )
+            rc.start(
+                lambda: self.n + z,
+                lambda: (own_(), own_(), (d, c, z - 1)),
+                lambda: z > 0,
+                self.n + 4,
+            )
+
+        def step(self, i):
+            t = lambda: order[i]
+            rc.arrived(self.n + t(), self.at(t()), (d, c, z))
+            rc.start(
+                lambda: self.n + t(),
+                lambda: (
+                    self.at(t()),
+                    self.at(t()),
+                    (d, c, jnp.where(t() < z, z + 1, z - 1)),
+                ),
+                lambda: jnp.where(t() < z, z < 3, z > 0),
+                self.n + i - 1,
+            )
+
+    head_line = Line(lambda t: wh_at(d * nc + t))
+    lines = (Line(lambda t: w_at(row, t)), Line(lambda t: o_at(row, t)))
+    full_at = (w_at, o_at)
+    n_hx = four()
+    n_x, n_y, n_d = ([four(), four()] for _ in range(3))
+    n_c = [[four(), four()] for _ in range(4)]
+
+    def pass_on(n, i, r, device):
+        t = lambda: order[i]
+        for w in range(2):
+            rc.start(
+                lambda w=w: n[w] + t(),
+                lambda w=w: (full_at[w](r, t()), full_at[w](r, t()), device()),
+                None,
+                n[w] + i,
+            )
+
+    def came(n, i, r, device):
+        t = order[i]
+        for w in range(2):
+            rc.arrived(n[w] + t, full_at[w](r, t), device)
+
+    def head_x(i):
+        t = lambda: order[i]
+        at = lambda: wh_at(d * nc + t())
+        rc.start(lambda: n_hx + t(), lambda: (at(), at(), at_x), None, n_hx + i)
+
+    def dense_step(i, chips):
+        for line in lines:
+            line.step(i)
+        pass_on(n_x, i, row, to_x)
+        if chips:
+            dense_y(i)
+
+    def dense_y(i):
+        pass_on(n_y, i, row, to_c(2))
+        pass_on(n_c[0], i, row, to_c(1))
+
+    def from_x(i):
+        came(n_x, i, row_x, at_x)
+        if i >= 3:
+            pass_on(n_d, i, row_x, to_c(2))
+        pass_on(n_c[1], i, row_x, to_c(1))
+
+    def from_y(i):
+        came(n_y, i, row_y, at_c(2))
+        if i < 3:
+            pass_on(n_d, i, row_y, to_x)
+        pass_on(n_c[2], i, row_y, to_c(1))
+
+    def from_corner(i):
+        came(n_d, i, row_d, at_x)
+        pass_on(n_c[3], i, row_d, to_c(1))
+
+    for copy in w_here:
+        copy.wait()
+    for line in lines:
+        line.begin()
+    pass_on(n_x, 0, row, to_x)
+    pass_on(n_y, 0, row, to_c(2))
+    pass_on(n_c[0], 0, row, to_c(1))
+    n_bu = four()
+    for k in (1, 2, 3):
+        rc.start(n_bu + k, lambda k=k: (b_unit, bu_full.at[z], at_z(k)))
+
+    @pl.when(c != z)
+    def _():
+        rc.arrived(n_wa, wh_at(d * nc + z), across)
+        rc.arrived(n_ba, bh, across)
 
     @pl.when(c == z)
     def _():
         for copy in here:
             copy.wait()
 
-    n_wx = [next(number) for _ in pairs]
-    for i, p in zip(n_wx, pairs):
-        rc.start(i, lambda p=p: (wh_at(row_w), wh_at(row_w), at_xz(*p)))
-
-    n_bu = [next(number) for _ in range(3)]
-    n_z = [[next(number) for _ in range(3)] for _ in range(3)]
-    full_at = (o_at, i_at, b_at)
+    head_line.begin()
+    head_x(0)
+    q_scr[...] = jnp.zeros_like(q_scr)
+    head_line.step(1)
+    head_x(1)
+    dense_step(1, True)
+    head_line.step(2)
+    head_x(2)
+    head_line.step(3)
+    head_x(3)
     for k in (1, 2, 3):
-        rc.start(n_bu[k - 1], lambda k=k: (b_unit, bu_full.at[z], at_xz(0, k)))
-    for w, src in enumerate((w_o, w_i, w_b)):
-        for k in (1, 2, 3):
-            rc.start(n_z[w][k - 1], lambda k=k, w=w, src=src: (src, full_at[w](row, z), at_xz(0, k)))
-
-    rc.arrived(n_ty, tok_at(c ^ 2), at_c(2))
-    rc.start(n_tf, lambda: (tok_at(c ^ 2), tok_at(c ^ 2), at_c(1)))
-    for k in (1, 2, 3):
-        rc.arrived(n_seg[k - 1], seg.at[c ^ k], at_c(k))
+        rc.arrived(n_seg + k, seg.at[c ^ k], at_c(k))
     seg_here.wait()
-    q_scr[...] = jnp.zeros_like(q_scr)
     for i in range(nc):
         for s in range(2):
             line = seg[i, s : s + 1, :].astype(F32)
             segr[2 * i + s, 0:1, :] = line
             segc[2 * i + s] = jnp.broadcast_to(line, (128, ln)).T
-    for i, (kd, kt) in zip(n_wx, pairs):
-        rc.arrived(i, wh_at((d ^ kd) * nc + (z ^ kt)), at_xz(kd, kt))
+    rc.arrived(n_ty, tok_at(c ^ 2), at_c(2))
+    rc.start(n_tf, lambda: (tok_at(c ^ 2), tok_at(c ^ 2), at_c(1)))
+    dense_step(2, True)
+    for t in range(4):
+        rc.arrived(n_hx + t, wh_at((1 - d) * nc + t), at_x)
     mine.wait()
     rc.arrived(n_tc, tok_at(c ^ 1), at_c(1))
     rc.arrived(n_tf, tok_at(c ^ 3), at_c(1))
@@ -517,6 +615,8 @@
     x_here = copy_here(xt, xt_out)
     q_here = copy_here(q_scr, q_out)
     kv_here = copy_here(kv, kv_out)
+    dense_step(3, True)
+    from_x(0)
 
     @pl.loop(0, nc)
     def _(j):
@@ -527,48 +627,7 @@
                     rows, 128 * h : 128 * h + 128
                 ].T
 
-    groups = ((0, 1), (2,))
-    row_at = (lambda r: o_full.at[:, r], lambda r: i_full.at[r], lambda r: b_full.at[r])
-    hw = wr // 2
-    low_at = (
-        lambda r: o_full.at[:, r, pl.ds(0, hw)],
-        lambda r: i_full.at[r, pl.ds(0, hw)],
-        lambda r: b_full.at[r, pl.ds(0, hw)],
-    )
-    high_at = (
-        lambda r: o_full.at[:, r, pl.ds(hw, hw)],
-        lambda r: i_full.at[r, pl.ds(hw, hw)],
-        lambda r: b_full.at[r, pl.ds(hw, hw)],
-    )
-    n_x, n_y, n_d1, n_d2 = ([next(number) for _ in range(3)] for _ in range(4))
-    n_c = [[next(number) for _ in range(4)] for _ in range(3)]
-
-    def stage_plane(w):
-        w_here[w].wait()
-        for k in (1, 2, 3):
-            rc.arrived(n_z[w][k - 1], full_at[w](row, z ^ k), at_xz(0, k))
-        rc.start(n_x[w], lambda w=w: (row_at[w](row), row_at[w](row), at_x))
-        rc.start(n_y[w], lambda w=w: (row_at[w](row), row_at[w](row), at_c(2)))
-        rc.start(n_c[w][0], lambda w=w: (row_at[w](row), row_at[w](row), at_c(1)))
-
-    row_x, row_y, row_d = row ^ 4, row ^ 2, row ^ 6
-
-    def stage_corner(w):
-        rc.arrived(n_x[w], row_at[w](row_x), at_x)
-        rc.start(n_d1[w], lambda w=w: (low_at[w](row_x), low_at[w](row_x), at_c(2)))
-        rc.start(n_c[w][1], lambda w=w: (row_at[w](row_x), row_at[w](row_x), at_c(1)))
-        rc.arrived(n_y[w], row_at[w](row_y), at_c(2))
-        rc.start(n_d2[w], lambda w=w: (high_at[w](row_y), high_at[w](row_y), at_x))
-        rc.start(n_c[w][2], lambda w=w: (row_at[w](row_y), row_at[w](row_y), at_c(1)))
-
-    def stage_core(w):
-        rc.arrived(n_d1[w], low_at[w](row_d), at_c(2))
-        rc.arrived(n_d2[w], high_at[w](row_d), at_x)
-        rc.start(n_c[w][3], lambda w=w: (row_at[w](row_d), row_at[w](row_d), at_c(1)))
-
-    def stage_end(w):
-        for i, r in zip(n_c[w], (row, row_x, row_y, row_d)):
-            rc.arrived(i, row_at[w](r ^ 1), at_c(1))
+    from_x(1)
 
     def block(qb):
         r0, r1, o0, o1, seq = block_rows(qb, half, ln)
@@ -626,44 +685,40 @@
         context[pl.ds(o0, hl), :] = turned[:hl]
         context[pl.ds(o1, hl), :] = turned[hl:]
 
-    stage_plane(0)
-    stage_plane(1)
-
     @pl.loop(0, 6)
     def _(qb):
         block(qb)
 
         @pl.when(qb == 1)
         def _():
-            stage_plane(2)
+            from_y(0)
 
         @pl.when(qb == 3)
         def _():
-            stage_corner(0)
-            stage_corner(1)
-
-    n_ctx = [next(number) for _ in range(3)]
+            from_x(2)
+            from_y(1)
+
+    n_ctx = four()
     ctx_at = lambda i: context.at[pl.ds(pl.multiple_of(i * own, 128), own)]
     for k in (1, 2, 3):
-        rc.start(n_ctx[k - 1], lambda k=k: (ctx_at(c ^ k), ctx_all.at[c], at_c(k)))
+        rc.start(n_ctx + k, lambda k=k: (ctx_at(c ^ k), ctx_all.at[c], at_c(k)))
     ctx_here = copy_here(ctx_at(c), ctx_all.at[c])
-    stage_corner(2)
-    stage_core(0)
-    stage_core(1)
+    from_x(3)
+    from_y(2)
+    from_corner(0)
+    from_corner(1)
     for k in (1, 2, 3):
-        rc.arrived(n_ctx[k - 1], ctx_all.at[c ^ k], at_c(k))
-        rc.arrived(n_bu[k - 1], bu_full.at[z ^ k], at_xz(0, k))
-    stage_core(2)
-    for w in range(3):
-        stage_end(w)
+        rc.arrived(n_ctx + k, ctx_all.at[c ^ k], at_c(k))
+        rc.arrived(n_bu + k, bu_full.at[z ^ k], at_z(k))
+    from_y(3)
+    from_corner(2)
+    from_corner(3)
+    for n, r in zip(n_c, (row, row_x, row_y, row_d)):
+        for i in range(4):
+            came(n, i, r ^ 1, at_c(1))
     for copy in (bu_here, x_here, wh_here, q_here, kv_here, ctx_here):
         copy.wait()
-    rc.sent()
-
-    @pl.when(c != z)
-    def _():
-        for copy in across_copies():
-            copy.wait_send()
+    rc.all_sent()
 
 
 def forward(tok2, seg2, w_head, b_head, b_unit, w_o, w_i, w_b, heads):
@@ -684,15 +739,14 @@
             sds((2 * nc * ln, heads * 128), BF),
             sds((nr * wr, 3 * group), BF),
             sds((nt, nr, wr, group), BF),
-            sds((nr, wr, nt * units), BF),
-            sds((nr, wr, nt * units), BF),
+            sds((2, nr, wr, nt * units), BF),
             sds((nt, 8, units), F32),
             sds((8, rows), F32),
             sds((group, rows), F32),
             sds((nc, 8, ln), jnp.int32),
         ),
         in_specs=[hb] * 8,
-        out_specs=(hb,) * 9 + (vm,) * 3,
+        out_specs=(hb,) * 8 + (vm,) * 3,
         scratch_shapes=[
             pltpu.VMEM((2 * nc, ln, width), BF),
             pltpu.VMEM((width, 2 * nc * ln), BF),
@@ -706,8 +760,8 @@
             pltpu.VMEM((2 * nc, ln, 128), F32),
             pltpu.VMEM((2 * nc, 8, ln), F32),
             pltpu.VMEM((rows, group), BF),
-            pltpu.SemaphoreType.DMA((80,)),
-            pltpu.SemaphoreType.DMA((80,)),
+            pltpu.SemaphoreType.DMA((120,)),
+            pltpu.SemaphoreType.DMA((120,)),
             pltpu.SemaphoreType.DMA((32,)),
         ],
         compiler_params=pltpu.CompilerParams(
@@ -1045,8 +1099,6 @@
 
     q_here.wait()
     w_core_add(1)
-    w_core_add(2)
-    small_step(1)
 
     def block(qb):
         r0, r1, o0, o1, seq = block_rows(qb, half, ln)
@@ -1148,12 +1200,13 @@
 
     n_h = [next(number) for _ in range(8)]
 
-    def h_partial():
-        @pl.loop(0, 2 * nc)
+    def h_partial(seq):
+        @pl.loop(0, nc)
         def _(i):
-            rows = pl.ds(pl.multiple_of(i * ln, ln), ln)
+            rows = pl.ds(pl.multiple_of((2 * i + seq) * ln, ln), ln)
             acc_h[...] += dot_nn(xt[:, rows], d_proj[rows, :])
 
+    def h_send():
         o_h[...] = acc_h[...].astype(BF)
         rows_x = lambda x_: pl.ds(pl.multiple_of(x_ * 4 * wr, wr), 4 * wr)
         rc.start(n_h[0], lambda: (o_h.at[rows_x(1 - d)], x_h, at_x))
@@ -1202,62 +1255,72 @@
             bias_fin[...] = bias_sum[...]
 
     wh_here.wait()
+    xt_here.wait()
+    acc_h[...] = jnp.zeros_like(acc_h)
 
     @pl.loop(0, 6)
     def _(i):
         block(jnp.where(i < 2, i + 4, i - 2))
 
+        @pl.when(i == 0)
+        def _():
+            w_core_add(2)
+
         @pl.when(i == 1)
         def _():
             t_partial(1)
-            w_plane(0)
+            h_partial(1)
+            small_step(1)
             for line in out_lines:
                 line.step(1)
-            small_step(2)
+
+        @pl.when(i == 2)
+        def _():
+            w_plane(0)
             t_core(1)
 
         @pl.when(i == 3)
         def _():
-            w_plane(1)
-            w_plane(2)
+            small_step(2)
+
+        @pl.when(i == 4)
+        def _():
+            w_corner(0)
             small_step(3)
             for line in out_lines:
                 line.step(2)
-            t_shared()
-
-        @pl.when(i == 4)
-        def _():
-            w_corner(0)
-            small_step(4)
-            t_shared_end()
 
     t_partial(0)
+    h_partial(0)
+    h_send()
+    bias_send(0)
     t_core(0)
-    bias_send(0)
-    acc_h[...] = jnp.zeros_like(acc_h)
-    xt_here.wait()
-    h_partial()
-    w_corner(1)
-    w_corner(2)
+    t_shared()
+    w_plane(1)
+    small_step(4)
     t_whole(0)
     t_whole(1)
-    for line in out_lines:
-        line.step(3)
-    tok_lines[2].step(1)
+    w_plane(2)
+    t_shared_end()
+    bias_step(0)
     h_plane()
-    bias_step(0)
     w_line(0)
     tok_lines[0].step(1)
     tok_lines[1].step(1)
+    tok_lines[2].step(1)
+    w_corner(1)
+    bias_step(1)
+    w_corner(2)
+    tok_lines[0].step(2)
+    tok_lines[1].step(2)
     tok_lines[2].step(2)
+    h_line()
+    bias_step(2)
     w_line(1)
     w_line(2)
-    bias_step(1)
-    h_line()
-    tok_lines[0].step(2)
-    tok_lines[1].step(2)
-    bias_step(2)
     h_end()
+    for line in out_lines:
+        line.step(3)
     w_end(0)
     w_end(1)
     w_end(2)
@@ -1279,7 +1342,7 @@
 
     for copy in out_here + tok_here:
         copy.wait()
-    rc.sent()
+    rc.all_sent()
 
 
 def backward(d_ctx, g_b, g_i, g_o, out_low, d_first, small, q, kv, xt, wh, lse, ctx_t, seg, heads, seqs):
@@ -1410,8 +1473,7 @@
         kv,
         wh,
         o_full,
-        gather(w_i),
-        gather(w_b),
+        jnp.stack([gather(w_i), gather(w_b)]),
         b_all,
         lse,
         ctx_t,
@@ -1550,10 +1612,10 @@
     b_unit = jnp.broadcast_to(in_bias[None], (8, units))
     args = (tok2, seg2, w_head, b_head, b_unit, w_out, w_in, w_back, heads)
     got = forward(*args) if sizes == (2, 4, 4) else forward_plain(sizes, me, *args)
-    ctx_all, xt, q, kv, wh, w_o, w_i, w_b, b_in, lse, ctx_t, seg_all = got
+    ctx_all, xt, q, kv, wh, w_o, w_ib, b_in, lse, ctx_t, seg_all = got
     w_o = w_o.reshape(nt, width, group)
-    w_i = w_i.reshape(width, nt * units)
-    w_b = w_b.reshape(width, nt * units)
+    w_ib = w_ib.reshape(2, width, nt * units)
+    w_i, w_b = w_ib[0], w_ib[1]
     b_in = b_in[:, 0].reshape(nt * units)
     own = ln + hl
 

time: 344 us -> 327 us (0.951)
  Pallas kernels: 262 us -> 236 us
  local copies, waits for them, and re-layouts: 28.8 us -> 37.8 us
    pallas_call x1, Pallas kernels: 106 us -> 87.5 us  [forward(): pl.pallas_call(functools.partial(forward_kernel, heads, ln), out_shape=(s...]
    slice x0 -> x1, local copies, waits for them, and re-layouts: none -> 8.77 us  [per_device(): w_i, w_b = (w_ib[0], w_ib[1])]
    pallas_call x1, Pallas kernels: 156 us -> 149 us  [backward(): pl.pallas_call(functools.partial(backward_kernel, heads, ln), out_shape=(...]
    unnamed x91 -> x93, local copies, waits for them, and re-layouts: 12.6 us -> 12.6 us
where the time goes in v3:
time: 327 us; the launch traced here: 321 us
  Pallas kernels  236 us (72%)
  local copies, waits for them, and re-layouts  37.8 us (12%)
  matrix products  36.4 us (11%)
  other arithmetic  9.24 us (3%)
    pallas_call x1, Pallas kernels, backward(): pl.pallas_call(functools.partial(backward_kernel, heads, ln), out_shape=(...  149 us
    pallas_call x1, Pallas kernels, forward(): pl.pallas_call(functools.partial(forward_kernel, heads, ln), out_shape=(s...  87.5 us
    unnamed x93, local copies, waits for them, and re-layouts  12.6 us
    dot_general x1, matrix products, per_device(): inner = jnp.dot(normed_low, w_i, preferred_element_type=F32) + b_in  12 us
    slice x1, local copies, waits for them, and re-layouts, per_device(): w_i, w_b = (w_ib[0], w_ib[1])  8.77 us

profile of v3, /device:TPU:0, one launch (start us, length us, event | category | flops | bytes accessed | tf_op | source)
XLA Modules:
  0.0 321.5 jit_solution(15651311223651204695)
XLA Ops:
  0.7 1.3 constant_dynamic-slice_fusion.3
  2.1 0.8 constant_dynamic-slice_fusion.1
  3.2 0.1 copy.67
  3.7 0.9 copy-done.6
  4.6 87.5 %forward.1 = (bf16[4,384,192]{2,1,0:T(8,128)(2,1)S(1)}, bf16[768,2048]{1,0:T(8,128)(2,1)S(1)}, bf16[2048,384]{1,0:T(8,128)(2,1)S(1)}, bf16[2048,384]{1,0:T(8,128...) custom-call(bf16[2,256,768]{2,1,0:T(8,128)(2,1)S(1)} %pad_maximum_fu, ...), custom_call_target="tpu_custom_call" | custom-call | tf_op jit(solution)/shard_map/forward/pallas_call | solution.py:733
  92.1 1.6 copy-done
  93.7 1.2 copy-done.1
  94.9 1.2 copy-done.2
  96.1 1.0 copy-done.3
  97.1 1.0 copy-done.4
  98.1 0.6 copy-done.7
  98.7 0.6 copy-done.9
  99.3 0.6 copy-done.10
  100.0 8.8 %fusion.41 = (bf16[1,8,96,3072]{3,2,1,0:T(8,128)(2,1)}, bf16[1,8,96,3072]{3,2,1,0:T(8,128)(2,1)}) fusion(bf16[2,8,96,3072]{3,2,1,0:T(8,128)(2,1)} %get-tuple-element.36), kind=kLoop, calls=%fused_computation.110 | loop fusion | bytes 18874368 | tf_op jit(solution)/shard_map/slice | solution.py:1618
  108.8 1.2 dynamic-slice_bitcast_fusion.1
  110.0 0.9 fusion.44
  110.9 0.3 multiply_reduce_fusion.3
  111.2 1.9 slice.88
  113.1 12.0 %fusion.2 = (bf16[384,3072]{1,0:T(8,128)(2,1)S(1)}, f32[384,3072]{1,0:T(8,128)S(1)}) fusion(f32[3072]{0:T(1024)S(1)} %bitcast.86, bf16[768,3072]{1,0:T(8,128)(2,1)S(1)} %bitcast.69, f32[384,768]{1,0:T(8,128)S(1)} %get-tuple-element.84, f32[768]{0:T(1024)S(1)} %copy-done.34, f32[768]{0:T(1024)S(1)} %copy-done.28, f32[384]{0:T(512)S(1)} %add_rsqrt_fusion.1, ...), kind=kOutput, calls=%fused_computation.6 | convolution fusion | flops 1891270656 | bytes 12997632 | tf_op jit(solution)/shard_map/dot_general | solution.py:1627
  125.2 2.2 fusion.45
  127.4 0.3 multiply_reduce_fusion.2
  127.7 1.0 dynamic-slice_bitcast_fusion
  128.8 1.5 fusion.25
  130.3 0.4 fusion.38
  130.7 3.8 %fusion.46 = (f32[3072]{0:T(1024)S(1)}, bf16[384,3072]{1,0:T(8,128)(2,1)S(1)}) fusion(f32[384,3072]{1,0:T(8,128)S(1)} %get-tuple-element.86, f32[3072]{0:T(1024)S(1)} %bitcast.87, bf16[768,3072]{1,0:T(8,128)(2,1)S(1)} %bitcast.74, f32[384,768]{1,0:T(8,128)S(1)} %get-tuple-element.62), kind=kOutput, calls=%fused_computation.115 | convolution fusion | flops 1826386944 | bytes 13000704 | tf_op jit(solution)/shard_map/dot_general | solution.py:1640
  134.6 2.4 multiply_reduce_fusion
  137.0 1.4 fusion.40
  138.5 3.1 fusion.18
  141.7 2.6 copy.57
  144.3 6.4 %convolution_convert_fusion = bf16[768,3072]{1,0:T(8,128)(2,1)} fusion(bf16[384,3072]{1,0:T(8,128)(2,1)} %copy-done.37, f32[384,768]{1,0:T(8,128)S(1)} %copy-done.13, f32[768]{0:T(1024)S(1)} %copy-done.34, f32[768]{0:T(1024)S(1)} %copy-done.28, f32[384]{0:T(512)S(1)} %add_rsqrt_fusion.1, f32[384]{0:T(512)S(1)} %broadcast_multiply_fusion.5), kind=kOutput, calls=%fused_computation.2 | convolution fusion | flops 1815773184 | bytes 8266752 | tf_op jit(solution)/shard_map/td,tf->df/dot_general | solution.py:1644
  150.7 4.5 %convolution_convert_fusion.1 = bf16[768,3072]{1,0:T(8,128)(2,1)} fusion(bf16[384,3072]{1,0:T(8,128)(2,1)S(1)} %copy-done.36, f32[384,768]{1,0:T(8,128)S(1)} %copy-done.19), kind=kOutput, calls=%fused_computation.3 | convolution fusion | flops 1814593536 | bytes 8257536 | tf_op jit(solution)/shard_map/td,tf->df/dot_general | solution.py:1639
  155.2 1.0 convolution_convert_fusion.3
  156.2 1.2 copy.55
  157.4 148.8 %backward.1 = (bf16[6,256,768]{2,1,0:T(8,128)(2,1)}, bf16[6,256,768]{2,1,0:T(8,128)(2,1)}, f32[96,768]{1,0:T(8,128)}, f32[96,768]{1,0:T(8,128)}, f32[96,192]{1,0...) custom-call(bf16[4,384,192]{2,1,0:T(8,128)(2,1)} %bitcast.77, ...), custom_call_target="tpu_custom_call" | custom-call | tf_op jit(solution)/shard_map/backward/pallas_call | solution.py:1361
  306.2 0.9 slice.91
  307.2 0.1 copy.58
  307.5 0.9 slice_bitcast_fusion
  308.4 0.7 pad_maximum_fusion.2
  309.1 4.4 %convert_element_type.58 = f32[6,256,768]{2,1,0:T(8,128)} convert(bf16[6,256,768]{2,1,0:T(8,128)(2,1)} %get-tuple-element.46) | non-fusion elementwise | flops 1179648 | bytes 7077888 | tf_op jit(solution)/shard_map/convert_element_type | solution.py:1675
  313.6 0.6 dynamic-slice_reduce_fusion
  314.2 0.6 slice_bitcast_fusion.2
  314.8 0.7 slice_reduce_fusion.1
  315.6 0.6 reshape_squeeze.11
  316.3 1.3 slice.94
  317.6 1.4 copy.80
  319.0 0.6 copy.81
  319.6 0.7 copy.82
  320.3 0.7 copy.83
  (110 shorter events, 1.2 us)
Async XLA Ops:
  0.6 2.4 copy-start.22
  0.7 2.8 copy-start.30
  0.7 3.0 copy-start.31
  0.7 3.0 copy-start.29
  0.7 3.0 copy-start.8
  0.7 3.0 copy-start.5
  2.0 1.7 copy-start.16
  3.7 0.9 copy-start.6
  92.1 1.6 copy-start
  93.7 1.2 copy-start.1
  94.9 1.2 copy-start.2
  96.1 1.0 copy-start.3
  97.1 1.0 copy-start.4
  98.1 0.6 copy-start.7
  98.7 0.6 copy-start.9
  99.3 0.6 copy-start.10
  100.0 9.9 %copy-start.17 = (bf16[1,256,768]{2,1,0:T(8,128)(2,1)S(1)}, bf16[1,256,768]{2,1,0:T(8,128)(2,1)}, u32[]{:S(2)}) copy-start(bf16[1,256,768]{2,1,0:T(8,128)(2,1)} %copy-done.16) | copy-start | bytes 1179652
  100.0 9.9 %copy-start.32 = (f32[768]{0:T(1024)S(1)}, f32[768]{0:T(1024)}, u32[]{:S(2)}) copy-start(f32[768]{0:T(1024)} %param.22) | copy-start | bytes 9220
  108.8 4.3 %copy-start.28 = (f32[768]{0:T(1024)S(1)}, f32[768]{0:T(1024)}, u32[]{:S(2)}) copy-start(f32[768]{0:T(1024)} %param.23) | copy-start | bytes 9220
  108.8 4.3 %copy-start.34 = (f32[768]{0:T(1024)S(1)}, f32[768]{0:T(1024)}, u32[]{:S(2)}) copy-start(f32[768]{0:T(1024)} %param.24) | copy-start | bytes 9220
  109.9 3.2 copy-start.14
  109.9 15.2 %slice-start = ((s8[4718592]{0:T(1024)(128)(4,1)}), s8[4194304]{0:T(1024)(128)(4,1)S(1)}, s32[]{:S(2)}) async-start(s8[4718592]{0:T(1024)(128)(4,1)} %bitcast.71), calls=%async_computation | async-start | bytes 8388608
  110.9 26.1 %copy-start.12 = (f32[384,768]{1,0:T(8,128)}, f32[384,768]{1,0:T(8,128)S(1)}, u32[]{:S(2)}) copy-start(f32[384,768]{1,0:T(8,128)S(1)} %get-tuple-element.84) | copy-start | bytes 3538948
  113.1 12.0 %slice-start.1 = ((s8[4718592]{0:T(1024)(128)(4,1)}), s8[524288]{0:T(1024)(128)(4,1)S(1)}, s32[]{:S(2)}) async-start(s8[4718592]{0:T(1024)(128)(4,1)} %bitcast.71), calls=%async_computation.1 | async-start | bytes 1048576
  113.1 12.0 %copy-start.33 = (f32[768]{0:T(1024)S(1)}, f32[768]{0:T(1024)}, u32[]{:S(2)}) copy-start(f32[768]{0:T(1024)} %param.28) | copy-start | bytes 9220
  125.1 2.3 copy-start.35
  125.2 3.6 %copy-start.26 = (f32[768]{0:T(1024)S(1)}, f32[768]{0:T(1024)}, u32[]{:S(2)}) copy-start(f32[768]{0:T(1024)} %param.29) | copy-start | bytes 9220
  125.2 3.6 %copy-start.27 = (f32[768]{0:T(1024)S(1)}, f32[768]{0:T(1024)}, u32[]{:S(2)}) copy-start(f32[768]{0:T(1024)} %param.30) | copy-start | bytes 9220
  130.7 3.9 %copy-start.18 = (f32[384,768]{1,0:T(8,128)}, f32[384,768]{1,0:T(8,128)S(1)}, u32[]{:S(2)}) copy-start(f32[384,768]{1,0:T(8,128)S(1)} %get-tuple-element.62) | copy-start | bytes 3538948
  134.5 2.4 copy-start.37
  138.5 5.8 %copy-start.25 = (f32[8192]{0:T(1024)}, f32[8192]{0:T(1024)S(1)}, u32[]{:S(2)}) copy-start(f32[8192]{0:T(1024)S(1)} %constant_dynamic-update-slice_fusion) | copy-start | bytes 98308
  141.7 2.6 copy-start.13
  144.3 6.4 %copy-start.19 = (f32[384,768]{1,0:T(8,128)S(1)}, f32[384,768]{1,0:T(8,128)}, u32[]{:S(2)}) copy-start(f32[384,768]{1,0:T(8,128)} %copy-done.18) | copy-start | bytes 3538948
  144.3 6.4 %copy-start.36 = (bf16[384,3072]{1,0:T(8,128)(2,1)S(1)}, bf16[384,3072]{1,0:T(8,128)(2,1)}, u32[]{:S(2)}) copy-start(bf16[384,3072]{1,0:T(8,128)(2,1)} %copy-done.35) | copy-start | bytes 7077892
  150.7 4.5 %copy-start.11 = (f32[384,768]{1,0:T(8,128)S(1)}, f32[384,768]{1,0:T(8,128)}, u32[]{:S(2)}) copy-start(f32[384,768]{1,0:T(8,128)} %get-tuple-element.64.d_first) | copy-start | bytes 3538948
  309.1 4.4 %copy-start.24 = (f32[64,128]{1,0:T(8,128)S(1)}, f32[64,128]{1,0:T(8,128)}, u32[]{:S(2)}) copy-start(f32[64,128]{1,0:T(8,128)} %get-tuple-element.50) | copy-start | bytes 98308
  309.1 8.4 %copy-start.15 = (bf16[6,256,768]{2,1,0:T(8,128)(2,1)S(1)}, bf16[6,256,768]{2,1,0:T(8,128)(2,1)}, u32[]{:S(2)}) copy-start(bf16[6,256,768]{2,1,0:T(8,128)(2,1)} %get-tuple-element.111) | copy-start | bytes 7077892
  317.5 1.4 copy-start.23
  317.6 2.1 copy-start.21
  317.6 2.8 copy-start.20

commit v4 on v3

--- a/solution.py
+++ b/solution.py
@@ -388,6 +388,8 @@
     segc,
     segr,
     context,
+    w_src,
+    o_src,
     send,
     recv,
     local,
@@ -423,11 +425,7 @@
     o_at = lambda r, t: o_full.at[t, r]
     wh_at = lambda r: wh.at[pl.ds(pl.multiple_of(r * wr, wr), wr)]
     tok_at = lambda i: x2.at[pl.ds(2 * i, 2)]
-    w_here = [
-        copy_here(w_i, w_full.at[0, row, :, t_cols(z)]),
-        copy_here(w_b, w_full.at[1, row, :, t_cols(z)]),
-        copy_here(w_o, o_at(row, z)),
-    ]
+    w_here = [copy_here(w_i, w_src.at[0]), copy_here(w_b, w_src.at[1]), copy_here(w_o, o_src)]
     mine = copy_here(tok2, tok_at(c))
     seg_here = copy_here(seg2, seg.at[c])
     bu_here = copy_here(b_unit, bu_full.at[z])
@@ -454,10 +452,10 @@
     pl.semaphore_wait(barrier, len(everyone) + jnp.where(c != z, 1, 0))
 
     n_ty, n_tc, n_tf, n_wa, n_ba = (next(number) for _ in range(5))
-    rc.start(n_ty, lambda: (tok2, tok_at(c), at_c(2)))
     not_here = lambda: c != z
     rc.start(n_wa, lambda: (w_head, wh_at(row), across), not_here)
     rc.start(n_ba, lambda: (b_head, bh, across), not_here)
+    rc.start(n_ty, lambda: (tok2, tok_at(c), at_c(2)))
     rc.start(n_tc, lambda: (tok2, tok_at(c), at_c(1)))
     n_seg = four()
     for k in (1, 2, 3):
@@ -468,17 +466,16 @@
             self.at = at
             self.n = [next(number) for _ in range(5)][0]
 
-        def begin(self):
-            own_ = lambda: self.at(z)
+        def begin(self, src):
             rc.start(
                 lambda: self.n + z,
-                lambda: (own_(), own_(), (d, c, z + 1)),
+                lambda: (src, self.at(z), (d, c, z + 1)),
                 lambda: z < 3,
                 self.n + 3,
             )
             rc.start(
                 lambda: self.n + z,
-                lambda: (own_(), own_(), (d, c, z - 1)),
+                lambda: (src, self.at(z), (d, c, z - 1)),
                 lambda: z > 0,
                 self.n + 4,
             )
@@ -497,19 +494,24 @@
                 self.n + i - 1,
             )
 
-    head_line = Line(lambda t: wh_at(d * nc + t))
+    n_hz = four()
     lines = (Line(lambda t: w_at(row, t)), Line(lambda t: o_at(row, t)))
     full_at = (w_at, o_at)
+    sources = (w_src, o_src)
     n_hx = four()
     n_x, n_y, n_d = ([four(), four()] for _ in range(3))
     n_c = [[four(), four()] for _ in range(4)]
 
-    def pass_on(n, i, r, device):
+    def pass_on(n, i, r, device, first=False):
         t = lambda: order[i]
         for w in range(2):
             rc.start(
                 lambda w=w: n[w] + t(),
-                lambda w=w: (full_at[w](r, t()), full_at[w](r, t()), device()),
+                lambda w=w: (
+                    sources[w] if first and i == 0 else full_at[w](r, t()),
+                    full_at[w](r, t()),
+                    device(),
+                ),
                 None,
                 n[w] + i,
             )
@@ -519,21 +521,16 @@
         for w in range(2):
             rc.arrived(n[w] + t, full_at[w](r, t), device)
 
-    def head_x(i):
-        t = lambda: order[i]
-        at = lambda: wh_at(d * nc + t())
-        rc.start(lambda: n_hx + t(), lambda: (at(), at(), at_x), None, n_hx + i)
-
     def dense_step(i, chips):
         for line in lines:
             line.step(i)
-        pass_on(n_x, i, row, to_x)
+        pass_on(n_x, i, row, to_x, True)
         if chips:
             dense_y(i)
 
     def dense_y(i):
-        pass_on(n_y, i, row, to_c(2))
-        pass_on(n_c[0], i, row, to_c(1))
+        pass_on(n_y, i, row, to_c(2), True)
+        pass_on(n_c[0], i, row, to_c(1), True)
 
     def from_x(i):
         came(n_x, i, row_x, at_x)
@@ -553,11 +550,10 @@
 
     for copy in w_here:
         copy.wait()
-    for line in lines:
-        line.begin()
-    pass_on(n_x, 0, row, to_x)
-    pass_on(n_y, 0, row, to_c(2))
-    pass_on(n_c[0], 0, row, to_c(1))
+    pass_on(n_x, 0, row, to_x, True)
+    pass_on(n_y, 0, row, to_c(2), True)
+    pass_on(n_c[0], 0, row, to_c(1), True)
+    own_here = [copy_here(w_src, w_at(row, z)), copy_here(o_src, o_at(row, z))]
     n_bu = four()
     for k in (1, 2, 3):
         rc.start(n_bu + k, lambda k=k: (b_unit, bu_full.at[z], at_z(k)))
@@ -572,16 +568,17 @@
         for copy in here:
             copy.wait()
 
-    head_line.begin()
-    head_x(0)
+    head_at = lambda t: wh_at(d * nc + t)
+    for k in (1, 2, 3):
+        rc.start(n_hz + k, lambda k=k: (head_at(z), head_at(z), at_z(k)))
+    rc.start(n_hx, lambda: (head_at(z), head_at(z), at_x))
+    for line, src in zip(lines, sources):
+        line.begin(src)
     q_scr[...] = jnp.zeros_like(q_scr)
-    head_line.step(1)
-    head_x(1)
+    for k in (1, 2, 3):
+        rc.arrived(n_hz + k, head_at(z ^ k), at_z(k))
+        rc.start(n_hx + k, lambda k=k: (head_at(z ^ k), head_at(z ^ k), at_x))
     dense_step(1, True)
-    head_line.step(2)
-    head_x(2)
-    head_line.step(3)
-    head_x(3)
     for k in (1, 2, 3):
         rc.arrived(n_seg + k, seg.at[c ^ k], at_c(k))
     seg_here.wait()
@@ -594,7 +591,7 @@
     rc.start(n_tf, lambda: (tok_at(c ^ 2), tok_at(c ^ 2), at_c(1)))
     dense_step(2, True)
     for t in range(4):
-        rc.arrived(n_hx + t, wh_at((1 - d) * nc + t), at_x)
+        rc.arrived(n_hx + t, wh_at((1 - d) * nc + (z ^ t)), at_x)
     mine.wait()
     rc.arrived(n_tc, tok_at(c ^ 1), at_c(1))
     rc.arrived(n_tf, tok_at(c ^ 3), at_c(1))
@@ -716,7 +713,7 @@
     for n, r in zip(n_c, (row, row_x, row_y, row_d)):
         for i in range(4):
             came(n, i, r ^ 1, at_c(1))
-    for copy in (bu_here, x_here, wh_here, q_here, kv_here, ctx_here):
+    for copy in own_here + [bu_here, x_here, wh_here, q_here, kv_here, ctx_here]:
         copy.wait()
     rc.all_sent()
 
@@ -727,7 +724,7 @@
     group = w_o.shape[1]
     nc, nt, nr = 4, 4, 8
     rows = 3 * ln // 2 * nc
-    hb = pl.BlockSpec(memory_space=pl.ANY)
+    hb = pl.BlockSpec(memory_space=pltpu.HBM)
     vm = pl.BlockSpec(memory_space=pltpu.VMEM)
     sds = jax.ShapeDtypeStruct
     return pl.pallas_call(
@@ -745,7 +742,7 @@
             sds((group, rows), F32),
             sds((nc, 8, ln), jnp.int32),
         ),
-        in_specs=[hb] * 8,
+        in_specs=[hb] * 4 + [vm] + [hb] * 3,
         out_specs=(hb,) * 8 + (vm,) * 3,
         scratch_shapes=[
             pltpu.VMEM((2 * nc, ln, width), BF),
@@ -760,15 +757,252 @@
             pltpu.VMEM((2 * nc, ln, 128), F32),
             pltpu.VMEM((2 * nc, 8, ln), F32),
             pltpu.VMEM((rows, group), BF),
+            pltpu.VMEM((2, wr, units), BF),
+            pltpu.VMEM((wr, group), BF),
             pltpu.SemaphoreType.DMA((120,)),
             pltpu.SemaphoreType.DMA((120,)),
             pltpu.SemaphoreType.DMA((32,)),
         ],
         compiler_params=pltpu.CompilerParams(
-            vmem_limit_bytes=40 << 20, collective_id=0, has_side_effects=True
+            vmem_limit_bytes=60 << 20, collective_id=0, has_side_effects=True
         ),
         name="forward",
     )(tok2, seg2, w_head, b_head, b_unit, w_o, w_i, w_b)
+
+
+def middle_kernel(
+    ln,
+    tokens,
+    cotangent,
+    ctx_all,
+    w_o,
+    w_ib,
+    b_in,
+    vectors,
+    d_ctx,
+    g_b,
+    g_i,
+    g_o,
+    out_low,
+    d_first,
+    small,
+    x_own,
+    c_own,
+    w_v,
+    ctx_v,
+    w_ov,
+    n_one,
+    r_one,
+    normed,
+    low,
+    low_t,
+    tmp,
+    acc,
+    active,
+    slope,
+    n_two,
+    d_sec,
+    d_low,
+    gb_v,
+    gi_v,
+    w_sem,
+    g_sem,
+    sem,
+):
+    z = lax.axis_index("tp")
+    hl = ln // 2
+    own = ln + hl
+    blocks, _, group = ctx_all.shape
+    width = x_own.shape[1]
+    units = w_v.shape[2] // 4
+    step = 32
+    out_bias, gain_one, shift_one, back_bias, gain_two, shift_two = (
+        vectors.at[pl.ds(i, 1)] for i in range(6)
+    )
+    half_rows = pl.ds(pl.multiple_of((z % 2) * hl, 128), hl)
+    first_rows = []
+    for i, (src, dst) in enumerate(((tokens, x_own), (cotangent, c_own))):
+        for j, (a, b) in enumerate(
+            (
+                (src.at[(3 * z + 1) // 2], dst.at[pl.ds(0, ln)]),
+                (src.at[1 + 3 * (z // 2), half_rows], dst.at[pl.ds(ln, hl)]),
+            )
+        ):
+            first_rows.append(pltpu.make_async_copy(a, b, sem.at[2 * i + j]))
+    first_rows.append(pltpu.make_async_copy(ctx_all, ctx_v, sem.at[4]))
+    first_rows.append(pltpu.make_async_copy(w_o, w_ov, sem.at[5]))
+    for copy in first_rows:
+        copy.start()
+    t_cols = lambda t: pl.ds(pl.multiple_of(t * units, 128), units)
+
+    def weight(which, t):
+        return pltpu.make_async_copy(
+            w_ib.at[which, :, t_cols(t)], w_v.at[which, :, t_cols(t)], w_sem.at[which, t]
+        )
+
+    for t in range(4):
+        for which in range(2):
+            weight(which, t).start()
+    for copy in first_rows:
+        copy.wait()
+
+    def chunks(body):
+        @pl.loop(0, own // step)
+        def _(i):
+            body(pl.ds(pl.multiple_of(i * step, step), step))
+
+    mean = lambda v: jnp.mean(v, -1, keepdims=True)
+    add = lambda i, v: small.__setitem__(
+        (slice(i, i + 1), slice(None)), small[i : i + 1, :] + jnp.sum(v, 0, keepdims=True)
+    )
+    small[...] = jnp.zeros_like(small)
+
+    tmp[...] = dot_nt(ctx_v[0], w_ov[0])
+    for g in range(1, blocks):
+        tmp[...] += dot_nt(ctx_v[g], w_ov[g])
+
+    def norm_one(r):
+        value = x_own[r, :].astype(F32) + (tmp[r, :] + out_bias[...])
+        centered = value - mean(value)
+        rstd = lax.rsqrt(mean(centered * centered) + 1e-12)
+        normal = centered * rstd
+        n_one[r, :] = normal
+        r_one[r, :] = jnp.broadcast_to(rstd, (step, 128))
+        got = normal * gain_one[...] + shift_one[...]
+        normed[r, :] = got
+        low[r, :] = got.astype(BF)
+        acc[r, :] = got + back_bias[...]
+
+    chunks(norm_one)
+    low_t[...] = low[...].T
+
+    @pl.loop(0, 4)
+    def _(t):
+        weight(0, t).wait()
+        weight(1, t).wait()
+        tmp[...] = dot_nn(low[...], w_v[0, :, t_cols(t)]) + b_in[pl.ds(t, 1), 0, :]
+
+        def gelu(r):
+            u = tmp[r, :]
+            cdf = 0.5 * (1.0 + lax.erf(u * math.sqrt(0.5)))
+            active[r, t_cols(t)] = (u * cdf).astype(BF)
+            slope[r, t_cols(t)] = cdf + u * jnp.exp(-0.5 * u * u) * (
+                1.0 / math.sqrt(2.0 * math.pi)
+            )
+
+        chunks(gelu)
+        acc[...] += dot_nt(active[:, t_cols(t)], w_v[1, :, t_cols(t)])
+
+    def norm_two(r):
+        value = acc[r, :]
+        centered = value - mean(value)
+        rstd = lax.rsqrt(mean(centered * centered) + 1e-12)
+        normal = centered * rstd
+        out_low[r, :] = (normal * gain_two[...] + shift_two[...]).astype(BF)
+        grad = c_own[r, :].astype(F32)
+        add(4, grad * normal)
+        add(5, grad)
+        scaled = grad * gain_two[...]
+        got = rstd * (scaled - mean(scaled) - normal * mean(scaled * normal))
+        d_sec[r, :] = got
+        add(3, got)
+        d_low[r, :] = got.astype(BF)
+        acc[r, :] = got
+
+    chunks(norm_two)
+    n_two[...] = d_low[...].T
+
+    @pl.loop(0, 4)
+    def _(t):
+        gb_v[:, t_cols(t)] = dot_nn(n_two[...], active[:, t_cols(t)]).astype(BF)
+        pltpu.make_async_copy(gb_v.at[:, t_cols(t)], g_b.at[:, t_cols(t)], g_sem.at[0, t]).start()
+        tmp[...] = dot_nn(d_low[...], w_v[1, :, t_cols(t)])
+
+        def inner_back(r):
+            got = tmp[r, :] * slope[r, t_cols(t)]
+            at = pl.ds(6 + t, 1)
+            small[at, :] += jnp.sum(got, 0, keepdims=True)
+            active[r, t_cols(t)] = got.astype(BF)
+
+        chunks(inner_back)
+        gi_v[:, t_cols(t)] = dot_nn(low_t[...], active[:, t_cols(t)]).astype(BF)
+        pltpu.make_async_copy(gi_v.at[:, t_cols(t)], g_i.at[:, t_cols(t)], g_sem.at[1, t]).start()
+        acc[...] += dot_nt(active[:, t_cols(t)], w_v[0, :, t_cols(t)])
+
+    def norm_one_back(r):
+        grad = acc[r, :]
+        normal = n_one[r, :]
+        add(1, grad * normal)
+        add(2, grad)
+        scaled = grad * gain_one[...]
+        got = r_one[r, 0:1] * (scaled - mean(scaled) - normal * mean(scaled * normal))
+        d_first[r, :] = got
+        add(0, got)
+        d_low[r, :] = got.astype(BF)
+
+    chunks(norm_one_back)
+    n_two[...] = d_low[...].T
+    for g in range(blocks):
+        d_ctx[g] = dot_nn(d_low[...], w_ov[g]).astype(BF)
+        g_o[g] = dot_nn(n_two[...], ctx_v[g]).astype(BF)
+    for t in range(4):
+        pltpu.make_async_copy(gb_v.at[:, t_cols(t)], g_b.at[:, t_cols(t)], g_sem.at[0, t]).wait()
+        pltpu.make_async_copy(gi_v.at[:, t_cols(t)], g_i.at[:, t_cols(t)], g_sem.at[1, t]).wait()
+
+
+def middle(tokens, cotangent, ctx_all, w_o, w_ib, b_in, vectors):
+    blocks, own, group = ctx_all.shape
+    ln, width = tokens.shape[1:]
+    all_units = w_ib.shape[2]
+    hb = pl.BlockSpec(memory_space=pltpu.HBM)
+    vm = pl.BlockSpec(memory_space=pltpu.VMEM)
+    sds = jax.ShapeDtypeStruct
+    v = pltpu.VMEM
+    return pl.pallas_call(
+        functools.partial(middle_kernel, ln),
+        out_shape=(
+            sds((blocks, own, group), BF),
+            sds((width, all_units), BF),
+            sds((width, all_units), BF),
+            sds((blocks, width, group), BF),
+            sds((own, width), BF),
+            sds((own, width), F32),
+            sds((16, width), F32),
+        ),
+        in_specs=[hb] * 5 + [vm] * 2,
+        out_specs=(vm, hb, hb, vm, vm, vm, vm),
+        scratch_shapes=[
+            v((own, width), BF),
+            v((own, width), BF),
+            v((2, width, all_units), BF),
+            v((blocks, own, group), BF),
+            v((blocks, width, group), BF),
+            v((own, width), F32),
+            v((own, 128), F32),
+            v((own, width), F32),
+            v((own, width), BF),
+            v((width, own), BF),
+            v((own, width), F32),
+            v((own, width), F32),
+            v((own, all_units), BF),
+            v((own, all_units), F32),
+            v((width, own), BF),
+            v((own, width), F32),
+            v((own, width), BF),
+            v((width, all_units), BF),
+            v((width, all_units), BF),
+            pltpu.SemaphoreType.DMA((2, 4)),
+            pltpu.SemaphoreType.DMA((2, 4)),
+            pltpu.SemaphoreType.DMA((6,)),
+        ],
+        compiler_params=pltpu.CompilerParams(vmem_limit_bytes=60 << 20),
+        cost_estimate=pl.CostEstimate(
+            flops=2 * own * width * (6 * all_units + 3 * width),
+            bytes_accessed=24 << 20,
+            transcendentals=2 * own * all_units,
+        ),
+        name="middle",
+    )(tokens, cotangent, ctx_all, w_o, w_ib, b_in, vectors)
 
 
 def add_into(dst, other, rows):
@@ -966,22 +1200,55 @@
         add_into(views(w, blk(d, y), 0), buf_views(w, w[3], 2), wr)
         rc.arrived(n[6], w[2].at[2], at_x)
         add_into(views(w, blk(d, y), 1), buf_views(w, w[2], 2), wr)
-        rc.start(n[7], lambda: (unit_at(w, z ^ 1), w[4].at[0], at_z(1)))
-        rc.start(n[8], lambda: (unit_at(w, z ^ 3), w[4].at[1], at_z(1)))
+        for t in (0, 1, 2):
+            chain_send(w, t, 3)
+        for t in (3, 2, 1):
+            chain_send(w, t, 0)
+
+    def chain_send(w, t, at):
+        to = at + 1 if t > at else at - 1
+        slot = 4 if to == t and t > at else t
+        n = w[8]
+        rc.start(
+            n[7 + slot],
+            lambda: (unit_at(w, t), w[4].at[slot], (d, c, to)),
+            lambda: z == at,
+            n[7 + t],
+        )
+
+    def chain_pass(w, t, at):
+        @pl.when(z == at)
+        def _():
+            rc.arrived(w[8][7 + t], w[4].at[t], at_x)
+            add_into([unit_at(w, t)], [w[4].at[t]], wr)
+
+        chain_send(w, t, at)
 
     def w_line(i):
         w = weights[i]
-        n = w[8]
-        rc.arrived(n[8], w[4].at[1], at_z(1))
-        add_into([unit_at(w, z ^ 2)], [w[4].at[1]], wr)
-        rc.start(n[9], lambda: (unit_at(w, z ^ 2), w[4].at[2], at_z(2)))
-        rc.arrived(n[7], w[4].at[0], at_z(1))
-        add_into([unit_at(w, z)], [w[4].at[0]], wr)
+        for t in (0, 1):
+            chain_pass(w, t, 2)
+        for t in (3, 2):
+            chain_pass(w, t, 1)
+
+    def w_next(i):
+        w = weights[i]
+        chain_pass(w, 3, 2)
+        chain_pass(w, 0, 1)
 
     def w_end(i):
         w = weights[i]
-        rc.arrived(w[8][9], w[4].at[2], at_z(2))
-        w[6][...] = unit_at(w, z)[...].astype(F32) + w[4].at[2][...].astype(F32)
+        for t in range(4):
+
+            @pl.when(z == t)
+            def _():
+                if t < 3:
+                    rc.arrived(w[8][7 + t], w[4].at[t], at_x)
+                if t > 0:
+                    rc.arrived(w[8][11], w[4].at[4], at_x)
+
+        total = unit_at(w, z)[...].astype(F32) + w[4].at[z][...].astype(F32)
+        w[6][...] = total + w[4].at[4][...].astype(F32)
 
     whole_of = lambda t: (3 * t + 1) // 2
     shared_of = lambda t: 1 + 3 * (t // 2)
@@ -1036,8 +1303,6 @@
     for k in (1, 2, 3):
         rc.start(n_ctx[k - 1], lambda k=k: (d_ctx.at[c ^ k], d_got.at[c], at_c(k)))
     ctx_here = copy_here(d_ctx.at[c], d_got.at[c])
-    for w in weights:
-        w_core_send(w)
     kv_here = copy_here(kv_in, kv)
     q_here = copy_here(q_in, q_scr)
     n_small = [next(number) for _ in range(5)]
@@ -1055,50 +1320,12 @@
             small_send(i + 1)
 
     small_got[0, 1] = small_in[...]
-    small_send(0)
     wh_here = copy_here(wh_in, wh)
     xt_here = copy_here(xt_in, xt)
-    out_lines[0].begin(out_low.at[pl.ds(0, ln)])
-    out_lines[1].begin(out_low.at[pl.ds(ln, hl)])
     out_here = [
         copy_here(out_low.at[pl.ds(0, ln)], out_lines[0].at(z)),
         copy_here(out_low.at[pl.ds(ln, hl)], out_lines[1].at(z)),
     ]
-
-    for i in range(nc):
-        for s in range(2):
-            line = seg[i, s : s + 1, :].astype(F32)
-            segr[2 * i + s, 0:1, :] = line
-            segc[2 * i + s] = jnp.broadcast_to(line, (128, ln)).T
-    dkv[...] = jnp.zeros_like(dkv)
-    d_o[...] = jnp.zeros_like(d_o)
-    d_proj[...] = jnp.zeros_like(d_proj)
-    bias_sum[...] = jnp.zeros_like(bias_sum)
-    kv_here.wait()
-
-    @pl.loop(0, nc)
-    def _(j):
-        for s in range(2):
-            rows = pl.ds(pl.multiple_of((2 * j + s) * ln, ln), ln)
-            for h in range(heads):
-                kvt[s * heads + h, :, pl.ds(pl.multiple_of(j * ln, ln), ln)] = kv[
-                    rows, 128 * h : 128 * h + 128
-                ].T
-
-    w_core_add(0)
-    small_step(0)
-    for k in (1, 2, 3):
-        rc.arrived(n_ctx[k - 1], d_got.at[c ^ k], at_c(k))
-    ctx_here.wait()
-
-    @pl.loop(0, nc)
-    def _(i):
-        rows = pl.ds(pl.multiple_of(i * own, 128), own)
-        for h in range(heads):
-            d_o[rows, 128 * h + HEAD : 128 * h + 128] = d_got[i, :, HEAD * h : HEAD * h + HEAD]
-
-    q_here.wait()
-    w_core_add(1)
 
     def block(qb):
         r0, r1, o0, o1, seq = block_rows(qb, half, ln)
@@ -1254,83 +1481,136 @@
         def _():
             bias_fin[...] = bias_sum[...]
 
-    wh_here.wait()
-    xt_here.wait()
+    for w in weights:
+
+        @pl.when(z == 0)
+        def _():
+            w[4][4] = jnp.zeros_like(w[4][4])
+
+        @pl.when(z == 3)
+        def _():
+            w[4][3] = jnp.zeros_like(w[4][3])
+
+    def get_ctx():
+        for k in (1, 2, 3):
+            rc.arrived(n_ctx[k - 1], d_got.at[c ^ k], at_c(k))
+        ctx_here.wait()
+
+        @pl.loop(0, nc)
+        def _(i):
+            rows = pl.ds(pl.multiple_of(i * own, 128), own)
+            for h in range(heads):
+                d_o[rows, 128 * h + HEAD : 128 * h + 128] = d_got[
+                    i, :, HEAD * h : HEAD * h + HEAD
+                ]
+
+        q_here.wait()
+        wh_here.wait()
+        xt_here.wait()
+
+    def out_begin():
+        out_lines[0].begin(out_low.at[pl.ds(0, ln)])
+        out_lines[1].begin(out_low.at[pl.ds(ln, hl)])
+
+    out_begin()
+    w_core_send(weights[0])
+    w_core_send(weights[2])
+    for i in range(nc):
+        for s in range(2):
+            line = seg[i, s : s + 1, :].astype(F32)
+            segr[2 * i + s, 0:1, :] = line
+            segc[2 * i + s] = jnp.broadcast_to(line, (128, ln)).T
+    dkv[...] = jnp.zeros_like(dkv)
+    d_o[...] = jnp.zeros_like(d_o)
+    d_proj[...] = jnp.zeros_like(d_proj)
+    bias_sum[...] = jnp.zeros_like(bias_sum)
     acc_h[...] = jnp.zeros_like(acc_h)
+    kv_here.wait()
+
+    @pl.loop(0, nc)
+    def _(j):
+        for s in range(2):
+            rows = pl.ds(pl.multiple_of((2 * j + s) * ln, ln), ln)
+            for h in range(heads):
+                kvt[s * heads + h, :, pl.ds(pl.multiple_of(j * ln, ln), ln)] = kv[
+                    rows, 128 * h : 128 * h + 128
+                ].T
+
+    small_send(0)
+    w_core_add(0)
+    get_ctx()
 
     @pl.loop(0, 6)
     def _(i):
-        block(jnp.where(i < 2, i + 4, i - 2))
+        block(jnp.where(i == 0, 0, jnp.where(i == 1, 1, jnp.where(i == 2, 2, jnp.where(i == 3, 3, jnp.where(i == 4, 4, 5))))))
 
         @pl.when(i == 0)
         def _():
+            w_core_send(weights[1])
+            small_step(0)
             w_core_add(2)
-
-        @pl.when(i == 1)
-        def _():
-            t_partial(1)
-            h_partial(1)
-            small_step(1)
-            for line in out_lines:
-                line.step(1)
-
-        @pl.when(i == 2)
-        def _():
-            w_plane(0)
-            t_core(1)
+            out_lines[0].step(1)
+            out_lines[1].step(1)
 
         @pl.when(i == 3)
         def _():
-            small_step(2)
-
-        @pl.when(i == 4)
-        def _():
-            w_corner(0)
-            small_step(3)
-            for line in out_lines:
-                line.step(2)
-
-    t_partial(0)
+            t_partial(0)
+            out_lines[0].step(2)
+            out_lines[1].step(2)
+            t_core(0)
+            w_plane(2)
+
+    t_whole(0)
     h_partial(0)
+    t_whole(1)
+    w_plane(0)
+    t_partial(1)
+    w_corner(2)
+    t_core(1)
+    small_step(1)
+    bias_send(0)
+    w_core_add(1)
+    tok_lines[0].step(1)
+    w_corner(0)
+    w_line(2)
+    small_step(2)
+    bias_step(0)
+    tok_lines[1].step(1)
+    h_partial(1)
+    out_lines[0].step(3)
+    out_lines[1].step(3)
+    tok_lines[0].step(2)
+    t_shared()
+    bias_step(1)
     h_send()
-    bias_send(0)
-    t_core(0)
-    t_shared()
+    t_shared_end()
+    tok_lines[1].step(2)
     w_plane(1)
+    tok_lines[0].step(3)
+    w_line(0)
+    h_plane()
+    tok_lines[2].step(1)
+    w_next(0)
+    bias_step(2)
+    h_line()
+    small_step(3)
+    w_next(2)
+    w_corner(1)
+    w_end(2)
+    w_end(0)
+    h_end()
+    tok_lines[2].step(2)
+    w_line(1)
+    w_next(1)
+    tok_lines[1].step(3)
+    tok_lines[2].step(3)
     small_step(4)
-    t_whole(0)
-    t_whole(1)
-    w_plane(2)
-    t_shared_end()
-    bias_step(0)
-    h_plane()
-    w_line(0)
-    tok_lines[0].step(1)
-    tok_lines[1].step(1)
-    tok_lines[2].step(1)
-    w_corner(1)
-    bias_step(1)
-    w_corner(2)
-    tok_lines[0].step(2)
-    tok_lines[1].step(2)
-    tok_lines[2].step(2)
-    h_line()
-    bias_step(2)
-    w_line(1)
-    w_line(2)
-    h_end()
-    for line in out_lines:
-        line.step(3)
-    w_end(0)
     w_end(1)
-    w_end(2)
     tok_here = [
         copy_here(done.at[pl.ds(0, hl)], tok_lines[0].at(z)),
         copy_here(done.at[pl.ds(hl, hl)], tok_lines[1].at(z)),
         copy_here(done.at[pl.ds(ln, hl)], tok_lines[2].at(z)),
     ]
-    for line in tok_lines:
-        line.step(3)
 
     @pl.when(c != z)
     def _():
@@ -1352,7 +1632,7 @@
     width = out_low.shape[1]
     wr, all_units = g_b.shape[2:]
     units = all_units // 4
-    hb = pl.BlockSpec(memory_space=pl.ANY)
+    hb = pl.BlockSpec(memory_space=pltpu.HBM)
     vm = pl.BlockSpec(memory_space=pltpu.VMEM)
     sds = jax.ShapeDtypeStruct
     v = pltpu.VMEM
@@ -1370,7 +1650,7 @@
             sds(small.shape, F32),
             sds((8, 3 * group), F32),
         ),
-        in_specs=[hb] * 5 + [vm, vm] + [hb] * 4 + [vm] * 3,
+        in_specs=[hb] * 4 + [vm] * 3 + [hb] * 4 + [vm] * 3,
         out_specs=(hb, hb) + (vm,) * 6,
         scratch_shapes=[
             v((n2, heads * 128), BF),
@@ -1405,9 +1685,9 @@
             v((3, wr, 2 * units), BF),
             v((3, wr, 2 * units), BF),
             v((3, 2, wr, group), BF),
-            v((3, wr, units), BF),
-            v((3, wr, units), BF),
-            v((3, wr, group), BF),
+            v((5, wr, units), BF),
+            v((5, wr, units), BF),
+            v((5, wr, group), BF),
             v((width, 3 * group), F32),
             v((width, 3 * group), BF),
             v((4 * wr, 3 * group), BF),
@@ -1423,10 +1703,60 @@
             pltpu.SemaphoreType.DMA((40,)),
         ],
         compiler_params=pltpu.CompilerParams(
-            vmem_limit_bytes=58 << 20, collective_id=1, has_side_effects=True
+            vmem_limit_bytes=60 << 20, collective_id=1, has_side_effects=True
         ),
         name="backward",
     )(d_ctx, g_b, g_i, g_o, out_low, d_first, small, q, kv, xt, wh, lse, ctx_t, seg)
+
+
+def finish_kernel(
+    heads, tok_in, out_in, g_b, g_i, g_o, g_h, small, bias,
+    tok, out, gb, gi, go, gh, gq, gv, w0, w1, w2, in_b, w3, w4, w5,
+):
+    tok[...] = tok_in[...].astype(F32)
+    out[...] = out_in[...]
+    z = lax.axis_index("tp")
+    wide = heads * 128
+
+    @pl.when(pl.program_id(0) == 0)
+    def _():
+        gb[...] = g_b[...]
+        gi[...] = g_i[...]
+        go[...] = g_o[...]
+        pick = lambda ref, rows, at: jnp.concatenate(
+            [ref[rows, 128 * h + at : 128 * h + at + HEAD] for h in range(heads)], -1
+        )
+        gh[:, 0, :] = g_h[:, wide:]
+        gh[:, 1, :] = pick(g_h, slice(None), 0)
+        gh[:, 2, :] = pick(g_h, slice(None), HEAD)
+        gq[...] = bias[0, wide:]
+        gv[...] = pick(bias, 0, HEAD)
+        for i, ref in ((0, w0), (1, w1), (2, w2), (3, w3), (4, w4), (5, w5)):
+            ref[...] = small[i, :]
+        in_b[...] = small[pl.ds(6 + z, 1), :].reshape(in_b.shape)
+
+
+def finish(d_tokens, output, g_b, g_i, g_o, g_h, small, d_bias, heads):
+    seqs, ln, width = d_tokens.shape
+    wr, units = g_b.shape
+    group = g_o.shape[1]
+    one = lambda: pl.BlockSpec((1, ln, width), lambda i: (i, 0, 0))
+    whole = lambda shape: pl.BlockSpec(shape, lambda i: (0,) * len(shape))
+    sds = jax.ShapeDtypeStruct
+    rest = [
+        (wr, units), (wr, units), (wr, group), (wr, 3, group), (group,), (group,),
+        (width,), (width,), (width,), (units,), (width,), (width,), (width,),
+    ]
+    return pl.pallas_call(
+        functools.partial(finish_kernel, heads),
+        grid=(seqs,),
+        out_shape=[sds(d_tokens.shape, F32), sds(output.shape, BF)] + [sds(s, F32) for s in rest],
+        in_specs=[one(), one()]
+        + [whole(a.shape) for a in (g_b, g_i, g_o, g_h, small, d_bias)],
+        out_specs=[one(), one()] + [whole(s) for s in rest],
+        compiler_params=pltpu.CompilerParams(vmem_limit_bytes=60 << 20),
+        name="finish",
+    )(d_tokens, output, g_b, g_i, g_o, g_h, small, d_bias)
 
 
 def head_order(kinds, heads):
@@ -1434,13 +1764,6 @@
     q, k, v = (a.reshape(lead + (heads, HEAD)) for a in kinds)
     kv = jnp.concatenate([k, v], -1).reshape(lead + (heads * 2 * HEAD,))
     return jnp.concatenate([kv, q.reshape(lead + (heads * HEAD,))], -1)
-
-
-def head_kinds(value, heads):
-    lead = value.shape[:-1]
-    kv = value[..., : heads * 2 * HEAD].reshape(lead + (heads, 2, HEAD))
-    flat = lambda a: a.reshape(lead + (heads * HEAD,))
-    return value[..., heads * 2 * HEAD :], flat(kv[..., 0, :]), flat(kv[..., 1, :])
 
 
 def forward_plain(sizes, me, tok2, seg2, w_head, b_head, b_unit, w_o, w_i, w_b, heads):
@@ -1549,11 +1872,12 @@
         lax.dynamic_index_in_dim(shared, 1 - half, 0, keepdims=False), "tp", nt, 1
     )
     d_own = (jnp.concatenate([part[0], shared], 0) + d_first).astype(BF)
-    d_tokens = spread_rows(d_own, F32)
+    d_tokens = spread_rows(d_own, BF)
     g_h = scatter_heads(jnp.dot(xt, d_proj, preferred_element_type=F32).astype(BF), sizes, me)
     slots = jnp.zeros((nc,) + d_bias[0].shape, F32)
     slots = lax.psum(lax.dynamic_update_index_in_dim(slots, d_bias[0], c, 0), ALL)
     d_bias = lax.dynamic_index_in_dim(slots, z, 0, keepdims=False)
+    d_bias = jnp.broadcast_to(d_bias[None], (8,) + d_bias.shape)
     return output, d_tokens, g_back, g_in, g_out, g_h, small, d_bias
 
 
@@ -1578,7 +1902,6 @@
 ):
     nd, nc, nt = sizes
     seqs, ln, width = tokens.shape
-    hl = ln // 2
     group = w_out.shape[1]
     heads = group // HEAD
     units = w_in.shape[1]
@@ -1589,11 +1912,6 @@
     shared_of = lambda t: 1 + 3 * (t // 2)
     half_of = lambda t: t % 2
     sf, sh, half = whole_of(z), shared_of(z), half_of(z)
-
-    def own_rows(a):
-        one = lax.dynamic_index_in_dim(a, sf, 0, keepdims=False)
-        two_ = lax.dynamic_index_in_dim(a, sh, 0, keepdims=False)
-        return jnp.concatenate([one, lax.dynamic_slice_in_dim(two_, half * hl, hl, 0)], 0)
 
     def own_pair(a):
         return jnp.stack(
@@ -1615,45 +1933,12 @@
     ctx_all, xt, q, kv, wh, w_o, w_ib, b_in, lse, ctx_t, seg_all = got
     w_o = w_o.reshape(nt, width, group)
     w_ib = w_ib.reshape(2, width, nt * units)
-    w_i, w_b = w_ib[0], w_ib[1]
-    b_in = b_in[:, 0].reshape(nt * units)
-    own = ln + hl
-
-    x_own = own_rows(tokens).astype(F32)
-    attended = jnp.einsum("gtf,gdf->td", ctx_all, w_o, preferred_element_type=F32) + out_bias
-    normal_one, rstd_one = norm_parts(x_own + attended)
-    normed = normal_one * gain_one + shift_one
-    normed_low = normed.astype(BF)
-    inner = jnp.dot(normed_low, w_i, preferred_element_type=F32) + b_in
-    active = jax.nn.gelu(inner, approximate=False).astype(BF)
-    branch = jnp.einsum("tf,df->td", active, w_b, preferred_element_type=F32)
-    second = normed + branch + back_bias
-    normal_two, rstd_two = norm_parts(second)
-    out_low = (normal_two * gain_two + shift_two).astype(BF)
-
-    d_second, d_gain_two, d_shift_two = norm_back(
-        own_rows(cotangent).astype(F32), normal_two, rstd_two, gain_two
+    vectors = jnp.stack([out_bias, gain_one, shift_one, back_bias, gain_two, shift_two])
+    d_ctx, g_b, g_i, g_o, out_low, d_first, small = middle(
+        tokens, cotangent, ctx_all, w_o, w_ib, b_in, vectors
     )
-    d_second_low = d_second.astype(BF)
-    d_back_bias = jnp.sum(d_second, 0)
-    d_w_back = jnp.einsum("td,tf->df", d_second_low, active, preferred_element_type=F32)
-    d_active = jnp.dot(d_second_low, w_b, preferred_element_type=F32)
-    d_inner = d_active * gelu_slope(inner)
-    d_in_bias = jnp.sum(d_inner, 0)
-    d_inner_low = d_inner.astype(BF)
-    d_w_in = jnp.einsum("td,tf->df", normed_low, d_inner_low, preferred_element_type=F32)
-    d_normed = jnp.einsum("tf,df->td", d_inner_low, w_i, preferred_element_type=F32) + d_second
-    d_first, d_gain_one, d_shift_one = norm_back(d_normed, normal_one, rstd_one, gain_one)
-    d_first_low = d_first.astype(BF)
-    d_out_bias = jnp.sum(d_first, 0)
-    d_w_out = jnp.einsum("td,gtf->gdf", d_first_low, ctx_all, preferred_element_type=F32)
-    d_ctx = jnp.einsum("td,gdf->gtf", d_first_low, w_o, preferred_element_type=F32).astype(BF)
-    small = jnp.concatenate(
-        [d_out_bias, d_gain_one, d_shift_one, d_back_bias, d_gain_two, d_shift_two, d_in_bias]
-    )
-    low = (d_w_back.astype(BF), d_w_in.astype(BF), d_w_out.astype(BF))
+    low = (g_b, g_i, g_o)
     if sizes == (2, 4, 4):
-        small = jnp.concatenate([small, jnp.zeros((-small.shape[0] % 1024,), F32)])
         output, d_tokens, g_back, g_in, g_out, g_h, small, d_bias = backward(
             d_ctx,
             low[0].reshape(4, 2, wr, nt * units),
@@ -1661,7 +1946,7 @@
             low[2].reshape(nt, 4, 2, wr, group),
             out_low,
             d_first,
-            small.reshape(-1, 128),
+            small,
             q,
             kv,
             xt,
@@ -1672,37 +1957,14 @@
             heads,
             seqs,
         )
-        d_tokens = d_tokens.astype(F32)
-        small = small.reshape(-1)
-        d_bias = d_bias[0]
     else:
         output, d_tokens, g_back, g_in, g_out, g_h, small, d_bias = backward_plain(
             sizes, me, d_ctx, low, out_low, d_first, small, q, kv, xt, wh, lse, ctx_t, seg_all, heads, seqs
         )
-    g_qkv = jnp.stack(head_kinds(g_h, heads), 1)
-    d_qb, _, d_vb = head_kinds(d_bias, heads)
-    qv = jnp.concatenate([d_qb, d_vb])
-    wide = small[: 6 * width].reshape(6, width)
-    g_in_bias = lax.dynamic_index_in_dim(
-        small[6 * width : 6 * width + nt * units].reshape(nt, units), z, 0, keepdims=False
+    d_tokens, output, g_b, g_i, g_o, g_h, d_qb, d_vb, w0, w1, w2, d_in, w3, w4, w5 = finish(
+        d_tokens, output, g_back, g_in, g_out, g_h, small, d_bias, heads
     )
-    return (
-        output,
-        d_tokens,
-        g_qkv,
-        qv[:group],
-        qv[group:],
-        g_out,
-        wide[0],
-        wide[1],
-        wide[2],
-        g_in,
-        g_in_bias,
-        g_back,
-        wide[3],
-        wide[4],
-        wide[5],
-    )
+    return (output, d_tokens, g_h, d_qb, d_vb, g_o, w0, w1, w2, g_i, d_in, g_b, w3, w4, w5)
 
 
 def solution(mesh):

time: 327 us -> 273 us (0.83); the launches traced: 321 us -> 273 us
  matrix products: 36.4 us -> 0 us
  local copies, waits for them, and re-layouts: 37.8 us -> 12.5 us
  Pallas kernels: 236 us -> 256 us
  other arithmetic: 9.24 us -> 3 us
    pallas_call x0 -> x2, Pallas kernels: none -> 45.9 us  [the longest x1 38.6 us: middle(): pl.pallas_call(functools.partial(middle_kernel, ln), out_shape=(sds((bloc...]
    dot_general x9 -> x0, matrix products: 36.4 us -> none  [the longest x1 12 us: per_device(): inner = jnp.dot(normed_low, w_i, preferred_element_type=F32) + b_in]
    pallas_call x1, Pallas kernels: 149 us -> 125 us  [backward(): pl.pallas_call(functools.partial(backward_kernel, heads, ln), out_shape=(...]
    slice x9 -> x0, local copies, waits for them, and re-layouts: 13.8 us -> none  [the longest x1 8.77 us: per_device(): w_i, w_b = (w_ib[0], w_ib[1])]
    unnamed x93 -> x3, local copies, waits for them, and re-layouts: 12.6 us -> 1.99 us
    convert_element_type x1 -> x0, other arithmetic: 4.42 us -> none  [per_device(): d_tokens = d_tokens.astype(F32)]
    reduce_sum x5 -> x0, other arithmetic: 3.84 us -> none  [the longest x1 1.49 us: norm_back(): d_gain = jnp.sum(grad * normal, 0)]
    convert_element_type x2 -> x0, local copies, waits for them, and re-layouts: 3.79 us -> none  [the longest x1 2.63 us: per_device(): low = (d_w_back.astype(BF), d_w_in.astype(BF), d_w_out.astype(BF))]
where the time goes in v4:
time: 273 us
  Pallas kernels  256 us (94%)
  local copies, waits for them, and re-layouts  12.5 us (5%)
  other arithmetic  3 us (1%)
    pallas_call x1, Pallas kernels, backward(): pl.pallas_call(functools.partial(backward_kernel, heads, ln), out_shape=(...  125 us
    pallas_call x1, Pallas kernels, forward(): pl.pallas_call(functools.partial(forward_kernel, heads, ln), out_shape=(s...  85.2 us
    pallas_call x1, Pallas kernels, middle(): pl.pallas_call(functools.partial(middle_kernel, ln), out_shape=(sds((bloc...  38.6 us
    pallas_call x1, Pallas kernels, finish(): pl.pallas_call(functools.partial(finish_kernel, heads), grid=(seqs,), out...  7.29 us

profile of v4, /device:TPU:0, one launch (start us, length us, event | category | flops | bytes accessed | tf_op | source)
XLA Modules:
  0.0 272.5 jit_solution(4508100592055967675)
XLA Ops:
  0.7 0.1 pad.9.clone
  0.8 0.8 reshape.58
  1.5 0.1 pad_bitcast_fusion
  1.6 0.7 pad_maximum_fusion.3
  2.3 0.8 constant_dynamic-slice_fusion.1
  3.1 0.7 stack.29
  3.7 0.7 stack.30
  4.4 0.7 stack.31
  5.1 0.7 stack.32
  5.8 0.7 stack.33
  6.5 0.7 stack.34
  7.2 0.7 add_add_fusion.seg2
  7.9 0.6 stack.35.vectors
  8.5 0.6 broadcast_in_dim.7.b_head
  9.1 1.3 broadcast_in_dim.8.b_unit
  10.4 0.9 fusion
  11.3 0.1 copy.37
  11.4 0.1 copy.38
  11.5 0.1 copy.36
  11.6 0.7 pad_maximum_fusion.1.w_head
  12.3 1.2 constant_dynamic-slice_fusion.3
  13.5 0.9 pad_maximum_fusion.tok2
  14.4 85.2 %forward.1 = (bf16[4,384,192]{2,1,0:T(8,128)(2,1)}, bf16[768,2048]{1,0:T(8,128)(2,1)}, bf16[2048,384]{1,0:T(8,128)(2,1)}, bf16[2048,384]{1,0:T(8,128)(2,1)}, bf1...) custom-call(bf16[2,256,768]{2,1,0:T(8,128)(2,1)} %pad_maximum_fusion, ...), custom_call_target="tpu_custom_call" | custom-call | tf_op jit(solution)/shard_map/forward/pallas_call | solution.py:730
  99.6 38.6 %middle.1 = (bf16[4,384,192]{2,1,0:T(8,128)(2,1)}, bf16[768,3072]{1,0:T(8,128)(2,1)}, bf16[768,3072]{1,0:T(8,128)(2,1)}, bf16[4,768,192]{2,1,0:T(8,128)(2,1)}, b...) custom-call(bf16[6,256,768]{2,1,0:T(8,128)(2,1)} %tokens.1, bf16[6,256,768]{2,1,0:T(8,128)(2,1)} %cotangent.1, ...), custom_call_target="tpu_custom_call" | custom-call | flops 12230590464 | bytes 25165824 | tf_op jit(solution)/shard_map/middle/pallas_call | solution.py:961
  138.3 125.2 %backward.1 = (bf16[6,256,768]{2,1,0:T(8,128)(2,1)}, bf16[6,256,768]{2,1,0:T(8,128)(2,1)}, f32[96,768]{1,0:T(8,128)}, f32[96,768]{1,0:T(8,128)}, f32[96,192]{1,0...) custom-call(bf16[4,384,192]{2,1,0:T(8,128)(2,1)} %get-tuple-element.60.d_ctx, ...), custom_call_target="tpu_custom_call" | custom-call | tf_op jit(solution)/shard_map/backward/pallas_call | solution.py:1641
  263.4 7.3 %finish.1 = (f32[6,256,768]{2,1,0:T(8,128)}, bf16[6,256,768]{2,1,0:T(8,128)(2,1)}, f32[96,768]{1,0:T(8,128)}, f32[96,768]{1,0:T(8,128)}, f32[96,192]{1,0:T(8,128...) custom-call(bf16[6,256,768]{2,1,0:T(8,128)(2,1)} %get-tuple-element., ...), custom_call_target="tpu_custom_call" | custom-call | tf_op jit(solution)/shard_map/finish/pallas_call | solution.py:1750
  270.7 1.8 copy.35
  (2 shorter events, 0.0 us)

commit v5 on v4

--- a/solution.py
+++ b/solution.py
@@ -357,11 +357,12 @@
 def forward_kernel(
     heads,
     ln,
-    tok2,
-    seg2,
-    w_head,
-    b_head,
-    b_unit,
+    tokens,
+    segments,
+    w_kinds,
+    q_bias,
+    v_bias,
+    in_bias,
     w_o,
     w_i,
     w_b,
@@ -390,6 +391,10 @@
     context,
     w_src,
     o_src,
+    seg2,
+    w_head,
+    b_head,
+    b_unit,
     send,
     recv,
     local,
@@ -426,37 +431,54 @@
     wh_at = lambda r: wh.at[pl.ds(pl.multiple_of(r * wr, wr), wr)]
     tok_at = lambda i: x2.at[pl.ds(2 * i, 2)]
     w_here = [copy_here(w_i, w_src.at[0]), copy_here(w_b, w_src.at[1]), copy_here(w_o, o_src)]
-    mine = copy_here(tok2, tok_at(c))
-    seg_here = copy_here(seg2, seg.at[c])
-    bu_here = copy_here(b_unit, bu_full.at[z])
+    tok_src = lambda s: tokens.at[(3 * z + 1) // 2 if s == 0 else 1 + 3 * (z // 2)]
+    mine = [copy_here(tok_src(s), x2.at[2 * c + s]) for s in range(2)]
     here_sem = [local.at[next(local_number)] for _ in range(2)]
     here = [
         pltpu.make_async_copy(w_head, wh_at(row), here_sem[0]),
         pltpu.make_async_copy(b_head, bh, here_sem[1]),
     ]
 
+    barrier = pltpu.get_barrier_semaphore()
+    everyone = [at_c(k) for k in (1, 2, 3)] + [at_z(k) for k in (1, 2, 3)] + [at_x]
+    for device in everyone:
+        pl.semaphore_signal(barrier, inc=1, device_id=device, device_id_type=MESH)
+
+    @pl.when(c != z)
+    def _():
+        pl.semaphore_signal(barrier, inc=1, device_id=across, device_id_type=MESH)
+
+    seg2[...] = jnp.zeros_like(seg2)
+    seg2[0:1, :] = segments[pl.ds((3 * z + 1) // 2, 1), :]
+    seg2[1:2, :] = segments[pl.ds(1 + 3 * (z // 2), 1), :]
+    wide = heads * 128
+    b_head[...] = jnp.zeros_like(b_head)
+    b_unit[...] = jnp.zeros_like(b_unit)
+    qb = q_bias[...].reshape(1, heads * HEAD)
+    vb = v_bias[...].reshape(1, heads * HEAD)
+    for h in range(heads):
+        cols = slice(HEAD * h, HEAD * h + HEAD)
+        w_head[:, 128 * h : 128 * h + HEAD] = w_kinds[1, :, cols]
+        w_head[:, 128 * h + HEAD : 128 * h + 128] = w_kinds[2, :, cols]
+        b_head[0:1, 128 * h + HEAD : 128 * h + 128] = vb[:, cols]
+    w_head[:, wide:] = w_kinds[0]
+    b_head[0:1, wide:] = qb
+    b_unit[0:1, :] = in_bias[...].reshape(1, units)
+    seg_here = copy_here(seg2, seg.at[c])
+    bu_here = copy_here(b_unit, bu_full.at[z])
+
     @pl.when(c == z)
     def _():
         for copy in here:
             copy.start()
 
-    barrier = pltpu.get_barrier_semaphore()
-    everyone = [at_c(k) for k in (1, 2, 3)] + [at_z(k) for k in (1, 2, 3)] + [at_x]
-    for device in everyone:
-        pl.semaphore_signal(barrier, inc=1, device_id=device, device_id_type=MESH)
-
-    @pl.when(c != z)
-    def _():
-        pl.semaphore_signal(barrier, inc=1, device_id=across, device_id_type=MESH)
-
     pl.semaphore_wait(barrier, len(everyone) + jnp.where(c != z, 1, 0))
 
-    n_ty, n_tc, n_tf, n_wa, n_ba = (next(number) for _ in range(5))
+    n_tf, n_wa, n_ba = (next(number) for _ in range(3))
+    n_ty, n_tc = ([next(number) for _ in range(2)] for _ in range(2))
     not_here = lambda: c != z
     rc.start(n_wa, lambda: (w_head, wh_at(row), across), not_here)
     rc.start(n_ba, lambda: (b_head, bh, across), not_here)
-    rc.start(n_ty, lambda: (tok2, tok_at(c), at_c(2)))
-    rc.start(n_tc, lambda: (tok2, tok_at(c), at_c(1)))
     n_seg = four()
     for k in (1, 2, 3):
         rc.start(n_seg + k, lambda k=k: (seg2, seg.at[c], at_c(k)))
@@ -495,16 +517,23 @@
             )
 
     n_hz = four()
-    lines = (Line(lambda t: w_at(row, t)), Line(lambda t: o_at(row, t)))
-    full_at = (w_at, o_at)
-    sources = (w_src, o_src)
+    full_at = (
+        lambda r, t: w_full.at[0, r, :, t_cols(t)],
+        o_at,
+        lambda r, t: w_full.at[1, r, :, t_cols(t)],
+    )
+    sources = (w_src.at[0], o_src, w_src.at[1])
+    lines = [Line(lambda t, w=w: full_at[w](row, t)) for w in range(3)]
     n_hx = four()
-    n_x, n_y, n_d = ([four(), four()] for _ in range(3))
-    n_c = [[four(), four()] for _ in range(4)]
-
-    def pass_on(n, i, r, device, first=False):
+    n_x, n_y, n_d = ([four() for _ in range(3)] for _ in range(3))
+    n_c = [[four() for _ in range(3)] for _ in range(4)]
+
+    groups = [(0, 1), (2,)]
+    over_y = ((0, 2), (1, 1), (1, 3))
+
+    def pass_on(n, g, i, r, device, first=False):
         t = lambda: order[i]
-        for w in range(2):
+        for w in groups[g]:
             rc.start(
                 lambda w=w: n[w] + t(),
                 lambda w=w: (
@@ -516,115 +545,88 @@
                 n[w] + i,
             )
 
-    def came(n, i, r, device):
+    def came(n, g, i, r, device):
         t = order[i]
-        for w in range(2):
+        for w in groups[g]:
             rc.arrived(n[w] + t, full_at[w](r, t), device)
 
-    def dense_step(i, chips):
-        for line in lines:
-            line.step(i)
-        pass_on(n_x, i, row, to_x, True)
-        if chips:
-            dense_y(i)
-
-    def dense_y(i):
-        pass_on(n_y, i, row, to_c(2), True)
-        pass_on(n_c[0], i, row, to_c(1), True)
-
-    def from_x(i):
-        came(n_x, i, row_x, at_x)
-        if i >= 3:
-            pass_on(n_d, i, row_x, to_c(2))
-        pass_on(n_c[1], i, row_x, to_c(1))
-
-    def from_y(i):
-        came(n_y, i, row_y, at_c(2))
-        if i < 3:
-            pass_on(n_d, i, row_y, to_x)
-        pass_on(n_c[2], i, row_y, to_c(1))
-
-    def from_corner(i):
-        came(n_d, i, row_d, at_x)
-        pass_on(n_c[3], i, row_d, to_c(1))
-
-    for copy in w_here:
-        copy.wait()
-    pass_on(n_x, 0, row, to_x, True)
-    pass_on(n_y, 0, row, to_c(2), True)
-    pass_on(n_c[0], 0, row, to_c(1), True)
-    own_here = [copy_here(w_src, w_at(row, z)), copy_here(o_src, o_at(row, z))]
+    def own_send(g):
+        pass_on(n_x, g, 0, row, to_x, True)
+        pass_on(n_c[0], g, 0, row, to_c(1), True)
+
+    def line_begin(g):
+        for w in groups[g]:
+            lines[w].begin(sources[w])
+
+    def y_send(g, i):
+        pass_on(n_y, g, i, row, to_c(2), True)
+
+    def line_step(g, i):
+        for w in groups[g]:
+            lines[w].step(i)
+        pass_on(n_x, g, i, row, to_x)
+        pass_on(n_c[0], g, i, row, to_c(1))
+
+    def from_x(g, i):
+        came(n_x, g, i, row_x, at_x)
+        if (g, i) in over_y:
+            pass_on(n_d, g, i, row_x, to_c(2))
+        pass_on(n_c[1], g, i, row_x, to_c(1))
+
+    def from_y(g, i):
+        came(n_y, g, i, row_y, at_c(2))
+        if (g, i) not in over_y:
+            pass_on(n_d, g, i, row_y, to_x)
+        pass_on(n_c[2], g, i, row_y, to_c(1))
+
+    def from_corner(g, i):
+        came(n_d, g, i, row_d, at_x)
+        pass_on(n_c[3], g, i, row_d, to_c(1))
+
+    head_at = lambda t: wh_at(d * nc + t)
     n_bu = four()
-    for k in (1, 2, 3):
-        rc.start(n_bu + k, lambda k=k: (b_unit, bu_full.at[z], at_z(k)))
-
-    @pl.when(c != z)
-    def _():
-        rc.arrived(n_wa, wh_at(d * nc + z), across)
-        rc.arrived(n_ba, bh, across)
-
-    @pl.when(c == z)
-    def _():
-        for copy in here:
-            copy.wait()
-
-    head_at = lambda t: wh_at(d * nc + t)
-    for k in (1, 2, 3):
-        rc.start(n_hz + k, lambda k=k: (head_at(z), head_at(z), at_z(k)))
-    rc.start(n_hx, lambda: (head_at(z), head_at(z), at_x))
-    for line, src in zip(lines, sources):
-        line.begin(src)
-    q_scr[...] = jnp.zeros_like(q_scr)
-    for k in (1, 2, 3):
+    n_ctx = four()
+    ctx_at = lambda i: context.at[pl.ds(pl.multiple_of(i * own, 128), own)]
+
+    def head_send():
+        @pl.when(c != z)
+        def _():
+            rc.arrived(n_wa, wh_at(d * nc + z), across)
+            rc.arrived(n_ba, bh, across)
+
+        @pl.when(c == z)
+        def _():
+            for copy in here:
+                copy.wait()
+
+        for k in (1, 2, 3):
+            rc.start(n_hz + k, lambda k=k: (head_at(z), head_at(z), at_z(k)))
+        rc.start(n_hx, lambda: (head_at(z), head_at(z), at_x))
+        for k in (1, 2, 3):
+            rc.start(n_bu + k, lambda k=k: (b_unit, bu_full.at[z], at_z(k)))
+
+    def head_pass(k):
         rc.arrived(n_hz + k, head_at(z ^ k), at_z(k))
-        rc.start(n_hx + k, lambda k=k: (head_at(z ^ k), head_at(z ^ k), at_x))
-    dense_step(1, True)
-    for k in (1, 2, 3):
-        rc.arrived(n_seg + k, seg.at[c ^ k], at_c(k))
-    seg_here.wait()
-    for i in range(nc):
+        rc.start(n_hx + k, lambda: (head_at(z ^ k), head_at(z ^ k), at_x))
+
+    def token_pass():
         for s in range(2):
-            line = seg[i, s : s + 1, :].astype(F32)
-            segr[2 * i + s, 0:1, :] = line
-            segc[2 * i + s] = jnp.broadcast_to(line, (128, ln)).T
-    rc.arrived(n_ty, tok_at(c ^ 2), at_c(2))
-    rc.start(n_tf, lambda: (tok_at(c ^ 2), tok_at(c ^ 2), at_c(1)))
-    dense_step(2, True)
-    for t in range(4):
-        rc.arrived(n_hx + t, wh_at((1 - d) * nc + (z ^ t)), at_x)
-    mine.wait()
-    rc.arrived(n_tc, tok_at(c ^ 1), at_c(1))
-    rc.arrived(n_tf, tok_at(c ^ 3), at_c(1))
-    wh_here = copy_here(wh, wh_out)
-    wide = heads * 128
-
-    @pl.loop(0, 2 * nc)
-    def _(i):
-        x = x2[i]
-        rows = pl.ds(pl.multiple_of(i * ln, ln), ln)
-        xt[:, rows] = x.T
-        got = (dot_nn(x, wh[:, :wide]) + bh[0:1, :wide]).astype(BF)
-        kv[rows, :] = got
-        qp = ((dot_nn(x, wh[:, wide:]) + bh[0:1, wide:]).astype(BF).astype(F32) * 0.125).astype(BF)
-        for h in range(heads):
-            q_scr[rows, 128 * h : 128 * h + HEAD] = qp[:, HEAD * h : HEAD * h + HEAD]
-
-    x_here = copy_here(xt, xt_out)
-    q_here = copy_here(q_scr, q_out)
-    kv_here = copy_here(kv, kv_out)
-    dense_step(3, True)
-    from_x(0)
-
-    @pl.loop(0, nc)
-    def _(j):
-        for s in range(2):
-            rows = pl.ds(pl.multiple_of((2 * j + s) * ln, ln), ln)
-            for h in range(heads):
-                kvt[s * heads + h, :, pl.ds(pl.multiple_of(j * ln, ln), ln)] = kv[
-                    rows, 128 * h : 128 * h + 128
-                ].T
-
-    from_x(1)
+            rc.arrived(n_ty[s], x2.at[2 * (c ^ 2) + s], at_c(2))
+        rc.start(n_tf, lambda: (tok_at(c ^ 2), tok_at(c ^ 2), at_c(1)))
+
+    def context_send():
+        for k in (2, 3, 1):
+            rc.start(n_ctx + k, lambda k=k: (ctx_at(c ^ k), ctx_all.at[c], at_c(k)))
+
+    def segments_done():
+        for k in (1, 2, 3):
+            rc.arrived(n_seg + k, seg.at[c ^ k], at_c(k))
+        seg_here.wait()
+        for i in range(nc):
+            for s in range(2):
+                line = seg[i, s : s + 1, :].astype(F32)
+                segr[2 * i + s, 0:1, :] = line
+                segc[2 * i + s] = jnp.broadcast_to(line, (128, ln)).T
 
     def block(qb):
         r0, r1, o0, o1, seq = block_rows(qb, half, ln)
@@ -682,44 +684,128 @@
         context[pl.ds(o0, hl), :] = turned[:hl]
         context[pl.ds(o1, hl), :] = turned[hl:]
 
+    for copy in w_here:
+        copy.wait()
+    own_here = [
+        copy_here(sources[w], full_at[w](row, z)) for w in range(3)
+    ]
+    q_scr[...] = jnp.zeros_like(q_scr)
+    y_send(1, 0)
+    own_send(0)
+    line_begin(1)
+    for s in range(2):
+        rc.start(n_ty[s], lambda s=s: (tok_src(s), x2.at[2 * c + s], at_c(2)))
+        rc.start(n_tc[s], lambda s=s: (tok_src(s), x2.at[2 * c + s], at_c(1)))
+    line_begin(0)
+    head_send()
+    line_step(0, 1)
+    y_send(0, 0)
+    line_step(1, 1)
+    y_send(0, 1)
+    head_pass(2)
+    head_pass(1)
+    head_pass(3)
+    line_step(0, 2)
+    segments_done()
+    token_pass()
+    y_send(0, 2)
+    own_send(1)
+    line_step(1, 2)
+    y_send(1, 1)
+    from_y(1, 0)
+    for t in range(4):
+        rc.arrived(n_hx + t, wh_at((1 - d) * nc + (z ^ t)), at_x)
+    for s in range(2):
+        mine[s].wait()
+        rc.arrived(n_tc[s], x2.at[2 * (c ^ 1) + s], at_c(1))
+    rc.arrived(n_tf, tok_at(c ^ 3), at_c(1))
+    wh_here = copy_here(wh, wh_out)
+
+    @pl.loop(0, 2 * nc)
+    def _(i):
+        x = x2[i]
+        rows = pl.ds(pl.multiple_of(i * ln, ln), ln)
+        xt[:, rows] = x.T
+        got = (dot_nn(x, wh[:, :wide]) + bh[0:1, :wide]).astype(BF)
+        kv[rows, :] = got
+        qp = ((dot_nn(x, wh[:, wide:]) + bh[0:1, wide:]).astype(BF).astype(F32) * 0.125).astype(BF)
+        for h in range(heads):
+            q_scr[rows, 128 * h : 128 * h + HEAD] = qp[:, HEAD * h : HEAD * h + HEAD]
+
+    x_here = copy_here(xt, xt_out)
+    q_here = copy_here(q_scr, q_out)
+    kv_here = copy_here(kv, kv_out)
+    y_send(1, 2)
+    line_step(1, 3)
+    from_x(0, 2)
+    @pl.loop(0, nc)
+    def _(j):
+        for s in range(2):
+            rows = pl.ds(pl.multiple_of((2 * j + s) * ln, ln), ln)
+            for h in range(heads):
+                kvt[s * heads + h, :, pl.ds(pl.multiple_of(j * ln, ln), ln)] = kv[
+                    rows, 128 * h : 128 * h + 128
+                ].T
+
+    from_x(0, 1)
+    line_step(0, 3)
+    y_send(0, 3)
+    y_send(1, 3)
+    from_x(0, 0)
+
     @pl.loop(0, 6)
     def _(qb):
         block(qb)
 
         @pl.when(qb == 1)
         def _():
-            from_y(0)
+            from_y(0, 0)
+            from_x(1, 2)
+            from_x(1, 1)
+
+        @pl.when(qb == 2)
+        def _():
+            from_y(0, 2)
+            from_y(0, 1)
 
         @pl.when(qb == 3)
         def _():
-            from_x(2)
-            from_y(1)
-
-    n_ctx = four()
-    ctx_at = lambda i: context.at[pl.ds(pl.multiple_of(i * own, 128), own)]
-    for k in (1, 2, 3):
-        rc.start(n_ctx + k, lambda k=k: (ctx_at(c ^ k), ctx_all.at[c], at_c(k)))
+            from_x(1, 3)
+
+        @pl.when(qb == 4)
+        def _():
+            from_corner(0, 0)
+            from_y(1, 2)
+
+    context_send()
     ctx_here = copy_here(ctx_at(c), ctx_all.at[c])
-    from_x(3)
-    from_y(2)
-    from_corner(0)
-    from_corner(1)
+    from_y(1, 1)
+    from_x(0, 3)
+    from_y(0, 3)
+    from_x(1, 0)
+    from_corner(0, 2)
+    from_y(1, 3)
+    from_corner(1, 3)
+    from_corner(1, 0)
+    from_corner(1, 2)
+    from_corner(1, 1)
+    from_corner(0, 1)
+    from_corner(0, 3)
     for k in (1, 2, 3):
         rc.arrived(n_ctx + k, ctx_all.at[c ^ k], at_c(k))
-        rc.arrived(n_bu + k, bu_full.at[z ^ k], at_z(k))
-    from_y(3)
-    from_corner(2)
-    from_corner(3)
     for n, r in zip(n_c, (row, row_x, row_y, row_d)):
         for i in range(4):
-            came(n, i, r ^ 1, at_c(1))
+            for g in range(len(groups)):
+                came(n, g, i, r ^ 1, at_c(1))
+    for k in (1, 2, 3):
+        rc.arrived(n_bu + k, bu_full.at[z ^ k], at_z(k))
     for copy in own_here + [bu_here, x_here, wh_here, q_here, kv_here, ctx_here]:
         copy.wait()
     rc.all_sent()
 
 
-def forward(tok2, seg2, w_head, b_head, b_unit, w_o, w_i, w_b, heads):
-    ln, width = tok2.shape[1:]
+def forward(tokens, segments, w_kinds, q_bias, v_bias, in_bias, w_o, w_i, w_b, heads):
+    ln, width = tokens.shape[1:]
     wr, units = w_i.shape
     group = w_o.shape[1]
     nc, nt, nr = 4, 4, 8
@@ -742,7 +828,7 @@
             sds((group, rows), F32),
             sds((nc, 8, ln), jnp.int32),
         ),
-        in_specs=[hb] * 4 + [vm] + [hb] * 3,
+        in_specs=[hb] + [vm] * 5 + [hb] * 3,
         out_specs=(hb,) * 8 + (vm,) * 3,
         scratch_shapes=[
             pltpu.VMEM((2 * nc, ln, width), BF),
@@ -759,15 +845,19 @@
             pltpu.VMEM((rows, group), BF),
             pltpu.VMEM((2, wr, units), BF),
             pltpu.VMEM((wr, group), BF),
-            pltpu.SemaphoreType.DMA((120,)),
-            pltpu.SemaphoreType.DMA((120,)),
+            pltpu.VMEM((8, ln), jnp.int32),
+            pltpu.VMEM((wr, 3 * group), BF),
+            pltpu.VMEM((8, 3 * group), F32),
+            pltpu.VMEM((8, units), F32),
+            pltpu.SemaphoreType.DMA((140,)),
+            pltpu.SemaphoreType.DMA((140,)),
             pltpu.SemaphoreType.DMA((32,)),
         ],
         compiler_params=pltpu.CompilerParams(
             vmem_limit_bytes=60 << 20, collective_id=0, has_side_effects=True
         ),
         name="forward",
-    )(tok2, seg2, w_head, b_head, b_unit, w_o, w_i, w_b)
+    )(tokens, segments, w_kinds, q_bias, v_bias, in_bias, w_o, w_i, w_b)
 
 
 def middle_kernel(
@@ -778,7 +868,12 @@
     w_o,
     w_ib,
     b_in,
-    vectors,
+    out_bias,
+    gain_one,
+    shift_one,
+    back_bias,
+    gain_two,
+    shift_two,
     d_ctx,
     g_b,
     g_i,
@@ -815,9 +910,10 @@
     blocks, _, group = ctx_all.shape
     width = x_own.shape[1]
     units = w_v.shape[2] // 4
-    step = 32
+    step, thin = 128, 64
     out_bias, gain_one, shift_one, back_bias, gain_two, shift_two = (
-        vectors.at[pl.ds(i, 1)] for i in range(6)
+        a[...].reshape(1, width)
+        for a in (out_bias, gain_one, shift_one, back_bias, gain_two, shift_two)
     )
     half_rows = pl.ds(pl.multiple_of((z % 2) * hl, 128), hl)
     first_rows = []
@@ -846,10 +942,10 @@
     for copy in first_rows:
         copy.wait()
 
-    def chunks(body):
-        @pl.loop(0, own // step)
+    def chunks(body, size=step):
+        @pl.loop(0, own // size)
         def _(i):
-            body(pl.ds(pl.multiple_of(i * step, step), step))
+            body(pl.ds(pl.multiple_of(i * size, size), size))
 
     mean = lambda v: jnp.mean(v, -1, keepdims=True)
     add = lambda i, v: small.__setitem__(
@@ -862,16 +958,16 @@
         tmp[...] += dot_nt(ctx_v[g], w_ov[g])
 
     def norm_one(r):
-        value = x_own[r, :].astype(F32) + (tmp[r, :] + out_bias[...])
+        value = x_own[r, :].astype(F32) + (tmp[r, :] + out_bias)
         centered = value - mean(value)
         rstd = lax.rsqrt(mean(centered * centered) + 1e-12)
         normal = centered * rstd
         n_one[r, :] = normal
         r_one[r, :] = jnp.broadcast_to(rstd, (step, 128))
-        got = normal * gain_one[...] + shift_one[...]
+        got = normal * gain_one + shift_one
         normed[r, :] = got
         low[r, :] = got.astype(BF)
-        acc[r, :] = got + back_bias[...]
+        acc[r, :] = got + back_bias
 
     chunks(norm_one)
     low_t[...] = low[...].T
@@ -890,7 +986,7 @@
                 1.0 / math.sqrt(2.0 * math.pi)
             )
 
-        chunks(gelu)
+        chunks(gelu, thin)
         acc[...] += dot_nt(active[:, t_cols(t)], w_v[1, :, t_cols(t)])
 
     def norm_two(r):
@@ -898,11 +994,11 @@
         centered = value - mean(value)
         rstd = lax.rsqrt(mean(centered * centered) + 1e-12)
         normal = centered * rstd
-        out_low[r, :] = (normal * gain_two[...] + shift_two[...]).astype(BF)
+        out_low[r, :] = (normal * gain_two + shift_two).astype(BF)
         grad = c_own[r, :].astype(F32)
         add(4, grad * normal)
         add(5, grad)
-        scaled = grad * gain_two[...]
+        scaled = grad * gain_two
         got = rstd * (scaled - mean(scaled) - normal * mean(scaled * normal))
         d_sec[r, :] = got
         add(3, got)
@@ -924,7 +1020,7 @@
             small[at, :] += jnp.sum(got, 0, keepdims=True)
             active[r, t_cols(t)] = got.astype(BF)
 
-        chunks(inner_back)
+        chunks(inner_back, thin)
         gi_v[:, t_cols(t)] = dot_nn(low_t[...], active[:, t_cols(t)]).astype(BF)
         pltpu.make_async_copy(gi_v.at[:, t_cols(t)], g_i.at[:, t_cols(t)], g_sem.at[1, t]).start()
         acc[...] += dot_nt(active[:, t_cols(t)], w_v[0, :, t_cols(t)])
@@ -934,7 +1030,7 @@
         normal = n_one[r, :]
         add(1, grad * normal)
         add(2, grad)
-        scaled = grad * gain_one[...]
+        scaled = grad * gain_one
         got = r_one[r, 0:1] * (scaled - mean(scaled) - normal * mean(scaled * normal))
         d_first[r, :] = got
         add(0, got)
@@ -969,7 +1065,7 @@
             sds((own, width), F32),
             sds((16, width), F32),
         ),
-        in_specs=[hb] * 5 + [vm] * 2,
+        in_specs=[hb] * 5 + [vm] * 7,
         out_specs=(vm, hb, hb, vm, vm, vm, vm),
         scratch_shapes=[
             v((own, width), BF),
@@ -1002,7 +1098,7 @@
             transcendentals=2 * own * all_units,
         ),
         name="middle",
-    )(tokens, cotangent, ctx_all, w_o, w_ib, b_in, vectors)
+    )(tokens, cotangent, ctx_all, w_o, w_ib, b_in, *vectors)
 
 
 def add_into(dst, other, rows):
@@ -1922,18 +2018,23 @@
             0,
         )
 
-    tok2 = own_pair(tokens)
-    seg2 = jnp.concatenate([own_pair(segments), jnp.zeros((6, ln), jnp.int32)], 0)
-    w_head = head_order([w_qkv[:, i] for i in range(3)], heads)
-    b_head = head_order([q_bias, jnp.zeros_like(q_bias), v_bias], heads)
-    b_head = jnp.broadcast_to(b_head[None], (8, 3 * group))
-    b_unit = jnp.broadcast_to(in_bias[None], (8, units))
-    args = (tok2, seg2, w_head, b_head, b_unit, w_out, w_in, w_back, heads)
-    got = forward(*args) if sizes == (2, 4, 4) else forward_plain(sizes, me, *args)
+    w_kinds = jnp.transpose(w_qkv, (1, 0, 2))
+    biases = (q_bias, v_bias, in_bias)
+    weights = (w_out, w_in, w_back)
+    if sizes == (2, 4, 4):
+        got = forward(tokens, segments, w_kinds, *biases, *weights, heads)
+    else:
+        tok2 = own_pair(tokens)
+        seg2 = jnp.concatenate([own_pair(segments), jnp.zeros((6, ln), jnp.int32)], 0)
+        w_head = head_order(w_kinds, heads)
+        b_head = head_order([q_bias, jnp.zeros_like(q_bias), v_bias], heads)
+        b_head = jnp.broadcast_to(b_head[None], (8, 3 * group))
+        b_unit = jnp.broadcast_to(in_bias[None], (8, units))
+        got = forward_plain(sizes, me, tok2, seg2, w_head, b_head, b_unit, *weights, heads)
     ctx_all, xt, q, kv, wh, w_o, w_ib, b_in, lse, ctx_t, seg_all = got
     w_o = w_o.reshape(nt, width, group)
     w_ib = w_ib.reshape(2, width, nt * units)
-    vectors = jnp.stack([out_bias, gain_one, shift_one, back_bias, gain_two, shift_two])
+    vectors = (out_bias, gain_one, shift_one, back_bias, gain_two, shift_two)
     d_ctx, g_b, g_i, g_o, out_low, d_first, small = middle(
         tokens, cotangent, ctx_all, w_o, w_ib, b_in, vectors
     )

time: 273 us -> 247 us (0.905)
  Pallas kernels: 256 us -> 245 us
  local copies, waits for them, and re-layouts: 12.5 us -> 1.77 us
  other arithmetic: 3 us -> 0 us
    pallas_call x1, Pallas kernels: 38.6 us -> 33.2 us  [middle(): pl.pallas_call(functools.partial(middle_kernel, ln), out_shape=(sds((bloc...]
    another operation x7 -> x0, local copies, waits for them, and re-layouts: 4.77 us -> none  [per_device(): jnp.stack([out_bias, gain_one, shift_one, back_bias, gain_two, shift_two])]
    pallas_call x1, Pallas kernels: 85.2 us -> 82.1 us  [forward(): pl.pallas_call(functools.partial(forward_kernel, heads, ln), out_shape=(s...]
    pallas_call x1, Pallas kernels: 125 us -> 122 us  [backward(): pl.pallas_call(functools.partial(backward_kernel, heads, ln), out_shape=(...]
where the time goes in v5:
time: 247 us
  Pallas kernels  245 us (99%)
    pallas_call x1, Pallas kernels, backward(): pl.pallas_call(functools.partial(backward_kernel, heads, ln), out_shape=(...  122 us
    pallas_call x1, Pallas kernels, forward(): pl.pallas_call(functools.partial(forward_kernel, heads, ln), out_shape=(s...  82.1 us
    pallas_call x1, Pallas kernels, middle(): pl.pallas_call(functools.partial(middle_kernel, ln), out_shape=(sds((bloc...  33.2 us
    pallas_call x1, Pallas kernels, finish(): pl.pallas_call(functools.partial(finish_kernel, heads), grid=(seqs,), out...  7.29 us

profile of v5, /device:TPU:0, one launch (start us, length us, event | category | flops | bytes accessed | tf_op | source)
XLA Modules:
  0.0 247.1 jit_solution(11727878775985442653)
XLA Ops:
  0.6 82.1 %forward.1 = (bf16[4,384,192]{2,1,0:T(8,128)(2,1)}, bf16[768,2048]{1,0:T(8,128)(2,1)}, bf16[2048,384]{1,0:T(8,128)(2,1)}, bf16[2048,384]{1,0:T(8,128)(2,1)}, bf1...) custom-call(bf16[6,256,768]{2,1,0:T(8,128)(2,1)} %tokens.3, ...), custom_call_target="tpu_custom_call" | custom-call | tf_op jit(solution)/shard_map/forward/pallas_call | solution.py:816
  82.7 33.2 %middle.1 = (bf16[4,384,192]{2,1,0:T(8,128)(2,1)}, bf16[768,3072]{1,0:T(8,128)(2,1)}, bf16[768,3072]{1,0:T(8,128)(2,1)}, bf16[4,768,192]{2,1,0:T(8,128)(2,1)}, b...) custom-call(bf16[6,256,768]{2,1,0:T(8,128)(2,1)} %tokens.3, bf16[6,256,768]{2,1,0:T(8,128)(2,1)} %cotangent.1, ...), custom_call_target="tpu_custom_call" | custom-call | flops 12230590464 | bytes 25165824 | tf_op jit(solution)/shard_map/middle/pallas_call | solution.py:1057
  116.0 122.1 %backward.1 = (bf16[6,256,768]{2,1,0:T(8,128)(2,1)}, bf16[6,256,768]{2,1,0:T(8,128)(2,1)}, f32[96,768]{1,0:T(8,128)}, f32[96,768]{1,0:T(8,128)}, f32[96,192]{1,0...) custom-call(bf16[4,384,192]{2,1,0:T(8,128)(2,1)} %get-tuple-element.60.d_ctx, ...), custom_call_target="tpu_custom_call" | custom-call | tf_op jit(solution)/shard_map/backward/pallas_call | solution.py:1737
  238.0 7.3 %finish.1 = (f32[6,256,768]{2,1,0:T(8,128)}, bf16[6,256,768]{2,1,0:T(8,128)(2,1)}, f32[96,768]{1,0:T(8,128)}, f32[96,768]{1,0:T(8,128)}, f32[96,192]{1,0:T(8,128...) custom-call(bf16[6,256,768]{2,1,0:T(8,128)(2,1)} %get-tuple-element., ...), custom_call_target="tpu_custom_call" | custom-call | tf_op jit(solution)/shard_map/finish/pallas_call | solution.py:1846
  245.3 1.8 copy.31

commit v6 on v5

--- a/solution.py
+++ b/solution.py
@@ -366,17 +366,27 @@
     w_o,
     w_i,
     w_b,
-    ctx_all,
+    cotangent,
+    out_bias,
+    gain_one,
+    shift_one,
+    back_bias,
+    gain_two,
+    shift_two,
     xt_out,
     q_out,
     kv_out,
     wh_out,
-    o_full,
-    w_full,
-    bu_full,
+    g_b,
+    g_i,
+    output,
     lse,
     ctx_t,
     seg,
+    d_ctx,
+    g_o,
+    d_first,
+    small,
     x2,
     xt,
     wh,
@@ -395,6 +405,26 @@
     w_head,
     b_head,
     b_unit,
+    ctx_all,
+    o_full,
+    w_full,
+    bu_full,
+    x_own,
+    c_own,
+    n_one,
+    r_one,
+    low,
+    low_t,
+    tmp,
+    total,
+    active,
+    slope,
+    turn,
+    d_low,
+    gb_v,
+    gi_v,
+    out_low,
+    g_sem,
     send,
     recv,
     local,
@@ -433,6 +463,15 @@
     w_here = [copy_here(w_i, w_src.at[0]), copy_here(w_b, w_src.at[1]), copy_here(w_o, o_src)]
     tok_src = lambda s: tokens.at[(3 * z + 1) // 2 if s == 0 else 1 + 3 * (z // 2)]
     mine = [copy_here(tok_src(s), x2.at[2 * c + s]) for s in range(2)]
+    half_rows = pl.ds(pl.multiple_of(half * hl, 128), hl)
+    own_rows = [
+        copy_here(part, dst)
+        for src, to in ((tokens, x_own), (cotangent, c_own))
+        for part, dst in (
+            (src.at[(3 * z + 1) // 2], to.at[pl.ds(0, ln)]),
+            (src.at[1 + 3 * (z // 2), half_rows], to.at[pl.ds(ln, hl)]),
+        )
+    ]
     here_sem = [local.at[next(local_number)] for _ in range(2)]
     here = [
         pltpu.make_async_copy(w_head, wh_at(row), here_sem[0]),
@@ -529,7 +568,7 @@
     n_c = [[four() for _ in range(3)] for _ in range(4)]
 
     groups = [(0, 1), (2,)]
-    over_y = ((0, 2), (1, 1), (1, 3))
+    over_y = ((0, 1), (0, 3), (1, 1), (1, 2))
 
     def pass_on(n, g, i, r, device, first=False):
         t = lambda: order[i]
@@ -627,6 +666,26 @@
                 line = seg[i, s : s + 1, :].astype(F32)
                 segr[2 * i + s, 0:1, :] = line
                 segc[2 * i + s] = jnp.broadcast_to(line, (128, ln)).T
+
+    step, thin = 128, 64
+    width = x_own.shape[1]
+    w_of = lambda which, t: w_full[which, :, :, t_cols(t)].reshape(width, units)
+    w_out_of = lambda g: o_full[g].reshape(width, w_o.shape[1])
+    out_bias, gain_one, shift_one, back_bias, gain_two, shift_two = (
+        a[...].reshape(1, width)
+        for a in (out_bias, gain_one, shift_one, back_bias, gain_two, shift_two)
+    )
+
+    def chunks(body, size=step):
+        @pl.loop(0, own // size)
+        def _(i):
+            body(pl.ds(pl.multiple_of(i * size, size), size))
+
+    mean = lambda v: jnp.mean(v, -1, keepdims=True)
+    add = lambda i, v: small.__setitem__(
+        (slice(i, i + 1), slice(None)), small[i : i + 1, :] + jnp.sum(v, 0, keepdims=True)
+    )
+    small[...] = jnp.zeros_like(small)
 
     def block(qb):
         r0, r1, o0, o1, seq = block_rows(qb, half, ln)
@@ -674,7 +733,7 @@
         )
         whole = []
         for h in range(heads):
-            one = acc[h, HEAD:, :] / sums[h]
+            one = acc[h] / sums[h]
             whole.append(one)
             line = peaks[h] + jnp.log(sums[h])
             for part, at in ((0, o0), (hl, o1)):
@@ -690,29 +749,32 @@
         copy_here(sources[w], full_at[w](row, z)) for w in range(3)
     ]
     q_scr[...] = jnp.zeros_like(q_scr)
-    y_send(1, 0)
-    own_send(0)
-    line_begin(1)
+    line_begin(0)
     for s in range(2):
         rc.start(n_ty[s], lambda s=s: (tok_src(s), x2.at[2 * c + s], at_c(2)))
         rc.start(n_tc[s], lambda s=s: (tok_src(s), x2.at[2 * c + s], at_c(1)))
-    line_begin(0)
+    y_send(0, 0)
+    line_step(0, 1)
+    line_step(0, 2)
     head_send()
-    line_step(0, 1)
-    y_send(0, 0)
-    line_step(1, 1)
-    y_send(0, 1)
+    head_pass(1)
+    line_begin(1)
+    head_pass(3)
+    y_send(1, 0)
     head_pass(2)
-    head_pass(1)
-    head_pass(3)
-    line_step(0, 2)
     segments_done()
     token_pass()
+    y_send(0, 1)
+    own_send(0)
     y_send(0, 2)
+    line_step(0, 3)
+    from_x(0, 1)
     own_send(1)
-    line_step(1, 2)
+    y_send(0, 3)
+    line_step(1, 1)
     y_send(1, 1)
-    from_y(1, 0)
+    from_x(0, 2)
+    from_y(0, 0)
     for t in range(4):
         rc.arrived(n_hx + t, wh_at((1 - d) * nc + (z ^ t)), at_x)
     for s in range(2):
@@ -735,9 +797,7 @@
     x_here = copy_here(xt, xt_out)
     q_here = copy_here(q_scr, q_out)
     kv_here = copy_here(kv, kv_out)
-    y_send(1, 2)
-    line_step(1, 3)
-    from_x(0, 2)
+    line_step(1, 2)
     @pl.loop(0, nc)
     def _(j):
         for s in range(2):
@@ -745,91 +805,220 @@
             for h in range(heads):
                 kvt[s * heads + h, :, pl.ds(pl.multiple_of(j * ln, ln), ln)] = kv[
                     rows, 128 * h : 128 * h + 128
-                ].T
-
-    from_x(0, 1)
-    line_step(0, 3)
-    y_send(0, 3)
-    y_send(1, 3)
-    from_x(0, 0)
+                ].T[HEAD:]
+
+    from_x(0, 3)
 
     @pl.loop(0, 6)
     def _(qb):
         block(qb)
 
-        @pl.when(qb == 1)
+        @pl.when(qb == 0)
         def _():
-            from_y(0, 0)
-            from_x(1, 2)
-            from_x(1, 1)
-
-        @pl.when(qb == 2)
-        def _():
-            from_y(0, 2)
-            from_y(0, 1)
-
-        @pl.when(qb == 3)
-        def _():
-            from_x(1, 3)
-
-        @pl.when(qb == 4)
-        def _():
-            from_corner(0, 0)
-            from_y(1, 2)
+            line_step(1, 3)
+            y_send(1, 3)
 
     context_send()
     ctx_here = copy_here(ctx_at(c), ctx_all.at[c])
+    y_send(1, 2)
+    from_y(0, 2)
+    from_x(0, 0)
+    from_corner(0, 0)
+    from_x(1, 1)
+    from_y(0, 3)
     from_y(1, 1)
-    from_x(0, 3)
-    from_y(0, 3)
+    from_y(1, 0)
+    from_x(1, 3)
+    from_y(0, 1)
+    from_y(1, 3)
+    from_corner(0, 2)
+    from_corner(0, 3)
+    from_corner(0, 1)
+    from_x(1, 2)
     from_x(1, 0)
-    from_corner(0, 2)
-    from_y(1, 3)
-    from_corner(1, 3)
-    from_corner(1, 0)
-    from_corner(1, 2)
-    from_corner(1, 1)
-    from_corner(0, 1)
-    from_corner(0, 3)
     for k in (1, 2, 3):
         rc.arrived(n_ctx + k, ctx_all.at[c ^ k], at_c(k))
     for n, r in zip(n_c, (row, row_x, row_y, row_d)):
         for i in range(4):
-            for g in range(len(groups)):
-                came(n, g, i, r ^ 1, at_c(1))
+            came(n, 0, i, r ^ 1, at_c(1))
+    for copy in own_here + [ctx_here, bu_here] + own_rows:
+        copy.wait()
     for k in (1, 2, 3):
         rc.arrived(n_bu + k, bu_full.at[z ^ k], at_z(k))
-    for copy in own_here + [bu_here, x_here, wh_here, q_here, kv_here, ctx_here]:
+
+    tmp[...] = dot_nt(ctx_all[0], w_out_of(0))
+    for g in range(1, nc):
+        tmp[...] += dot_nt(ctx_all[g], w_out_of(g))
+
+    def norm_one(r):
+        value = x_own[r, :].astype(F32) + (tmp[r, :] + out_bias)
+        centered = value - mean(value)
+        rstd = lax.rsqrt(mean(centered * centered) + 1e-12)
+        normal = centered * rstd
+        n_one[r, :] = normal
+        r_one[r, :] = jnp.broadcast_to(rstd, (step, 128))
+        got = normal * gain_one + shift_one
+        low[r, :] = got.astype(BF)
+        total[r, :] = got + back_bias
+
+    chunks(norm_one)
+    low_t[...] = low[...].T
+
+    from_corner(1, 3)
+    @pl.loop(0, 4)
+    def _(t):
+        tmp[...] = dot_nn(low[...], w_of(0, t)) + bu_full[pl.ds(t, 1), 0, :]
+
+        def gelu(r):
+            u = tmp[r, :]
+            cdf = 0.5 * (1.0 + lax.erf(u * math.sqrt(0.5)))
+            active[r, t_cols(t)] = (u * cdf).astype(BF)
+            slope[r, t_cols(t)] = cdf + u * jnp.exp(-0.5 * u * u) * (
+                1.0 / math.sqrt(2.0 * math.pi)
+            )
+
+        chunks(gelu, thin)
+
+        @pl.when(t == 0)
+        def _():
+            from_corner(1, 1)
+            from_y(1, 2)
+
+        @pl.when(t == 1)
+        def _():
+            from_corner(1, 0)
+            from_corner(1, 2)
+
+    for n, r in zip(n_c, (row, row_x, row_y, row_d)):
+        for i in range(4):
+            came(n, 1, i, r ^ 1, at_c(1))
+
+    @pl.loop(0, 4)
+    def _(t):
+        total[...] += dot_nt(active[:, t_cols(t)], w_of(1, t))
+
+    def norm_two(r):
+        value = total[r, :]
+        centered = value - mean(value)
+        rstd = lax.rsqrt(mean(centered * centered) + 1e-12)
+        normal = centered * rstd
+        out_low[r, :] = (normal * gain_two + shift_two).astype(BF)
+        grad = c_own[r, :].astype(F32)
+        add(4, grad * normal)
+        add(5, grad)
+        scaled = grad * gain_two
+        got = rstd * (scaled - mean(scaled) - normal * mean(scaled * normal))
+        add(3, got)
+        d_low[r, :] = got.astype(BF)
+        total[r, :] = got
+
+    chunks(norm_two)
+    whole_at = lambda t: output.at[(3 * t + 1) // 2]
+    shared_at = lambda t: output.at[
+        1 + 3 * (t // 2), pl.ds(pl.multiple_of((t % 2) * hl, 128), hl)
+    ]
+    pieces = ((whole_at, out_low.at[pl.ds(0, ln)]), (shared_at, out_low.at[pl.ds(ln, hl)]))
+    n_out = four()
+    out_here = [copy_here(src, at(z)) for at, src in pieces]
+    for k, (at, src) in enumerate(pieces):
+        rc.start(
+            n_out + 2 * k,
+            lambda at=at, src=src: (src, at(z), (d, c, z + 1)),
+            lambda: z < 3,
+        )
+        rc.start(
+            n_out + 2 * k + 1,
+            lambda at=at, src=src: (src, at(z), (d, c, z - 1)),
+            lambda: z > 0,
+        )
+    turn[...] = d_low[...].T
+
+    @pl.loop(0, 4)
+    def _(t):
+        gb_v[:, t_cols(t)] = dot_nn(turn[...], active[:, t_cols(t)]).astype(BF)
+        pltpu.make_async_copy(gb_v.at[:, t_cols(t)], g_b.at[:, t_cols(t)], g_sem.at[0, t]).start()
+        tmp[...] = dot_nn(d_low[...], w_of(1, t))
+
+        def inner_back(r):
+            got = tmp[r, :] * slope[r, t_cols(t)]
+            at = pl.ds(6 + t, 1)
+            small[at, :] += jnp.sum(got, 0, keepdims=True)
+            active[r, t_cols(t)] = got.astype(BF)
+
+        chunks(inner_back, thin)
+        gi_v[:, t_cols(t)] = dot_nn(low_t[...], active[:, t_cols(t)]).astype(BF)
+        pltpu.make_async_copy(gi_v.at[:, t_cols(t)], g_i.at[:, t_cols(t)], g_sem.at[1, t]).start()
+        total[...] += dot_nt(active[:, t_cols(t)], w_of(0, t))
+
+    def norm_one_back(r):
+        grad = total[r, :]
+        normal = n_one[r, :]
+        add(1, grad * normal)
+        add(2, grad)
+        scaled = grad * gain_one
+        got = r_one[r, 0:1] * (scaled - mean(scaled) - normal * mean(scaled * normal))
+        d_first[r, :] = got
+        add(0, got)
+        d_low[r, :] = got.astype(BF)
+
+    chunks(norm_one_back)
+    turn[...] = d_low[...].T
+    for g in range(nc):
+        d_ctx[g] = dot_nn(d_low[...], w_out_of(g)).astype(BF)
+        g_o[g] = dot_nn(turn[...], ctx_all[g]).astype(BF)
+    for t in range(4):
+        pltpu.make_async_copy(gb_v.at[:, t_cols(t)], g_b.at[:, t_cols(t)], g_sem.at[0, t]).wait()
+        pltpu.make_async_copy(gi_v.at[:, t_cols(t)], g_i.at[:, t_cols(t)], g_sem.at[1, t]).wait()
+    for copy in (x_here, wh_here, q_here, kv_here):
         copy.wait()
+    for copy in out_here:
+        copy.wait()
+
+    @pl.when(z > 0)
+    def _():
+        for k, (at, _) in enumerate(pieces):
+            rc.arrived(n_out + 2 * k, at(z - 1), at_z(1))
+
+    @pl.when(z < 3)
+    def _():
+        for k, (at, _) in enumerate(pieces):
+            rc.arrived(n_out + 2 * k + 1, at(z + 1), at_z(1))
+
     rc.all_sent()
 
 
-def forward(tokens, segments, w_kinds, q_bias, v_bias, in_bias, w_o, w_i, w_b, heads):
+def forward(
+    tokens, segments, w_kinds, q_bias, v_bias, in_bias, w_o, w_i, w_b, cotangent, vectors, heads
+):
     ln, width = tokens.shape[1:]
     wr, units = w_i.shape
     group = w_o.shape[1]
     nc, nt, nr = 4, 4, 8
-    rows = 3 * ln // 2 * nc
+    own = 3 * ln // 2
+    rows = own * nc
     hb = pl.BlockSpec(memory_space=pltpu.HBM)
     vm = pl.BlockSpec(memory_space=pltpu.VMEM)
     sds = jax.ShapeDtypeStruct
     return pl.pallas_call(
         functools.partial(forward_kernel, heads, ln),
         out_shape=(
-            sds((nc, 3 * ln // 2, group), BF),
             sds((width, 2 * nc * ln), BF),
             sds((2 * nc * ln, heads * 128), BF),
             sds((2 * nc * ln, heads * 128), BF),
             sds((nr * wr, 3 * group), BF),
-            sds((nt, nr, wr, group), BF),
-            sds((2, nr, wr, nt * units), BF),
-            sds((nt, 8, units), F32),
+            sds((width, nt * units), BF),
+            sds((width, nt * units), BF),
+            sds(tokens.shape, BF),
             sds((8, rows), F32),
             sds((group, rows), F32),
             sds((nc, 8, ln), jnp.int32),
+            sds((nc, own, group), BF),
+            sds((nt, width, group), BF),
+            sds((own, width), F32),
+            sds((16, width), F32),
         ),
-        in_specs=[hb] + [vm] * 5 + [hb] * 3,
-        out_specs=(hb,) * 8 + (vm,) * 3,
+        in_specs=[hb] + [vm] * 5 + [hb] * 4 + [vm] * 6,
+        out_specs=(hb,) * 7 + (vm,) * 7,
         scratch_shapes=[
             pltpu.VMEM((2 * nc, ln, width), BF),
             pltpu.VMEM((width, 2 * nc * ln), BF),
@@ -838,8 +1027,8 @@
             pltpu.VMEM((2 * nc * ln, heads * 128), BF),
             pltpu.VMEM((2 * nc * ln, heads * 128), BF),
             pltpu.VMEM((heads, nc * ln, ln), F32),
-            pltpu.VMEM((2 * heads, 128, nc * ln), BF),
-            pltpu.VMEM((heads, 128, ln), F32),
+            pltpu.VMEM((2 * heads, HEAD, nc * ln), BF),
+            pltpu.VMEM((heads, HEAD, ln), F32),
             pltpu.VMEM((2 * nc, ln, 128), F32),
             pltpu.VMEM((2 * nc, 8, ln), F32),
             pltpu.VMEM((rows, group), BF),
@@ -849,15 +1038,35 @@
             pltpu.VMEM((wr, 3 * group), BF),
             pltpu.VMEM((8, 3 * group), F32),
             pltpu.VMEM((8, units), F32),
-            pltpu.SemaphoreType.DMA((140,)),
-            pltpu.SemaphoreType.DMA((140,)),
+            pltpu.VMEM((nc, own, group), BF),
+            pltpu.VMEM((nt, nr, wr, group), BF),
+            pltpu.VMEM((2, nr, wr, nt * units), BF),
+            pltpu.VMEM((nt, 8, units), F32),
+            pltpu.VMEM((own, width), BF),
+            pltpu.VMEM((own, width), BF),
+            pltpu.VMEM((own, width), F32),
+            pltpu.VMEM((own, 128), F32),
+            pltpu.VMEM((own, width), BF),
+            pltpu.VMEM((width, own), BF),
+            pltpu.VMEM((own, width), F32),
+            pltpu.VMEM((own, width), F32),
+            pltpu.VMEM((own, nt * units), BF),
+            pltpu.VMEM((own, nt * units), F32),
+            pltpu.VMEM((width, own), BF),
+            pltpu.VMEM((own, width), BF),
+            pltpu.VMEM((width, nt * units), BF),
+            pltpu.VMEM((width, nt * units), BF),
+            pltpu.VMEM((own, width), BF),
+            pltpu.SemaphoreType.DMA((2, 4)),
+            pltpu.SemaphoreType.DMA((150,)),
+            pltpu.SemaphoreType.DMA((150,)),
             pltpu.SemaphoreType.DMA((32,)),
         ],
         compiler_params=pltpu.CompilerParams(
             vmem_limit_bytes=60 << 20, collective_id=0, has_side_effects=True
         ),
         name="forward",
-    )(tokens, segments, w_kinds, q_bias, v_bias, in_bias, w_o, w_i, w_b)
+    )(tokens, segments, w_kinds, q_bias, v_bias, in_bias, w_o, w_i, w_b, cotangent, *vectors)
 
 
 def middle_kernel(
@@ -1116,7 +1325,7 @@
     g_b,
     g_i,
     g_o,
-    out_low,
+    out_in,
     d_first,
     small_in,
     q_in,
@@ -1191,7 +1400,7 @@
     core, y = c % 2, c // 2
     wr = gf_b.shape[0]
     units = gf_b.shape[1]
-    width = out_low.shape[1]
+    width = d_first.shape[1]
     wide = heads * 128
     rc = Copies(send, recv)
     at_c = lambda k: (d, c ^ k, z)
@@ -1359,12 +1568,14 @@
             rc.start(self.left[0], lambda: (src, self.at(z), (d, c, z + 1)), lambda: z < 3)
             rc.start(self.right[0], lambda: (src, self.at(z), (d, c, z - 1)), lambda: z > 0)
 
-        def step(self, j):
+        def step(self, j, wait=True):
             from_left, from_right = z - j, z + j
 
-            @pl.when(z >= j)
-            def _():
-                rc.arrived(self.left[j - 1], self.at(from_left), (d, c, z - 1))
+            if wait:
+
+                @pl.when(z >= j)
+                def _():
+                    rc.arrived(self.left[j - 1], self.at(from_left), (d, c, z - 1))
 
             if j < 3:
                 rc.start(
@@ -1373,9 +1584,11 @@
                     lambda: (z >= j) & (z < 3),
                 )
 
-            @pl.when(z + j <= 3)
-            def _():
-                rc.arrived(self.right[j - 1], self.at(from_right), (d, c, z + 1))
+            if wait:
+
+                @pl.when(z + j <= 3)
+                def _():
+                    rc.arrived(self.right[j - 1], self.at(from_right), (d, c, z + 1))
 
             if j < 3:
                 rc.start(
@@ -1418,10 +1631,6 @@
     small_got[0, 1] = small_in[...]
     wh_here = copy_here(wh_in, wh)
     xt_here = copy_here(xt_in, xt)
-    out_here = [
-        copy_here(out_low.at[pl.ds(0, ln)], out_lines[0].at(z)),
-        copy_here(out_low.at[pl.ds(ln, hl)], out_lines[1].at(z)),
-    ]
 
     def block(qb):
         r0, r1, o0, o1, seq = block_rows(qb, half, ln)
@@ -1444,6 +1653,7 @@
             turned = do[h].astype(F32).T[HEAD:, :]
             kept = two_lanes(ctx_t, slice(HEAD * h, HEAD * h + HEAD), o0, o1, hl)
             delta.append(jnp.sum(turned * kept, 0, keepdims=True))
+        q_do = [jnp.concatenate([q[h], do[h]], 0) for h in range(heads)]
         dqt[...] = jnp.zeros_like(dqt)
 
         @pl.loop(0, nc)
@@ -1456,12 +1666,11 @@
                 kvh = kv[rows, 128 * h : 128 * h + 128]
                 p = jnp.where(same, jnp.exp(dot_nt(kvh, q[h]) - line[h]), 0.0)
                 ds = (p * (dot_nt(kvh, do[h]) - delta[h])).astype(BF)
-                dkv[rows, 128 * h : 128 * h + 128] += dot_nn(ds, q[h]) + dot_nn(
-                    p.astype(BF), do[h]
-                )
+                both = jnp.concatenate([ds, p.astype(BF)], 1)
+                dkv[rows, 128 * h : 128 * h + 128] += dot_nn(both, q_do[h])
                 dqt[h] += dot_nn(kvt[seq * heads + h, :, keys], ds)
 
-        turned = jnp.concatenate([dqt[h, :HEAD, :] for h in range(heads)], 0).T * 0.125
+        turned = jnp.concatenate([dqt[h] for h in range(heads)], 0).T * 0.125
         bias_sum[0:1, wide:] += jnp.sum(turned, 0, keepdims=True)
         low = turned.astype(BF)
         d_proj[pl.ds(r0, hl), wide:] = low[:hl]
@@ -1605,12 +1814,12 @@
         xt_here.wait()
 
     def out_begin():
-        out_lines[0].begin(out_low.at[pl.ds(0, ln)])
-        out_lines[1].begin(out_low.at[pl.ds(ln, hl)])
-
+        for line in out_lines:
+            line.step(1, False)
+
+    w_core_send(weights[0])
     out_begin()
-    w_core_send(weights[0])
-    w_core_send(weights[2])
+    small_send(0)
     for i in range(nc):
         for s in range(2):
             line = seg[i, s : s + 1, :].astype(F32)
@@ -1630,78 +1839,76 @@
             for h in range(heads):
                 kvt[s * heads + h, :, pl.ds(pl.multiple_of(j * ln, ln), ln)] = kv[
                     rows, 128 * h : 128 * h + 128
-                ].T
-
-    small_send(0)
+                ].T[:HEAD]
+
+    small_step(0)
+    w_core_send(weights[2])
     w_core_add(0)
+    w_core_send(weights[1])
     get_ctx()
 
     @pl.loop(0, 6)
     def _(i):
         block(jnp.where(i == 0, 0, jnp.where(i == 1, 1, jnp.where(i == 2, 2, jnp.where(i == 3, 3, jnp.where(i == 4, 4, 5))))))
 
-        @pl.when(i == 0)
+        @pl.when(i == 1)
         def _():
-            w_core_send(weights[1])
-            small_step(0)
             w_core_add(2)
-            out_lines[0].step(1)
-            out_lines[1].step(1)
+            out_lines[0].step(2)
+            out_lines[1].step(2)
 
         @pl.when(i == 3)
         def _():
             t_partial(0)
-            out_lines[0].step(2)
-            out_lines[1].step(2)
             t_core(0)
-            w_plane(2)
 
     t_whole(0)
-    h_partial(0)
-    t_whole(1)
     w_plane(0)
     t_partial(1)
+    t_whole(1)
+    h_partial(1)
+    w_plane(2)
+    bias_send(0)
+    tok_lines[0].step(1)
+    small_step(1)
+    h_partial(0)
+    w_corner(0)
+    h_send()
+    bias_step(0)
+    t_core(1)
+    tok_lines[1].step(1)
+    w_core_add(1)
     w_corner(2)
-    t_core(1)
-    small_step(1)
-    bias_send(0)
-    w_core_add(1)
-    tok_lines[0].step(1)
-    w_corner(0)
+    tok_lines[0].step(2)
+    w_line(0)
+    tok_lines[1].step(2)
+    small_step(2)
+    t_shared()
     w_line(2)
-    small_step(2)
-    bias_step(0)
-    tok_lines[1].step(1)
-    h_partial(1)
+    small_step(3)
+    h_plane()
+    bias_step(1)
+    tok_lines[0].step(3)
+    t_shared_end()
+    w_plane(1)
+    h_line()
     out_lines[0].step(3)
     out_lines[1].step(3)
-    tok_lines[0].step(2)
-    t_shared()
-    bias_step(1)
-    h_send()
-    t_shared_end()
-    tok_lines[1].step(2)
-    w_plane(1)
-    tok_lines[0].step(3)
-    w_line(0)
-    h_plane()
     tok_lines[2].step(1)
+    w_corner(1)
+    w_next(2)
+    h_end()
     w_next(0)
+    tok_lines[2].step(2)
+    w_end(0)
     bias_step(2)
-    h_line()
-    small_step(3)
-    w_next(2)
-    w_corner(1)
     w_end(2)
-    w_end(0)
-    h_end()
-    tok_lines[2].step(2)
+    small_step(4)
     w_line(1)
+    tok_lines[1].step(3)
     w_next(1)
-    tok_lines[1].step(3)
+    w_end(1)
     tok_lines[2].step(3)
-    small_step(4)
-    w_end(1)
     tok_here = [
         copy_here(done.at[pl.ds(0, hl)], tok_lines[0].at(z)),
         copy_here(done.at[pl.ds(hl, hl)], tok_lines[1].at(z)),
@@ -1716,16 +1923,16 @@
     gf_h[...] = h_got[...]
     bias[...] = bias_fin[...]
 
-    for copy in out_here + tok_here:
+    for copy in tok_here:
         copy.wait()
     rc.all_sent()
 
 
-def backward(d_ctx, g_b, g_i, g_o, out_low, d_first, small, q, kv, xt, wh, lse, ctx_t, seg, heads, seqs):
+def backward(d_ctx, g_b, g_i, g_o, out_in, d_first, small, q, kv, xt, wh, lse, ctx_t, seg, heads, seqs):
     nc, own, group = d_ctx.shape
     ln = own * 2 // 3
     hl = ln // 2
-    width = out_low.shape[1]
+    width = out_in.shape[2]
     wr, all_units = g_b.shape[2:]
     units = all_units // 4
     hb = pl.BlockSpec(memory_space=pltpu.HBM)
@@ -1746,7 +1953,7 @@
             sds(small.shape, F32),
             sds((8, 3 * group), F32),
         ),
-        in_specs=[hb] * 4 + [vm] * 3 + [hb] * 4 + [vm] * 3,
+        in_specs=[hb] * 5 + [vm] * 2 + [hb] * 4 + [vm] * 3,
         out_specs=(hb, hb) + (vm,) * 6,
         scratch_shapes=[
             v((n2, heads * 128), BF),
@@ -1755,9 +1962,9 @@
             v((width, 3 * group), BF),
             v((nc, own, group), BF),
             v((rows, heads * 128), BF),
-            v((2 * heads, 128, nc * ln), BF),
+            v((2 * heads, HEAD, nc * ln), BF),
             v((n2, heads * 128), F32),
-            v((heads, 128, ln), F32),
+            v((heads, HEAD, ln), F32),
             v((n2, 3 * group), BF),
             v((2 * nc, ln, 128), F32),
             v((2 * nc, 8, ln), F32),
@@ -1801,8 +2008,9 @@
         compiler_params=pltpu.CompilerParams(
             vmem_limit_bytes=60 << 20, collective_id=1, has_side_effects=True
         ),
+        input_output_aliases={4: 0},
         name="backward",
-    )(d_ctx, g_b, g_i, g_o, out_low, d_first, small, q, kv, xt, wh, lse, ctx_t, seg)
+    )(d_ctx, g_b, g_i, g_o, out_in, d_first, small, q, kv, xt, wh, lse, ctx_t, seg)
 
 
 def finish_kernel(
@@ -2021,8 +2229,11 @@
     w_kinds = jnp.transpose(w_qkv, (1, 0, 2))
     biases = (q_bias, v_bias, in_bias)
     weights = (w_out, w_in, w_back)
+    vectors = (out_bias, gain_one, shift_one, back_bias, gain_two, shift_two)
     if sizes == (2, 4, 4):
-        got = forward(tokens, segments, w_kinds, *biases, *weights, heads)
+        xt, q, kv, wh, g_b, g_i, out_low, lse, ctx_t, seg_all, d_ctx, g_o, d_first, small = forward(
+            tokens, segments, w_kinds, *biases, *weights, cotangent, vectors, heads
+        )
     else:
         tok2 = own_pair(tokens)
         seg2 = jnp.concatenate([own_pair(segments), jnp.zeros((6, ln), jnp.int32)], 0)
@@ -2031,13 +2242,16 @@
         b_head = jnp.broadcast_to(b_head[None], (8, 3 * group))
         b_unit = jnp.broadcast_to(in_bias[None], (8, units))
         got = forward_plain(sizes, me, tok2, seg2, w_head, b_head, b_unit, *weights, heads)
-    ctx_all, xt, q, kv, wh, w_o, w_ib, b_in, lse, ctx_t, seg_all = got
-    w_o = w_o.reshape(nt, width, group)
-    w_ib = w_ib.reshape(2, width, nt * units)
-    vectors = (out_bias, gain_one, shift_one, back_bias, gain_two, shift_two)
-    d_ctx, g_b, g_i, g_o, out_low, d_first, small = middle(
-        tokens, cotangent, ctx_all, w_o, w_ib, b_in, vectors
-    )
+        ctx_all, xt, q, kv, wh, w_o, w_ib, b_in, lse, ctx_t, seg_all = got
+        d_ctx, g_b, g_i, g_o, out_low, d_first, small = middle(
+            tokens,
+            cotangent,
+            ctx_all,
+            w_o.reshape(nt, width, group),
+            w_ib.reshape(2, width, nt * units),
+            b_in,
+            vectors,
+        )
     low = (g_b, g_i, g_o)
     if sizes == (2, 4, 4):
         output, d_tokens, g_back, g_in, g_out, g_h, small, d_bias = backward(

time: 247 us -> 236 us (0.955)
  Pallas kernels: 245 us -> 233 us
    pallas_call x1 -> x0, Pallas kernels: 33.2 us -> none  [middle(): pl.pallas_call(functools.partial(middle_kernel, ln), out_shape=(sds((bloc...]
    pallas_call x1, Pallas kernels: 82.1 us -> 109 us  [forward(): pl.pallas_call(functools.partial(forward_kernel, heads, ln), out_shape=(s...]
    pallas_call x1, Pallas kernels: 122 us -> 117 us  [backward(): pl.pallas_call(functools.partial(backward_kernel, heads, ln), out_shape=(...]
where the time goes in v6:
time: 236 us
  Pallas kernels  233 us (99%)
    pallas_call x1, Pallas kernels, backward(): pl.pallas_call(functools.partial(backward_kernel, heads, ln), out_shape=(...  117 us
    pallas_call x1, Pallas kernels, forward(): pl.pallas_call(functools.partial(forward_kernel, heads, ln), out_shape=(s...  109 us
    pallas_call x1, Pallas kernels, finish(): pl.pallas_call(functools.partial(finish_kernel, heads), grid=(seqs,), out...  7.29 us

profile of v6, /device:TPU:0, one launch (start us, length us, event | category | flops | bytes accessed | tf_op | source)
XLA Modules:
  0.0 235.6 jit_solution(1854318923267176147)
XLA Ops:
  0.7 108.8 %forward.1 = (bf16[768,2048]{1,0:T(8,128)(2,1)}, bf16[2048,384]{1,0:T(8,128)(2,1)}, bf16[2048,384]{1,0:T(8,128)(2,1)}, bf16[768,576]{1,0:T(8,128)(2,1)}, bf16[76...) custom-call(bf16[6,256,768]{2,1,0:T(8,128)(2,1)} %tokens.1, ...), custom_call_target="tpu_custom_call" | custom-call | tf_op jit(solution)/shard_map/forward/pallas_call | solution.py:1002
  109.4 117.1 %backward.1 = (bf16[6,256,768]{2,1,0:T(8,128)(2,1)}, bf16[6,256,768]{2,1,0:T(8,128)(2,1)}, f32[96,768]{1,0:T(8,128)}, f32[96,768]{1,0:T(8,128)}, f32[96,192]{1,0...) custom-call(bf16[4,384,192]{2,1,0:T(8,128)(2,1)} %get-tuple-element.52., ...), custom_call_target="tpu_custom_call", output_to_operand_aliasing={{0}: (4, {})} | custom-call | tf_op jit(solution)/shard_map/backward/pallas_call | solution.py:1944
  226.5 7.3 %finish.1 = (f32[6,256,768]{2,1,0:T(8,128)}, bf16[6,256,768]{2,1,0:T(8,128)(2,1)}, f32[96,768]{1,0:T(8,128)}, f32[96,768]{1,0:T(8,128)}, f32[96,192]{1,0:T(8,128...) custom-call(bf16[6,256,768]{2,1,0:T(8,128)(2,1)} %get-tuple-element., ...), custom_call_target="tpu_custom_call" | custom-call | tf_op jit(solution)/shard_map/finish/pallas_call | solution.py:2054
  233.8 1.8 copy.32

commit v7 on v6

--- a/solution.py
+++ b/solution.py
@@ -568,7 +568,7 @@
     n_c = [[four() for _ in range(3)] for _ in range(4)]
 
     groups = [(0, 1), (2,)]
-    over_y = ((0, 1), (0, 3), (1, 1), (1, 2))
+    over_y = ((0, 2), (1, 0))
 
     def pass_on(n, g, i, r, device, first=False):
         t = lambda: order[i]
@@ -753,28 +753,32 @@
     for s in range(2):
         rc.start(n_ty[s], lambda s=s: (tok_src(s), x2.at[2 * c + s], at_c(2)))
         rc.start(n_tc[s], lambda s=s: (tok_src(s), x2.at[2 * c + s], at_c(1)))
+    own_send(0)
+    line_begin(1)
+    head_send()
+    line_step(0, 1)
     y_send(0, 0)
-    line_step(0, 1)
+    y_send(0, 1)
+    line_step(1, 1)
+    head_pass(2)
+    head_pass(1)
     line_step(0, 2)
-    head_send()
-    head_pass(1)
-    line_begin(1)
     head_pass(3)
-    y_send(1, 0)
-    head_pass(2)
+    y_send(1, 1)
+    from_x(0, 1)
     segments_done()
     token_pass()
-    y_send(0, 1)
-    own_send(0)
+    line_step(1, 2)
+    from_y(0, 0)
+    y_send(1, 2)
+    own_send(1)
+    from_x(0, 0)
+    line_step(0, 3)
     y_send(0, 2)
-    line_step(0, 3)
-    from_x(0, 1)
-    own_send(1)
     y_send(0, 3)
-    line_step(1, 1)
-    y_send(1, 1)
     from_x(0, 2)
-    from_y(0, 0)
+    y_send(1, 0)
+    from_y(0, 1)
     for t in range(4):
         rc.arrived(n_hx + t, wh_at((1 - d) * nc + (z ^ t)), at_x)
     for s in range(2):
@@ -797,7 +801,6 @@
     x_here = copy_here(xt, xt_out)
     q_here = copy_here(q_scr, q_out)
     kv_here = copy_here(kv, kv_out)
-    line_step(1, 2)
     @pl.loop(0, nc)
     def _(j):
         for s in range(2):
@@ -807,35 +810,37 @@
                     rows, 128 * h : 128 * h + 128
                 ].T[HEAD:]
 
-    from_x(0, 3)
 
     @pl.loop(0, 6)
     def _(qb):
         block(qb)
 
-        @pl.when(qb == 0)
+        @pl.when(qb == 2)
         def _():
+            from_y(1, 2)
             line_step(1, 3)
+
+        @pl.when(qb == 3)
+        def _():
             y_send(1, 3)
 
     context_send()
     ctx_here = copy_here(ctx_at(c), ctx_all.at[c])
-    y_send(1, 2)
-    from_y(0, 2)
-    from_x(0, 0)
-    from_corner(0, 0)
-    from_x(1, 1)
-    from_y(0, 3)
-    from_y(1, 1)
-    from_y(1, 0)
-    from_x(1, 3)
-    from_y(0, 1)
-    from_y(1, 3)
-    from_corner(0, 2)
-    from_corner(0, 3)
-    from_corner(0, 1)
     from_x(1, 2)
     from_x(1, 0)
+    from_y(0, 2)
+    from_y(0, 3)
+    from_corner(0, 2)
+    from_x(1, 1)
+    from_y(1, 0)
+    from_x(0, 3)
+    from_x(1, 3)
+    from_y(1, 3)
+    from_corner(1, 2)
+    from_corner(0, 0)
+    from_corner(0, 1)
+    from_y(1, 1)
+    from_corner(0, 3)
     for k in (1, 2, 3):
         rc.arrived(n_ctx + k, ctx_all.at[c ^ k], at_c(k))
     for n, r in zip(n_c, (row, row_x, row_y, row_d)):
@@ -879,15 +884,10 @@
 
         chunks(gelu, thin)
 
-        @pl.when(t == 0)
+        @pl.when(t == 1)
         def _():
             from_corner(1, 1)
-            from_y(1, 2)
-
-        @pl.when(t == 1)
-        def _():
             from_corner(1, 0)
-            from_corner(1, 2)
 
     for n, r in zip(n_c, (row, row_x, row_y, row_d)):
         for i in range(4):
@@ -1818,8 +1818,10 @@
             line.step(1, False)
 
     w_core_send(weights[0])
+    w_core_send(weights[2])
     out_begin()
     small_send(0)
+    w_core_add(0)
     for i in range(nc):
         for s in range(2):
             line = seg[i, s : s + 1, :].astype(F32)
@@ -1841,10 +1843,7 @@
                     rows, 128 * h : 128 * h + 128
                 ].T[:HEAD]
 
-    small_step(0)
-    w_core_send(weights[2])
-    w_core_add(0)
-    w_core_send(weights[1])
+    w_core_add(2)
     get_ctx()
 
     @pl.loop(0, 6)
@@ -1853,62 +1852,66 @@
 
         @pl.when(i == 1)
         def _():
-            w_core_add(2)
             out_lines[0].step(2)
             out_lines[1].step(2)
 
         @pl.when(i == 3)
         def _():
+            small_step(0)
+            w_plane(2)
             t_partial(0)
             t_core(0)
-
-    t_whole(0)
-    w_plane(0)
+            w_core_send(weights[1])
+            small_step(1)
+
+        @pl.when(i == 4)
+        def _():
+            w_plane(0)
+            t_whole(0)
+
+    t_whole(1)
     t_partial(1)
-    t_whole(1)
-    h_partial(1)
-    w_plane(2)
+    small_step(2)
+    tok_lines[0].step(1)
+    t_core(1)
     bias_send(0)
-    tok_lines[0].step(1)
-    small_step(1)
-    h_partial(0)
+    w_corner(2)
     w_corner(0)
-    h_send()
-    bias_step(0)
-    t_core(1)
     tok_lines[1].step(1)
     w_core_add(1)
-    w_corner(2)
+    h_partial(1)
+    bias_step(0)
+    w_line(2)
+    h_partial(0)
+    tok_lines[1].step(2)
+    w_next(2)
+    t_shared()
+    h_send()
+    w_line(0)
+    t_shared_end()
     tok_lines[0].step(2)
-    w_line(0)
-    tok_lines[1].step(2)
-    small_step(2)
-    t_shared()
-    w_line(2)
+    w_plane(1)
     small_step(3)
     h_plane()
+    tok_lines[2].step(1)
+    h_line()
     bias_step(1)
+    w_end(2)
+    tok_lines[1].step(3)
+    w_next(0)
+    w_corner(1)
+    bias_step(2)
     tok_lines[0].step(3)
-    t_shared_end()
-    w_plane(1)
-    h_line()
+    h_end()
+    tok_lines[2].step(2)
+    w_end(0)
+    w_line(1)
+    w_next(1)
+    small_step(4)
+    w_end(1)
+    tok_lines[2].step(3)
     out_lines[0].step(3)
     out_lines[1].step(3)
-    tok_lines[2].step(1)
-    w_corner(1)
-    w_next(2)
-    h_end()
-    w_next(0)
-    tok_lines[2].step(2)
-    w_end(0)
-    bias_step(2)
-    w_end(2)
-    small_step(4)
-    w_line(1)
-    tok_lines[1].step(3)
-    w_next(1)
-    w_end(1)
-    tok_lines[2].step(3)
     tok_here = [
         copy_here(done.at[pl.ds(0, hl)], tok_lines[0].at(z)),
         copy_here(done.at[pl.ds(hl, hl)], tok_lines[1].at(z)),
@@ -2030,9 +2033,9 @@
         pick = lambda ref, rows, at: jnp.concatenate(
             [ref[rows, 128 * h + at : 128 * h + at + HEAD] for h in range(heads)], -1
         )
-        gh[:, 0, :] = g_h[:, wide:]
-        gh[:, 1, :] = pick(g_h, slice(None), 0)
-        gh[:, 2, :] = pick(g_h, slice(None), HEAD)
+        gh[0] = g_h[:, wide:]
+        gh[1] = pick(g_h, slice(None), 0)
+        gh[2] = pick(g_h, slice(None), HEAD)
         gq[...] = bias[0, wide:]
         gv[...] = pick(bias, 0, HEAD)
         for i, ref in ((0, w0), (1, w1), (2, w2), (3, w3), (4, w4), (5, w5)):
@@ -2044,16 +2047,16 @@
     seqs, ln, width = d_tokens.shape
     wr, units = g_b.shape
     group = g_o.shape[1]
-    one = lambda: pl.BlockSpec((1, ln, width), lambda i: (i, 0, 0))
+    one = lambda: pl.BlockSpec((seqs // 3, ln, width), lambda i: (i, 0, 0))
     whole = lambda shape: pl.BlockSpec(shape, lambda i: (0,) * len(shape))
     sds = jax.ShapeDtypeStruct
     rest = [
-        (wr, units), (wr, units), (wr, group), (wr, 3, group), (group,), (group,),
+        (wr, units), (wr, units), (wr, group), (3, wr, group), (group,), (group,),
         (width,), (width,), (width,), (units,), (width,), (width,), (width,),
     ]
     return pl.pallas_call(
         functools.partial(finish_kernel, heads),
-        grid=(seqs,),
+        grid=(3,),
         out_shape=[sds(d_tokens.shape, F32), sds(output.shape, BF)] + [sds(s, F32) for s in rest],
         in_specs=[one(), one()]
         + [whole(a.shape) for a in (g_b, g_i, g_o, g_h, small, d_bias)],
@@ -2279,6 +2282,7 @@
     d_tokens, output, g_b, g_i, g_o, g_h, d_qb, d_vb, w0, w1, w2, d_in, w3, w4, w5 = finish(
         d_tokens, output, g_back, g_in, g_out, g_h, small, d_bias, heads
     )
+    g_h = jnp.transpose(g_h, (1, 0, 2))
     return (output, d_tokens, g_h, d_qb, d_vb, g_o, w0, w1, w2, g_i, d_in, g_b, w3, w4, w5)
 
 

time: 236 us -> 228 us (0.966)
  Pallas kernels: 233 us -> 227 us
    pallas_call x1, Pallas kernels: 109 us -> 106 us  [forward(): pl.pallas_call(functools.partial(forward_kernel, heads, ln), out_shape=(s...]
    pallas_call x1, Pallas kernels: 117 us -> 115 us  [backward(): pl.pallas_call(functools.partial(backward_kernel, heads, ln), out_shape=(...]
where the time goes in v7:
time: 228 us
  Pallas kernels  227 us (100%)
    pallas_call x1, Pallas kernels, backward(): pl.pallas_call(functools.partial(backward_kernel, heads, ln), out_shape=(...  115 us
    pallas_call x1, Pallas kernels, forward(): pl.pallas_call(functools.partial(forward_kernel, heads, ln), out_shape=(s...  106 us
    pallas_call x1, Pallas kernels, finish(): pl.pallas_call(functools.partial(finish_kernel, heads), grid=(3,), out_sh...  6.53 us

profile of v7, /device:TPU:0, one launch (start us, length us, event | category | flops | bytes accessed | tf_op | source)
XLA Modules:
  0.0 227.8 jit_solution(4314856392736359466)
XLA Ops:
  0.7 105.8 %forward.1 = (bf16[768,2048]{1,0:T(8,128)(2,1)}, bf16[2048,384]{1,0:T(8,128)(2,1)}, bf16[2048,384]{1,0:T(8,128)(2,1)}, bf16[768,576]{1,0:T(8,128)(2,1)}, bf16[76...) custom-call(bf16[6,256,768]{2,1,0:T(8,128)(2,1)} %tokens.1, ...), custom_call_target="tpu_custom_call" | custom-call | tf_op jit(solution)/shard_map/forward/pallas_call | solution.py:1002
  106.5 114.6 %backward.1 = (bf16[6,256,768]{2,1,0:T(8,128)(2,1)}, bf16[6,256,768]{2,1,0:T(8,128)(2,1)}, f32[96,768]{1,0:T(8,128)}, f32[96,768]{1,0:T(8,128)}, f32[96,192]{1,0...) custom-call(bf16[4,384,192]{2,1,0:T(8,128)(2,1)} %get-tuple-element.52., ...), custom_call_target="tpu_custom_call", output_to_operand_aliasing={{0}: (4, {})} | custom-call | tf_op jit(solution)/shard_map/backward/pallas_call | solution.py:1947
  221.1 6.5 %finish.1 = (f32[6,256,768]{2,1,0:T(8,128)}, bf16[6,256,768]{2,1,0:T(8,128)(2,1)}, f32[96,768]{1,0:T(8,128)}, f32[96,768]{1,0:T(8,128)}, f32[96,192]{1,0:T(8,128...) custom-call(bf16[6,256,768]{2,1,0:T(8,128)(2,1)} %get-tuple-element., ...), custom_call_target="tpu_custom_call" | custom-call | tf_op jit(solution)/shard_map/finish/pallas_call | solution.py:2057

commit v8 on v7

--- a/solution.py
+++ b/solution.py
@@ -1817,11 +1817,11 @@
         for line in out_lines:
             line.step(1, False)
 
-    w_core_send(weights[0])
-    w_core_send(weights[2])
     out_begin()
     small_send(0)
+    w_core_send(weights[0])
     w_core_add(0)
+    w_core_send(weights[2])
     for i in range(nc):
         for s in range(2):
             line = seg[i, s : s + 1, :].astype(F32)
@@ -1843,75 +1843,78 @@
                     rows, 128 * h : 128 * h + 128
                 ].T[:HEAD]
 
-    w_core_add(2)
     get_ctx()
 
     @pl.loop(0, 6)
     def _(i):
-        block(jnp.where(i == 0, 0, jnp.where(i == 1, 1, jnp.where(i == 2, 2, jnp.where(i == 3, 3, jnp.where(i == 4, 4, 5))))))
+        block(jnp.where(i == 0, 4, jnp.where(i == 1, 5, jnp.where(i == 2, 0, jnp.where(i == 3, 1, jnp.where(i == 4, 2, 3))))))
 
         @pl.when(i == 1)
         def _():
             out_lines[0].step(2)
             out_lines[1].step(2)
+            t_partial(1)
+            t_core(1)
+
+        @pl.when(i == 2)
+        def _():
+            small_step(0)
+            w_plane(0)
+            w_core_send(weights[1])
+            w_core_add(2)
 
         @pl.when(i == 3)
         def _():
-            small_step(0)
-            w_plane(2)
-            t_partial(0)
-            t_core(0)
-            w_core_send(weights[1])
-            small_step(1)
+            t_shared()
 
         @pl.when(i == 4)
         def _():
-            w_plane(0)
-            t_whole(0)
-
+            small_step(1)
+
+    small_step(2)
+    t_shared_end()
+    t_partial(0)
+    small_step(3)
+    t_core(0)
+    bias_send(0)
+    w_plane(2)
+    tok_lines[2].step(1)
+    w_core_add(1)
+    t_whole(0)
+    bias_step(0)
     t_whole(1)
-    t_partial(1)
-    small_step(2)
+    h_partial(1)
+    bias_step(1)
+    w_corner(0)
+    small_step(4)
+    tok_lines[2].step(2)
+    h_partial(0)
+    h_send()
+    tok_lines[1].step(1)
     tok_lines[0].step(1)
-    t_core(1)
-    bias_send(0)
+    bias_step(2)
+    w_plane(1)
     w_corner(2)
-    w_corner(0)
-    tok_lines[1].step(1)
-    w_core_add(1)
-    h_partial(1)
-    bias_step(0)
+    tok_lines[2].step(3)
+    w_line(0)
+    h_plane()
     w_line(2)
-    h_partial(0)
+    w_next(0)
+    tok_lines[0].step(2)
+    h_line()
+    w_corner(1)
     tok_lines[1].step(2)
+    w_end(0)
+    h_end()
+    tok_lines[1].step(3)
     w_next(2)
-    t_shared()
-    h_send()
-    w_line(0)
-    t_shared_end()
-    tok_lines[0].step(2)
-    w_plane(1)
-    small_step(3)
-    h_plane()
-    tok_lines[2].step(1)
-    h_line()
-    bias_step(1)
+    w_line(1)
     w_end(2)
-    tok_lines[1].step(3)
-    w_next(0)
-    w_corner(1)
-    bias_step(2)
-    tok_lines[0].step(3)
-    h_end()
-    tok_lines[2].step(2)
-    w_end(0)
-    w_line(1)
     w_next(1)
-    small_step(4)
-    w_end(1)
-    tok_lines[2].step(3)
     out_lines[0].step(3)
     out_lines[1].step(3)
+    tok_lines[0].step(3)
+    w_end(1)
     tok_here = [
         copy_here(done.at[pl.ds(0, hl)], tok_lines[0].at(z)),
         copy_here(done.at[pl.ds(hl, hl)], tok_lines[1].at(z)),
@@ -2047,7 +2050,7 @@
     seqs, ln, width = d_tokens.shape
     wr, units = g_b.shape
     group = g_o.shape[1]
-    one = lambda: pl.BlockSpec((seqs // 3, ln, width), lambda i: (i, 0, 0))
+    one = lambda: pl.BlockSpec((seqs // 2, ln, width), lambda i: (i, 0, 0))
     whole = lambda shape: pl.BlockSpec(shape, lambda i: (0,) * len(shape))
     sds = jax.ShapeDtypeStruct
     rest = [
@@ -2056,7 +2059,7 @@
     ]
     return pl.pallas_call(
         functools.partial(finish_kernel, heads),
-        grid=(3,),
+        grid=(2,),
         out_shape=[sds(d_tokens.shape, F32), sds(output.shape, BF)] + [sds(s, F32) for s in rest],
         in_specs=[one(), one()]
         + [whole(a.shape) for a in (g_b, g_i, g_o, g_h, small, d_bias)],

time: 228 us -> 227 us (level)
  no operation moved by 1% of the time
where the time goes in v8:
time: 227 us; the launch traced here: 226 us
  Pallas kernels  226 us (100%)
    pallas_call x1, Pallas kernels, backward(): pl.pallas_call(functools.partial(backward_kernel, heads, ln), out_shape=(...  114 us
    pallas_call x1, Pallas kernels, forward(): pl.pallas_call(functools.partial(forward_kernel, heads, ln), out_shape=(s...  106 us
    pallas_call x1, Pallas kernels, finish(): pl.pallas_call(functools.partial(finish_kernel, heads), grid=(2,), out_sh...  5.53 us

profile of v8, /device:TPU:0, one launch (start us, length us, event | category | flops | bytes accessed | tf_op | source)
XLA Modules:
  0.0 226.5 jit_solution(11524011834066899133)
XLA Ops:
  0.7 105.8 %forward.1 = (bf16[768,2048]{1,0:T(8,128)(2,1)}, bf16[2048,384]{1,0:T(8,128)(2,1)}, bf16[2048,384]{1,0:T(8,128)(2,1)}, bf16[768,576]{1,0:T(8,128)(2,1)}, bf16[76...) custom-call(bf16[6,256,768]{2,1,0:T(8,128)(2,1)} %tokens.1, ...), custom_call_target="tpu_custom_call" | custom-call | tf_op jit(solution)/shard_map/forward/pallas_call | solution.py:1002
  106.5 114.3 %backward.1 = (bf16[6,256,768]{2,1,0:T(8,128)(2,1)}, bf16[6,256,768]{2,1,0:T(8,128)(2,1)}, f32[96,768]{1,0:T(8,128)}, f32[96,768]{1,0:T(8,128)}, f32[96,192]{1,0...) custom-call(bf16[4,384,192]{2,1,0:T(8,128)(2,1)} %get-tuple-element.52., ...), custom_call_target="tpu_custom_call", output_to_operand_aliasing={{0}: (4, {})} | custom-call | tf_op jit(solution)/shard_map/backward/pallas_call | solution.py:1950
  220.8 5.5 %finish.1 = (f32[6,256,768]{2,1,0:T(8,128)}, bf16[6,256,768]{2,1,0:T(8,128)(2,1)}, f32[96,768]{1,0:T(8,128)}, f32[96,768]{1,0:T(8,128)}, f32[96,192]{1,0:T(8,128...) custom-call(bf16[6,256,768]{2,1,0:T(8,128)(2,1)} %get-tuple-element., ...), custom_call_target="tpu_custom_call" | custom-call | tf_op jit(solution)/shard_map/finish/pallas_call | solution.py:2060
